TPU v7x, 128 devices: a whole 4x4x4 slice. The times are simulated.
128 devices in a mesh: gy: 16 (over z, y_hi, core), gz: 8 (over y_lo, x).
Axes of the slice: x: 4, y: 4 (y_hi: 2, y_lo: 2; y = y_hi * 2 + y_lo), z: 4, core: 2. Of those that a mesh axis runs over, the one named last changes fastest.
Arguments:
- adjoint: float32 [5, 64, 1024, 256], P(None, 'gz', 'gy'), may hold values from -6 to 6
- speed: float32 [64, 1024, 256], P('gz', 'gy'), may hold values from 0.5 to 2
- x_derivative: float32 [256, 256], replicated, may hold values from -0.375 to 0.375
- y_operators: float32 [2, 1024, 1024], replicated, may hold values from -0.1875 to 0.1875
- coupling: float32 [3, 5, 5], replicated, may hold values from -2.5 to 2.5
Outputs:
- advanced: float32 [5, 64, 1024, 256], P(None, 'gz', 'gy')
All inputs are finite; a program needn't handle non-finite values.
Results may differ from a plain program's by a relative error of at most 0.0001.
Values sent between devices are 32-bit elements; how exact they have to be, the bound alone decides.
No kernel may reach another device: no remote copies, remote signals or barrier semaphores. Data moves between devices by JAX's collectives and lax.ppermute only.
A program may use at most 128 MiB of HBM per device.

v0:
```python
import functools

import jax
import jax.numpy as jnp
from jax import lax
from jax.experimental import pallas as pl
from jax.experimental.pallas import tpu as pltpu
from jax.sharding import PartitionSpec as P


stencil = (0.8, -0.2, 4.0 / 105.0, -1.0 / 280.0)
viscous = 0.5
stepping = 0.5

OFFSETS = ((0, 0), (1, 0), (3, 0), (0, 1), (2, 0), (1, 1), (3, 1), (2, 1))
EARLY = 4
HALO = len(stencil)


def chip_perm(dz, dy):
    pairs = []
    for i in range(16):
        z, h, c = i // 4, (i // 2) % 2, i % 2
        pairs.append((i, ((z + dz) % 4) * 4 + ((h + dy) % 2) * 2 + c))
    return pairs


CORE_SWAP = [(i, i ^ 1) for i in range(16)]
MIRRORED = [OFFSETS.index(((-dz) % 4, dy)) for dz, dy in OFFSETS]


def chip_at(me, dz, dy):
    return ((((me >> 2) + dz) & 3) << 1) | (((me >> 1) & 1) ^ dy)


def target(me, o):
    return chip_at(me, OFFSETS[o][0], OFFSETS[o][1])


def source(me, o):
    return chip_at(me, 4 - OFFSETS[o][0], OFFSETS[o][1])


def split3(value):
    high = value.astype(jnp.bfloat16)
    low = (value - high.astype(jnp.float32)).astype(jnp.bfloat16)
    return high, low


def pack_kernel(me_ref, adjoint_ref, speed_ref, *refs):
    count = len(OFFSETS)
    outs = refs[:count]
    hold, arrive, leave = refs[count:]
    fields = adjoint_ref.shape[0]

    def loads(o):
        plane = target(me_ref[0], o)
        return (
            pltpu.make_async_copy(
                adjoint_ref.at[:, plane], hold.at[o, pl.ds(0, fields)], arrive.at[o, 0]
            ),
            pltpu.make_async_copy(speed_ref.at[plane], hold.at[o, fields], arrive.at[o, 1]),
        )

    order = list(range(1, count)) + [0]
    for o in order:
        for copy in loads(o):
            copy.start()
    for o in order:
        for copy in loads(o):
            copy.wait()
        pltpu.make_async_copy(hold.at[o], outs[o], leave.at[o]).start()
    for o in order:
        pltpu.make_async_copy(hold.at[o], outs[o], leave.at[o]).wait()


def pack(me, adjoint, speed):
    fields, _, rows, width = adjoint.shape
    count = len(OFFSETS)
    anywhere = pl.BlockSpec(memory_space=pl.ANY)
    return pl.pallas_call(
        pack_kernel,
        in_specs=[pl.BlockSpec(memory_space=pltpu.SMEM), anywhere, anywhere],
        out_specs=[anywhere] * count,
        out_shape=[jax.ShapeDtypeStruct((fields + 1, rows, width), jnp.float32)] * count,
        scratch_shapes=[
            pltpu.VMEM((count, fields + 1, rows, width), jnp.float32),
            pltpu.SemaphoreType.DMA((count, 2)),
            pltpu.SemaphoreType.DMA((count,)),
        ],
        name="pack",
        cost_estimate=pl.CostEstimate(flops=0, bytes_accessed=6 * 1024 * 1024, transcendentals=0),
    )(me, adjoint, speed)


def operator_kernel(me_ref, op_ref, early_ref, late_ref):
    chips = op_ref.shape[1]
    pair = op_ref.shape[4] // 8
    size = EARLY * pair
    for t in range(chips):
        for o in range(len(OFFSETS)):
            start = pl.multiple_of(source(me_ref[0], o) * pair, pair)
            high, low = split3(op_ref[0, t, 0, :, pl.ds(start, pair)])
            out_ref = early_ref if o < EARLY else late_ref
            at = (o % EARLY) * pair
            out_ref[0, t, :, at : at + pair] = high
            out_ref[0, t, :, size + at : size + at + pair] = high
            out_ref[0, t, :, 2 * size + at : 2 * size + at + pair] = low


def own_operators(me, y_operators, chips, rows):
    ops, size, _ = y_operators.shape
    shaped = y_operators.reshape(ops, chips, 2, rows, size)
    wide = 3 * size // 2
    step = 4
    out_spec = pl.BlockSpec((1, step, rows, wide), lambda o, t, me: (o, t, 0, 0))
    early, late = pl.pallas_call(
        operator_kernel,
        grid_spec=pltpu.PrefetchScalarGridSpec(
            num_scalar_prefetch=1,
            grid=(ops, chips // step),
            in_specs=[
                pl.BlockSpec(
                    (1, step, 1, rows, size), lambda o, t, me: (o, t, me[0] & 1, 0, 0)
                )
            ],
            out_specs=[out_spec] * 2,
        ),
        out_shape=[jax.ShapeDtypeStruct((ops, chips, rows, wide), jnp.bfloat16)] * 2,
        name="operators",
        cost_estimate=pl.CostEstimate(
            flops=4 * 1024 * 1024, bytes_accessed=10 * 1024 * 1024, transcendentals=0
        ),
    )(me, shaped)
    return early.reshape(ops * chips * rows, wide), late.reshape(ops * chips * rows, wide)


def load_parts(core, same, other, parts):
    rows = same[0].shape[1]
    size = parts.shape[0] // 3
    for o in range(EARLY):
        for block, which in ((same[o], core), (other[o], 1 - core)):
            start = pl.multiple_of(o * 2 * rows + which * rows, rows)
            high, low = split3(block[0])
            parts[pl.ds(start, rows), :] = high
            parts[pl.ds(start + size, rows), :] = low
            parts[pl.ds(start + 2 * size, rows), :] = high


def early_kernel(me_ref, op_ref, *refs):
    same, other = refs[:EARLY], refs[EARLY : 2 * EARLY]
    out_ref, parts = refs[2 * EARLY :]
    load_parts(me_ref[0] & 1, same, other, parts)
    out_ref[0] = jnp.dot(op_ref[...], parts[...], preferred_element_type=jnp.float32)


def early_lines(me, operators, same, other):
    fields = same[0].shape[0] - 1
    rows, width = same[0].shape[1:]
    height, size = operators.shape
    piece = pl.BlockSpec((1, rows, width), lambda f, me: (f, 0, 0))
    return pl.pallas_call(
        early_kernel,
        grid_spec=pltpu.PrefetchScalarGridSpec(
            num_scalar_prefetch=1,
            grid=(fields,),
            in_specs=[pl.BlockSpec(operators.shape, lambda f, me: (0, 0))]
            + [piece] * (2 * EARLY),
            out_specs=pl.BlockSpec((1, height, width), lambda f, me: (f, 0, 0)),
            scratch_shapes=[pltpu.VMEM((size, width), jnp.bfloat16)],
        ),
        out_shape=jax.ShapeDtypeStruct((fields, height, width), jnp.float32),
        name="early_lines",
        cost_estimate=pl.CostEstimate(
            flops=2 * height * size * width * fields,
            bytes_accessed=12 * 1024 * 1024,
            transcendentals=0,
        ),
    )(me, operators, *same, *other)


def late_kernel(me_ref, coupling_ref, op_ref, sums_ref, *refs):
    count = len(OFFSETS)
    same, other = refs[:EARLY], refs[EARLY : 2 * EARLY]
    speeds = refs[2 * EARLY : 2 * EARLY + count]
    outs = refs[2 * EARLY + count : 2 * EARLY + 2 * count]
    parts, grads = refs[2 * EARLY + 2 * count :]
    field = pl.program_id(0)
    fields = pl.num_programs(0)
    rows = same[0].shape[1]
    load_parts(me_ref[0] & 1, same, other, parts)
    grads[field] = sums_ref[0] + jnp.dot(
        op_ref[...], parts[...], preferred_element_type=jnp.float32
    )

    @pl.when(field == fields - 1)
    def _():
        half = grads.shape[1] // 2
        for o in range(count):
            start = pl.multiple_of(target(me_ref[0], o) * rows, rows)
            for part in range(0, rows, 16):
                firsts = [grads[g, pl.ds(start + part, 16), :] for g in range(5)]
                speed = speeds[o][0, pl.ds(part, 16), :] * stepping
                for f in range(5):
                    second = grads[f, pl.ds(start + half + part, 16), :]
                    outs[o][f, pl.ds(part, 16), :] = (
                        speed * mixed(coupling_ref, 1, firsts, f)
                        + (viscous * stepping) * second
                    )


def late_lines(me, coupling, operators, sums, same, other, everyone):
    count = len(OFFSETS)
    fields = same[0].shape[0] - 1
    rows, width = same[0].shape[1:]
    height, size = operators.shape
    piece = pl.BlockSpec((1, rows, width), lambda f, me: (f, 0, 0))
    last = pl.BlockSpec((1, rows, width), lambda f, me: (fields, 0, 0))
    return pl.pallas_call(
        late_kernel,
        grid_spec=pltpu.PrefetchScalarGridSpec(
            num_scalar_prefetch=1,
            grid=(fields,),
            in_specs=[
                pl.BlockSpec(memory_space=pltpu.SMEM),
                pl.BlockSpec(operators.shape, lambda f, me: (0, 0)),
                pl.BlockSpec((1, height, width), lambda f, me: (f, 0, 0)),
            ]
            + [piece] * (2 * EARLY)
            + [last] * count,
            out_specs=[pl.BlockSpec((fields, rows, width), lambda f, me: (0, 0, 0))] * count,
            scratch_shapes=[
                pltpu.VMEM((size, width), jnp.bfloat16),
                pltpu.VMEM((fields, height, width), jnp.float32),
            ],
        ),
        out_shape=[jax.ShapeDtypeStruct((fields, rows, width), jnp.float32)] * count,
        name="late_lines",
        cost_estimate=pl.CostEstimate(
            flops=2 * height * size * width * fields,
            bytes_accessed=16 * 1024 * 1024,
            transcendentals=0,
        ),
    )(me, coupling, operators, sums, *same, *other, *[everyone[m] for m in MIRRORED])


def mixed(coupling_ref, axis, grads, f):
    total = coupling_ref[axis, 0, f] * grads[0]
    for g in range(1, len(grads)):
        total = total + coupling_ref[axis, g, f] * grads[g]
    return total


def along_x_kernel(
    coupling_ref, adjoint_ref, speed_ref, xd_ref, out_ref, top_ref, bottom_ref, gx_ref
):
    fields, depth, rows, width = adjoint_ref.shape
    top_ref[...] = adjoint_ref[:, depth - HALO :]
    bottom_ref[...] = adjoint_ref[:, :HALO]
    flat = adjoint_ref[...].reshape(fields * depth * rows, width)
    fh, fl = split3(flat)
    xh, xl = split3(xd_ref[...])

    def product(a, b):
        return lax.dot_general(a, b, (((1,), (1,)), ((), ())), preferred_element_type=jnp.float32)

    grad_x = product(fh, xh) + product(fl, xh) + product(fh, xl)
    gx_ref[...] = grad_x.reshape(fields, depth, rows, width)
    for z in range(depth):
        grads = [gx_ref[g, z] for g in range(fields)]
        speed = speed_ref[z] * stepping
        for f in range(fields):
            out_ref[f, z] = adjoint_ref[f, z] + speed * mixed(coupling_ref, 0, grads, f)


def along_x(coupling, adjoint, speed, x_derivative):
    fields, depth, rows, width = adjoint.shape
    step = 16
    counts = (HALO, HALO)
    return pl.pallas_call(
        along_x_kernel,
        grid=(rows // step,),
        in_specs=[
            pl.BlockSpec(memory_space=pltpu.SMEM),
            pl.BlockSpec((fields, depth, step, width), lambda r: (0, 0, r, 0)),
            pl.BlockSpec((depth, step, width), lambda r: (0, r, 0)),
            pl.BlockSpec((width, width), lambda r: (0, 0)),
        ],
        out_specs=[
            pl.BlockSpec((fields, depth, step, width), lambda r: (0, 0, r, 0)),
        ]
        + [
            pl.BlockSpec((fields, count, step, width), lambda r: (0, 0, r, 0)) for count in counts
        ],
        out_shape=[jax.ShapeDtypeStruct(adjoint.shape, jnp.float32)]
        + [jax.ShapeDtypeStruct((fields, count, rows, width), jnp.float32) for count in counts],
        scratch_shapes=[pltpu.VMEM((fields, depth, step, width), jnp.float32)],
        name="along_x",
        cost_estimate=pl.CostEstimate(
            flops=6 * fields * depth * rows * width * width,
            bytes_accessed=6 * 1024 * 1024,
            transcendentals=0,
        ),
    )(coupling, adjoint, speed, x_derivative)


def along_z_kernel(coupling_ref, base_ref, adjoint_ref, low_ref, high_ref, speed_ref, out_ref):
    fields, depth, _, _ = adjoint_ref.shape

    def plane(g, k):
        if k < 0:
            return low_ref[g, HALO + k]
        if k >= depth:
            return high_ref[g, k - depth]
        return adjoint_ref[g, k]

    for z in range(depth):
        grads = []
        for g in range(fields):
            total = None
            for step, weight in enumerate(stencil):
                term = weight * (plane(g, z + step + 1) - plane(g, z - step - 1))
                total = term if total is None else total + term
            grads.append(total)
        speed = speed_ref[z] * stepping
        for f in range(fields):
            out_ref[f, z] = base_ref[f, z] + speed * mixed(coupling_ref, 2, grads, f)


def along_z(coupling, base, adjoint, low, high, speed):
    fields, depth, rows, width = adjoint.shape
    step = 8
    whole = pl.BlockSpec((fields, depth, step, width), lambda r: (0, 0, r, 0))
    side = pl.BlockSpec((fields, HALO, step, width), lambda r: (0, 0, r, 0))
    return pl.pallas_call(
        along_z_kernel,
        grid=(rows // step,),
        in_specs=[
            pl.BlockSpec(memory_space=pltpu.SMEM),
            whole,
            whole,
            side,
            side,
            pl.BlockSpec((depth, step, width), lambda r: (0, r, 0)),
        ],
        out_specs=whole,
        out_shape=jax.ShapeDtypeStruct(adjoint.shape, jnp.float32),
        input_output_aliases={1: 0},
        name="along_z",
        cost_estimate=pl.CostEstimate(
            flops=70 * fields * depth * rows * width,
            bytes_accessed=12 * 1024 * 1024,
            transcendentals=0,
        ),
    )(coupling, base, adjoint, low, high, speed)


def join_kernel(me_ref, base_ref, *refs, where):
    parts, (out_ref, hold, extra, arrive, leave) = refs[:-5], refs[-5:]
    fields = base_ref.shape[0]

    def load(k):
        plane = source(me_ref[0], where[k])
        return pltpu.make_async_copy(base_ref.at[:, plane], hold.at[k], arrive.at[k])

    def fetch(k):
        return pltpu.make_async_copy(parts[k], extra.at[k], arrive.at[len(where) + k])

    def store(k):
        plane = source(me_ref[0], where[k])
        return pltpu.make_async_copy(hold.at[k], out_ref.at[:, plane], leave.at[k])

    for k in range(len(where)):
        load(k).start()
        fetch(k).start()
    for k in range(len(where)):
        load(k).wait()
        fetch(k).wait()
        for f in range(fields):
            hold[k, f] = hold[k, f] + extra[k, f]
        store(k).start()
    for k in range(len(where)):
        store(k).wait()


def join(me, base, parts, where):
    fields, _, rows, width = base.shape
    count = len(where)
    anywhere = pl.BlockSpec(memory_space=pl.ANY)
    return pl.pallas_call(
        functools.partial(join_kernel, where=where),
        in_specs=[pl.BlockSpec(memory_space=pltpu.SMEM), anywhere] + [anywhere] * count,
        out_specs=anywhere,
        out_shape=jax.ShapeDtypeStruct(base.shape, jnp.float32),
        scratch_shapes=[
            pltpu.VMEM((count, fields, rows, width), jnp.float32),
            pltpu.VMEM((count, fields, rows, width), jnp.float32),
            pltpu.SemaphoreType.DMA((2 * count,)),
            pltpu.SemaphoreType.DMA((count,)),
        ],
        input_output_aliases={1: 0},
        name="join",
        cost_estimate=pl.CostEstimate(
            flops=count * fields * rows * width,
            bytes_accessed=count * 1024 * 1024,
            transcendentals=0,
        ),
    )(me, base, *parts)


def shards(adjoint, speed, x_derivative, y_operators, coupling):
    _, depth, rows, _ = adjoint.shape
    chips = lax.axis_size("gy") // 2
    assert chips == depth == 8 and y_operators.shape[1] == 16 * rows
    me = lax.axis_index("gy").astype(jnp.int32)[None]
    pieces = pack(me, adjoint, speed)
    same = [pieces[0]]
    for o in range(1, 8):
        same.append(lax.ppermute(pieces[o], "gy", chip_perm(*OFFSETS[o])))
    other = []
    for o in range(8):
        other.append(lax.ppermute(same[o], "gy", CORE_SWAP))

    result, top, bottom = along_x(coupling, adjoint, speed, x_derivative)
    count = lax.axis_size("gz")
    forward = [(i, (i + 1) % count) for i in range(count)]
    backward = [(i, (i - 1) % count) for i in range(count)]
    low = lax.ppermute(top, "gz", forward)
    high = lax.ppermute(bottom, "gz", backward)

    early, late = own_operators(me, y_operators, chips, rows)
    sums = early_lines(me, early, same[:EARLY], other[:EARLY])
    parts = late_lines(me, coupling, late, sums, same[EARLY:], other[EARLY:], same)
    result = along_z(coupling, result, adjoint, low, high, speed)
    arrived = [parts[0]]
    for o in range(1, 8):
        arrived.append(lax.ppermute(parts[o], "gy", chip_perm(*OFFSETS[o])))
    for where in ((0, 1, 2), (3, 4), (5, 6, 7)):
        result = join(me, result, [arrived[o] for o in where], where)
    return result


def solution(mesh):
    placed = (P(None, "gz", "gy", None), P("gz", "gy", None), P(), P(), P())

    return jax.shard_map(
        shards, mesh=mesh, in_specs=placed, out_specs=P(None, "gz", "gy", None), check_vma=False
    )
```

profile of v0, /device:TPU:1, one launch (start us, length us, event | category | flops | bytes accessed | tf_op | source)
XLA Modules:
  0.0 128.0 jit_solution(5032153196154643995)
XLA Ops:
  0.0 2.9 %pack.1 = (f32[6,64,256]{2,1,0:T(8,128)}, f32[6,64,256]{2,1,0:T(8,128)}, f32[6,64,256]{2,1,0:T(8,128)}, f32[6,64,256]{2,1,0:T(8,128)}, f32[6,64,256]{2,1,0:T(8,1...) custom-call(s32[1]{0:T(128)} %bitcast.me_ref, f32[5,8,64,256]{3,2,1,0:T(8,128)} %adjoint_ref.5, ...), custom_call_target="tpu_custom_call" | custom-call | bytes 6291456 | tf_op jit(solution)/shard_map/pack/pallas_call | solution.py:81
  2.9 2.5 %collective-permute-start.2 = (f32[6,64,256]{2,1,0:T(8,128)}, f32[6,64,256]{2,1,0:T(8,128)S(1)}, u32[]{:S(2)}, u32[]{:S(2)}) collective-permute-start(f32[6,64,256]{2,1,0:T(8,128)} %get-tuple-element.32), channel_id=1, source_target_pairs={{0,32},{8,40},{16,48},{24,56},{32,64},{40,72},{48,80},{56,88},{64,... | collective-permute-start | bytes 1179656 | tf_op jit(solution)/shard_map/ppermute | solution.py:419
  5.4 2.2 %collective-permute-start.3 = (f32[6,64,256]{2,1,0:T(8,128)}, f32[6,64,256]{2,1,0:T(8,128)S(1)}, u32[]{:S(2)}, u32[]{:S(2)}) collective-permute-start(f32[6,64,256]{2,1,0:T(8,128)} %get-tuple-element.33), channel_id=1, source_target_pairs={{0,96},{8,104},{16,112},{24,120},{32,0},{40,8},{48,16},{56,24},{64... | collective-permute-start | bytes 1179656 | tf_op jit(solution)/shard_map/ppermute | solution.py:419
  7.6 2.9 %collective-permute-start.4 = (f32[6,64,256]{2,1,0:T(8,128)}, f32[6,64,256]{2,1,0:T(8,128)}, u32[]{:S(2)}, u32[]{:S(2)}) collective-permute-start(f32[6,64,256]{2,1,0:T(8,128)} %get-tuple-element.34), channel_id=1, source_target_pairs={{0,16},{8,24},{16,0},{24,8},{32,48},{40,56},{48,32},{56,40},{64,80... | collective-permute-start | bytes 1179656 | tf_op jit(solution)/shard_map/ppermute | solution.py:419
  10.5 1.2 collective-permute-start.5
  11.8 1.5 %collective-permute-start.9 = (f32[6,64,256]{2,1,0:T(8,128)}, f32[6,64,256]{2,1,0:T(8,128)}, u32[]{:S(2)}, u32[]{:S(2)}) collective-permute-start(f32[6,64,256]{2,1,0:T(8,128)} %get-tuple-element.35), channel_id=1, source_target_pairs={{0,64},{8,72},{16,80},{24,88},{32,96},{40,104},{48,112},{56,120},{... | collective-permute-start | bytes 1179656 | tf_op jit(solution)/shard_map/ppermute | solution.py:419
  13.3 3.4 %collective-permute-done.2.refs_1_.refs_10_ = f32[6,64,256]{2,1,0:T(8,128)S(1)} collective-permute-done((f32[6,64,256]{2,1,0:T(8,128)}, f32[6,64,256]{2,1,0:T(8,128)S(1)}, u32[]{:S(2)}, u32[]{:S(2)}) %collective-permute-start.2) | collective-permute-done | bytes 393248 | tf_op jit(solution)/shard_map/ppermute | solution.py:419
  16.7 1.7 %collective-permute-start.10 = (f32[6,64,256]{2,1,0:T(8,128)}, f32[6,64,256]{2,1,0:T(8,128)S(1)}, u32[]{:S(2)}, u32[]{:S(2)}) collective-permute-start(f32[6,64,256]{2,1,0:T(8,128)} %get-tuple-element.36), channel_id=1, source_target_pairs={{0,48},{8,56},{16,32},{24,40},{32,80},{40,88},{48,64},{56,72},{64,... | collective-permute-start | bytes 1179656 | tf_op jit(solution)/shard_map/ppermute | solution.py:419
  18.4 0.0 collective-permute-done.3.refs_2_.refs_9_
  18.4 4.2 %collective-permute-start.11 = (f32[6,64,256]{2,1,0:T(8,128)}, f32[6,64,256]{2,1,0:T(8,128)S(1)}, u32[]{:S(2)}, u32[]{:S(2)}) collective-permute-start(f32[6,64,256]{2,1,0:T(8,128)} %get-tuple-element.37), channel_id=1, source_target_pairs={{0,112},{8,120},{16,96},{24,104},{32,16},{40,24},{48,0},{56,8},{64... | collective-permute-start | bytes 1179656 | tf_op jit(solution)/shard_map/ppermute | solution.py:419
  22.6 0.0 collective-permute-done.4.refs_3_.refs_11_
  22.6 2.0 %collective-permute-start.12 = (f32[6,64,256]{2,1,0:T(8,128)}, f32[6,64,256]{2,1,0:T(8,128)S(1)}, u32[]{:S(2)}, u32[]{:S(2)}) collective-permute-start(f32[6,64,256]{2,1,0:T(8,128)} %get-tuple-element.38), channel_id=1, source_target_pairs={{0,80},{8,88},{16,64},{24,72},{32,112},{40,120},{48,96},{56,104},{... | collective-permute-start | bytes 1179656 | tf_op jit(solution)/shard_map/ppermute | solution.py:419
  24.6 0.0 collective-permute-done.5.refs_4_
  24.6 9.8 %collective-permute-start.6 = (f32[6,64,256]{2,1,0:T(8,128)S(1)}, f32[6,64,256]{2,1,0:T(8,128)S(1)}, u32[]{:S(2)}, u32[]{:S(2)}) collective-permute-start(f32[6,64,256]{2,1,0:T(8,128)S(1)} %collective-permute-done.2.refs_1_.refs_10_), channel_id=1, source_target_pairs={{0,8},{8,0},{16,24},{24,16},{32,40},{40,32},{48,56},{56,48},{64,72... | collective-permute-start | bytes 1179656 | tf_op jit(solution)/shard_map/ppermute | solution.py:422
  34.5 0.0 collective-permute-done.9.refs_0_.refs_12_
  34.5 3.3 %collective-permute-start.7 = (f32[6,64,256]{2,1,0:T(8,128)S(1)}, f32[6,64,256]{2,1,0:T(8,128)}, u32[]{:S(2)}, u32[]{:S(2)}) collective-permute-start(f32[6,64,256]{2,1,0:T(8,128)S(1)} %collective-permute-done.3.refs_2_.refs_9_), channel_id=1, source_target_pairs={{0,8},{8,0},{16,24},{24,16},{32,40},{40,32},{48,56},{56,48},{64,72... | collective-permute-start | bytes 1179656 | tf_op jit(solution)/shard_map/ppermute | solution.py:422
  37.8 0.0 collective-permute-done.10.refs_1_.refs_14_
  37.8 0.1 collective-permute-start.8
  37.8 0.0 collective-permute-done.11.refs_2_.refs_13_
  37.8 0.0 copy-done.12
  37.9 6.7 %collective-permute-start.13 = (f32[6,64,256]{2,1,0:T(8,128)}, f32[6,64,256]{2,1,0:T(8,128)}, u32[]{:S(2)}, u32[]{:S(2)}) collective-permute-start(f32[6,64,256]{2,1,0:T(8,128)} %collective-permute-done.9.refs_0_.refs_12_), channel_id=1, source_target_pairs={{0,8},{8,0},{16,24},{24,16},{32,40},{40,32},{48,56},{56,48},{64,72... | collective-permute-start | bytes 1179656 | tf_op jit(solution)/shard_map/ppermute | solution.py:422
  44.6 0.6 copy.11.coupling_ref
  45.2 5.9 %along_x.1 = (f32[5,8,64,256]{3,2,1,0:T(8,128)}, f32[5,4,64,256]{3,2,1,0:T(8,128)}, f32[5,4,64,256]{3,2,1,0:T(8,128)}) custom-call(f32[3,5,5]{2,1,0:T(8,128)} %copy.11.coupling_ref, f32[5,8,64,256]{3,2,1,0:T(8,128)} %adjoint_ref.5, f32[8,64,256]{2,1,0:T(8,128)} %speed_ref.5, f32[256,256]{1,0:T(8,128)} %xd_ref.1), custom_call_target="tpu_custom_call" | custom-call | flops 1006632960 | bytes 6291456 | tf_op jit(solution)/shard_map/along_x/pallas_call | solution.py:280
  51.1 0.0 collective-permute-done.12.refs_3_.refs_15_
  51.1 0.8 copy-done.11
  51.9 1.2 collective-permute-start
  53.1 0.0 collective-permute-done.6.refs_5_
  53.1 0.7 copy-done.13
  53.8 3.7 %collective-permute-start.1 = (f32[5,4,64,256]{3,2,1,0:T(8,128)}, f32[5,4,64,256]{3,2,1,0:T(8,128)S(1)}, u32[]{:S(2)}, u32[]{:S(2)}) collective-permute-start(f32[5,4,64,256]{3,2,1,0:T(8,128)} %get-tuple-element.28), channel_id=1, source_target_pairs={{0,7},{1,0},{2,1},{3,2},{4,3},{5,4},{6,5},{7,6},{8,15},{9,8},{10,9... | collective-permute-start | bytes 3932168 | tf_op jit(solution)/shard_map/ppermute | solution.py:429
  57.5 0.0 collective-permute-done.7.refs_6_
  57.5 0.3 collective-permute-start.14
  57.8 0.0 collective-permute-done.8.refs_7_
  57.8 0.2 collective-permute-start.15
  58.0 0.0 collective-permute-done.13.refs_4_
  58.0 0.3 collective-permute-start.16
  58.4 5.6 %operators.1 = (bf16[2,8,64,1536]{3,2,1,0:T(8,128)(2,1)}, bf16[2,8,64,1536]{3,2,1,0:T(8,128)(2,1)}) custom-call(s32[1]{0:T(128)} %bitcast.me_ref, f32[2,8,2,64,1024]{4,3,2,1,0:T(8,128)} %bitcast.4), custom_call_target="tpu_custom_call" | custom-call | flops 4194304 | bytes 10485760 | tf_op jit(solution)/shard_map/operators/pallas_call | solution.py:117
  63.9 9.4 %early_lines.1.sums_ref = f32[5,1024,256]{2,1,0:T(8,128)} custom-call(s32[1]{0:T(128)} %bitcast.me_ref, bf16[1024,1536]{1,0:T(8,128)(2,1)} %bitcast.6, f32[6,64,256]{2,1,0:T(8,128)} %get-tuple-element.31.refs_0_.refs_8_, f32[6,64,256]{2,1,0:T(8,128)} %copy-done.7, f32[6,64,256]{2,1,0:T(8,128)} %copy-done.8, ...), custom_call_target="tpu_custom_call" | custom-call | flops 4026531840 | bytes 12582912 | tf_op jit(solution)/shard_map/early_lines/pallas_call | solution.py:162
  73.3 0.0 collective-permute-done.14.refs_5_
  73.3 0.0 collective-permute-done.15.refs_6_
  73.3 0.0 collective-permute-done.16.refs_7_
  73.4 11.4 %late_lines.1 = (f32[5,64,256]{2,1,0:T(8,128)}, f32[5,64,256]{2,1,0:T(8,128)}, f32[5,64,256]{2,1,0:T(8,128)}, f32[5,64,256]{2,1,0:T(8,128)}, f32[5,64,256]{2,1,0...) custom-call(s32[1]{0:T(128)} %bitcast.me_ref, f32[3,5,5]{2,1,0:T(8,128)} %copy.11.coupling_ref, ...), custom_call_target="tpu_custom_call" | custom-call | flops 4026531840 | bytes 16777216 | tf_op jit(solution)/shard_map/late_lines/pallas_call | solution.py:219
  84.8 0.1 collective-permute-start.17
  84.9 5.2 %collective-permute-start.18 = (f32[5,64,256]{2,1,0:T(8,128)}, f32[5,64,256]{2,1,0:T(8,128)S(1)}, u32[]{:S(2)}, u32[]{:S(2)}) collective-permute-start(f32[5,64,256]{2,1,0:T(8,128)} %get-tuple-element.41), channel_id=1, source_target_pairs={{0,96},{8,104},{16,112},{24,120},{32,0},{40,8},{48,16},{56,24},{64... | collective-permute-start | bytes 983048 | tf_op jit(solution)/shard_map/ppermute | solution.py:437
  90.1 0.5 collective-permute-start.19
  90.6 7.7 %collective-permute-done.17.refs_1_ = f32[5,64,256]{2,1,0:T(8,128)S(1)} collective-permute-done((f32[5,64,256]{2,1,0:T(8,128)}, f32[5,64,256]{2,1,0:T(8,128)S(1)}, u32[]{:S(2)}, u32[]{:S(2)}) %collective-permute-start.17) | collective-permute-done | bytes 327712 | tf_op jit(solution)/shard_map/ppermute | solution.py:437
  98.3 0.3 collective-permute-start.20
  98.6 0.0 collective-permute-done.18.refs_2_
  98.6 0.4 copy-done.4
  99.0 1.5 %collective-permute-start.21 = (f32[5,64,256]{2,1,0:T(8,128)}, f32[5,64,256]{2,1,0:T(8,128)S(1)}, u32[]{:S(2)}, u32[]{:S(2)}) collective-permute-start(f32[5,64,256]{2,1,0:T(8,128)} %get-tuple-element.44), channel_id=1, source_target_pairs={{0,48},{8,56},{16,32},{24,40},{32,80},{40,88},{48,64},{56,72},{64,... | collective-permute-start | bytes 983048 | tf_op jit(solution)/shard_map/ppermute | solution.py:437
  100.5 0.0 collective-permute-done.low_ref
  100.5 3.6 %collective-permute-start.22 = (f32[5,64,256]{2,1,0:T(8,128)}, f32[5,64,256]{2,1,0:T(8,128)}, u32[]{:S(2)}, u32[]{:S(2)}) collective-permute-start(f32[5,64,256]{2,1,0:T(8,128)} %get-tuple-element.45), channel_id=1, source_target_pairs={{0,112},{8,120},{16,96},{24,104},{32,16},{40,24},{48,0},{56,8},{64... | collective-permute-start | bytes 983048 | tf_op jit(solution)/shard_map/ppermute | solution.py:437
  104.1 0.0 collective-permute-done.1.high_ref
  104.1 1.0 collective-permute-start.23
  105.1 0.1 copy-done.1
  105.2 7.8 %along_z.1.base_ref = f32[5,8,64,256]{3,2,1,0:T(8,128)} custom-call(f32[3,5,5]{2,1,0:T(8,128)} %copy.11.coupling_ref, f32[5,8,64,256]{3,2,1,0:T(8,128)} %get-tuple-element.26.base_ref, f32[5,8,64,256]{3,2,1,0:T(8,128)} %adjoint_ref.5, f32[5,4,64,256]{3,2,1,0:T(8,128)} %copy-done, f32[5,4,64,256]{3,2,1,0:T(8,128)} %copy-done.1, ...), custom_call_target="tpu_custom_call", output_to_operand_aliasing={{}: (1, {})} | custom-call | flops 45875200 | bytes 12582912 | tf_op jit(solution)/shard_map/along_z/pallas_call | solution.py:335
  113.0 2.3 %join.3.base_ref = f32[5,8,64,256]{3,2,1,0:T(8,128)} custom-call(s32[1]{0:T(128)} %bitcast.me_ref, f32[5,8,64,256]{3,2,1,0:T(8,128)} %along_z.1.base_ref, f32[5,64,256]{2,1,0:T(8,128)} %get-tuple-element.39.refs_0_, f32[5,64,256]{2,1,0:T(8,128)} %copy-done.4, f32[5,64,256]{2,1,0:T(8,128)} %copy-done.5), custom_call_target="tpu_custom_call", output_to_operand_aliasing={{}: (1, {})} | custom-call | flops 245760 | bytes 3145728 | tf_op jit(solution)/shard_map/join/pallas_call | solution.py:390
  115.3 0.0 collective-permute-done.19.refs_0_
  115.3 0.5 collective-permute-done.20.refs_1_
  115.8 0.2 copy-done.3
  116.1 2.1 %join.4.base_ref = f32[5,8,64,256]{3,2,1,0:T(8,128)} custom-call(s32[1]{0:T(128)} %bitcast.me_ref, f32[5,8,64,256]{3,2,1,0:T(8,128)} %join.3.base_ref, f32[5,64,256]{2,1,0:T(8,128)} %copy-done.3, f32[5,64,256]{2,1,0:T(8,128)} %collective-permute-done.20.refs_1_), custom_call_target="tpu_custom_call", output_to_operand_aliasing={{}: (1, {})} | custom-call | flops 163840 | bytes 2097152 | tf_op jit(solution)/shard_map/join/pallas_call | solution.py:390
  118.1 0.0 collective-permute-done.21.refs_0_
  118.2 0.0 collective-permute-done.22.refs_1_
  118.2 7.5 %collective-permute-done.23.refs_2_ = f32[5,64,256]{2,1,0:T(8,128)} collective-permute-done((f32[5,64,256]{2,1,0:T(8,128)}, f32[5,64,256]{2,1,0:T(8,128)}, u32[]{:S(2)}, u32[]{:S(2)}) %collective-permute-start.23) | collective-permute-done | bytes 327712 | tf_op jit(solution)/shard_map/ppermute | solution.py:437
  125.7 2.3 %join.5 = f32[5,8,64,256]{3,2,1,0:T(8,128)} custom-call(s32[1]{0:T(128)} %bitcast.me_ref, f32[5,8,64,256]{3,2,1,0:T(8,128)} %join.4.base_ref, f32[5,64,256]{2,1,0:T(8,128)} %copy-done.2, f32[5,64,256]{2,1,0:T(8,128)} %collective-permute-done.22.refs_1_, f32[5,64,256]{2,1,0:T(8,128)} %collective-permute-done.23.refs_2_), custom_call_target="tpu_custom_call", output_to_operand_aliasing={{}: (1, {})} | custom-call | flops 245760 | bytes 3145728 | tf_op jit(solution)/shard_map/join/pallas_call | solution.py:390
  (22 shorter events, 0.0 us)
Async XLA Ops:
  0.0 44.6 %copy-start.6 = (f32[3,5,5]{2,0,1:T(4,128)S(1)}, f32[3,5,5]{2,0,1:T(4,128)}, u32[]{:S(2)}) copy-start(f32[3,5,5]{2,0,1:T(4,128)} %param.9) | copy-start | bytes 904
  2.9 13.8 %collective-permute-start.2 = (f32[6,64,256]{2,1,0:T(8,128)}, f32[6,64,256]{2,1,0:T(8,128)S(1)}, u32[]{:S(2)}, u32[]{:S(2)}) collective-permute-start(f32[6,64,256]{2,1,0:T(8,128)} %get-tuple-element.32), channel_id=1, source_target_pairs={{0,32},{8,40},{16,48},{24,56},{32,64},{40,72},{48,80},{56,88},{64,... | collective-permute-start | bytes 1179656 | tf_op jit(solution)/shard_map/ppermute | solution.py:419
  5.4 13.0 %collective-permute-start.3 = (f32[6,64,256]{2,1,0:T(8,128)}, f32[6,64,256]{2,1,0:T(8,128)S(1)}, u32[]{:S(2)}, u32[]{:S(2)}) collective-permute-start(f32[6,64,256]{2,1,0:T(8,128)} %get-tuple-element.33), channel_id=1, source_target_pairs={{0,96},{8,104},{16,112},{24,120},{32,0},{40,8},{48,16},{56,24},{64... | collective-permute-start | bytes 1179656 | tf_op jit(solution)/shard_map/ppermute | solution.py:419
  7.6 15.0 %collective-permute-start.4 = (f32[6,64,256]{2,1,0:T(8,128)}, f32[6,64,256]{2,1,0:T(8,128)}, u32[]{:S(2)}, u32[]{:S(2)}) collective-permute-start(f32[6,64,256]{2,1,0:T(8,128)} %get-tuple-element.34), channel_id=1, source_target_pairs={{0,16},{8,24},{16,0},{24,8},{32,48},{40,56},{48,32},{56,40},{64,80... | collective-permute-start | bytes 1179656 | tf_op jit(solution)/shard_map/ppermute | solution.py:419
  10.5 14.1 %collective-permute-start.5 = (f32[6,64,256]{2,1,0:T(8,128)}, f32[6,64,256]{2,1,0:T(8,128)S(1)}, u32[]{:S(2)}, u32[]{:S(2)}) collective-permute-start(f32[6,64,256]{2,1,0:T(8,128)} %get-tuple-element.31.refs_0_.refs_8_), channel_id=1, source_target_pairs={{0,8},{8,0},{16,24},{24,16},{32,40},{40,32},{48,56},{56,48},{64,72... | collective-permute-start | bytes 1179656 | tf_op jit(solution)/shard_map/ppermute | solution.py:422
  11.8 22.7 %collective-permute-start.9 = (f32[6,64,256]{2,1,0:T(8,128)}, f32[6,64,256]{2,1,0:T(8,128)}, u32[]{:S(2)}, u32[]{:S(2)}) collective-permute-start(f32[6,64,256]{2,1,0:T(8,128)} %get-tuple-element.35), channel_id=1, source_target_pairs={{0,64},{8,72},{16,80},{24,88},{32,96},{40,104},{48,112},{56,120},{... | collective-permute-start | bytes 1179656 | tf_op jit(solution)/shard_map/ppermute | solution.py:419
  16.7 47.3 %copy-start.7 = (f32[6,64,256]{2,1,0:T(8,128)}, f32[6,64,256]{2,1,0:T(8,128)S(1)}, u32[]{:S(2)}) copy-start(f32[6,64,256]{2,1,0:T(8,128)S(1)} %collective-permute-done.2.refs_1_.refs_10_) | copy-start | bytes 1179652
  16.7 21.1 %collective-permute-start.10 = (f32[6,64,256]{2,1,0:T(8,128)}, f32[6,64,256]{2,1,0:T(8,128)S(1)}, u32[]{:S(2)}, u32[]{:S(2)}) collective-permute-start(f32[6,64,256]{2,1,0:T(8,128)} %get-tuple-element.36), channel_id=1, source_target_pairs={{0,48},{8,56},{16,32},{24,40},{32,80},{40,88},{48,64},{56,72},{64,... | collective-permute-start | bytes 1179656 | tf_op jit(solution)/shard_map/ppermute | solution.py:419
  18.4 45.6 %copy-start.8 = (f32[6,64,256]{2,1,0:T(8,128)}, f32[6,64,256]{2,1,0:T(8,128)S(1)}, u32[]{:S(2)}) copy-start(f32[6,64,256]{2,1,0:T(8,128)S(1)} %collective-permute-done.3.refs_2_.refs_9_) | copy-start | bytes 1179652
  18.4 19.5 %collective-permute-start.11 = (f32[6,64,256]{2,1,0:T(8,128)}, f32[6,64,256]{2,1,0:T(8,128)S(1)}, u32[]{:S(2)}, u32[]{:S(2)}) collective-permute-start(f32[6,64,256]{2,1,0:T(8,128)} %get-tuple-element.37), channel_id=1, source_target_pairs={{0,112},{8,120},{16,96},{24,104},{32,16},{40,24},{48,0},{56,8},{64... | collective-permute-start | bytes 1179656 | tf_op jit(solution)/shard_map/ppermute | solution.py:419
  22.6 28.5 %collective-permute-start.12 = (f32[6,64,256]{2,1,0:T(8,128)}, f32[6,64,256]{2,1,0:T(8,128)S(1)}, u32[]{:S(2)}, u32[]{:S(2)}) collective-permute-start(f32[6,64,256]{2,1,0:T(8,128)} %get-tuple-element.38), channel_id=1, source_target_pairs={{0,80},{8,88},{16,64},{24,72},{32,112},{40,120},{48,96},{56,104},{... | collective-permute-start | bytes 1179656 | tf_op jit(solution)/shard_map/ppermute | solution.py:419
  24.6 13.2 %copy-start.12 = (f32[6,64,256]{2,1,0:T(8,128)}, f32[6,64,256]{2,1,0:T(8,128)S(1)}, u32[]{:S(2)}) copy-start(f32[6,64,256]{2,1,0:T(8,128)S(1)} %collective-permute-done.5.refs_4_) | copy-start | bytes 1179652
  24.6 28.4 %collective-permute-start.6 = (f32[6,64,256]{2,1,0:T(8,128)S(1)}, f32[6,64,256]{2,1,0:T(8,128)S(1)}, u32[]{:S(2)}, u32[]{:S(2)}) collective-permute-start(f32[6,64,256]{2,1,0:T(8,128)S(1)} %collective-permute-done.2.refs_1_.refs_10_), channel_id=1, source_target_pairs={{0,8},{8,0},{16,24},{24,16},{32,40},{40,32},{48,56},{56,48},{64,72... | collective-permute-start | bytes 1179656 | tf_op jit(solution)/shard_map/ppermute | solution.py:422
  34.5 23.0 %collective-permute-start.7 = (f32[6,64,256]{2,1,0:T(8,128)S(1)}, f32[6,64,256]{2,1,0:T(8,128)}, u32[]{:S(2)}, u32[]{:S(2)}) collective-permute-start(f32[6,64,256]{2,1,0:T(8,128)S(1)} %collective-permute-done.3.refs_2_.refs_9_), channel_id=1, source_target_pairs={{0,8},{8,0},{16,24},{24,16},{32,40},{40,32},{48,56},{56,48},{64,72... | collective-permute-start | bytes 1179656 | tf_op jit(solution)/shard_map/ppermute | solution.py:422
  37.8 13.3 %copy-start.9 = (f32[6,64,256]{2,1,0:T(8,128)}, f32[6,64,256]{2,1,0:T(8,128)S(1)}, u32[]{:S(2)}) copy-start(f32[6,64,256]{2,1,0:T(8,128)S(1)} %collective-permute-done.10.refs_1_.refs_14_) | copy-start | bytes 1179652
  37.8 20.1 %collective-permute-start.8 = (f32[6,64,256]{2,1,0:T(8,128)}, f32[6,64,256]{2,1,0:T(8,128)}, u32[]{:S(2)}, u32[]{:S(2)}) collective-permute-start(f32[6,64,256]{2,1,0:T(8,128)} %collective-permute-done.4.refs_3_.refs_11_), channel_id=1, source_target_pairs={{0,8},{8,0},{16,24},{24,16},{32,40},{40,32},{48,56},{56,48},{64,72... | collective-permute-start | bytes 1179656 | tf_op jit(solution)/shard_map/ppermute | solution.py:422
  37.9 13.3 %copy-start.10 = (f32[6,64,256]{2,1,0:T(8,128)}, f32[6,64,256]{2,1,0:T(8,128)S(1)}, u32[]{:S(2)}) copy-start(f32[6,64,256]{2,1,0:T(8,128)S(1)} %collective-permute-done.11.refs_2_.refs_13_) | copy-start | bytes 1179652
  37.9 20.2 %collective-permute-start.13 = (f32[6,64,256]{2,1,0:T(8,128)}, f32[6,64,256]{2,1,0:T(8,128)}, u32[]{:S(2)}, u32[]{:S(2)}) collective-permute-start(f32[6,64,256]{2,1,0:T(8,128)} %collective-permute-done.9.refs_0_.refs_12_), channel_id=1, source_target_pairs={{0,8},{8,0},{16,24},{24,16},{32,40},{40,32},{48,56},{56,48},{64,72... | collective-permute-start | bytes 1179656 | tf_op jit(solution)/shard_map/ppermute | solution.py:422
  51.1 0.8 copy-start.11
  51.9 48.6 %collective-permute-start = (f32[5,4,64,256]{3,2,1,0:T(8,128)}, f32[5,4,64,256]{3,2,1,0:T(8,128)S(1)}, u32[]{:S(2)}, u32[]{:S(2)}) collective-permute-start(f32[5,4,64,256]{3,2,1,0:T(8,128)} %get-tuple-element.27), channel_id=1, source_target_pairs={{0,1},{1,2},{2,3},{3,4},{4,5},{5,6},{6,7},{7,0},{8,9},{9,10},{10,1... | collective-permute-start | bytes 3932168 | tf_op jit(solution)/shard_map/ppermute | solution.py:428
  53.1 0.7 copy-start.13
  53.8 50.3 %collective-permute-start.1 = (f32[5,4,64,256]{3,2,1,0:T(8,128)}, f32[5,4,64,256]{3,2,1,0:T(8,128)S(1)}, u32[]{:S(2)}, u32[]{:S(2)}) collective-permute-start(f32[5,4,64,256]{3,2,1,0:T(8,128)} %get-tuple-element.28), channel_id=1, source_target_pairs={{0,7},{1,0},{2,1},{3,2},{4,3},{5,4},{6,5},{7,6},{8,15},{9,8},{10,9... | collective-permute-start | bytes 3932168 | tf_op jit(solution)/shard_map/ppermute | solution.py:429
  57.5 15.8 %collective-permute-start.14 = (f32[6,64,256]{2,1,0:T(8,128)}, f32[6,64,256]{2,1,0:T(8,128)}, u32[]{:S(2)}, u32[]{:S(2)}) collective-permute-start(f32[6,64,256]{2,1,0:T(8,128)} %copy-done.9), channel_id=1, source_target_pairs={{0,8},{8,0},{16,24},{24,16},{32,40},{40,32},{48,56},{56,48},{64,72... | collective-permute-start | bytes 1179656 | tf_op jit(solution)/shard_map/ppermute | solution.py:422
  57.8 15.5 %collective-permute-start.15 = (f32[6,64,256]{2,1,0:T(8,128)}, f32[6,64,256]{2,1,0:T(8,128)}, u32[]{:S(2)}, u32[]{:S(2)}) collective-permute-start(f32[6,64,256]{2,1,0:T(8,128)} %copy-done.10), channel_id=1, source_target_pairs={{0,8},{8,0},{16,24},{24,16},{32,40},{40,32},{48,56},{56,48},{64,72... | collective-permute-start | bytes 1179656 | tf_op jit(solution)/shard_map/ppermute | solution.py:422
  58.0 15.3 %collective-permute-start.16 = (f32[6,64,256]{2,1,0:T(8,128)}, f32[6,64,256]{2,1,0:T(8,128)}, u32[]{:S(2)}, u32[]{:S(2)}) collective-permute-start(f32[6,64,256]{2,1,0:T(8,128)} %copy-done.11), channel_id=1, source_target_pairs={{0,8},{8,0},{16,24},{24,16},{32,40},{40,32},{48,56},{56,48},{64,72... | collective-permute-start | bytes 1179656 | tf_op jit(solution)/shard_map/ppermute | solution.py:422
  84.8 13.5 %collective-permute-start.17 = (f32[5,64,256]{2,1,0:T(8,128)}, f32[5,64,256]{2,1,0:T(8,128)S(1)}, u32[]{:S(2)}, u32[]{:S(2)}) collective-permute-start(f32[5,64,256]{2,1,0:T(8,128)} %get-tuple-element.40), channel_id=1, source_target_pairs={{0,32},{8,40},{16,48},{24,56},{32,64},{40,72},{48,80},{56,88},{64,... | collective-permute-start | bytes 983048 | tf_op jit(solution)/shard_map/ppermute | solution.py:437
  84.9 13.7 %collective-permute-start.18 = (f32[5,64,256]{2,1,0:T(8,128)}, f32[5,64,256]{2,1,0:T(8,128)S(1)}, u32[]{:S(2)}, u32[]{:S(2)}) collective-permute-start(f32[5,64,256]{2,1,0:T(8,128)} %get-tuple-element.41), channel_id=1, source_target_pairs={{0,96},{8,104},{16,112},{24,120},{32,0},{40,8},{48,16},{56,24},{64... | collective-permute-start | bytes 983048 | tf_op jit(solution)/shard_map/ppermute | solution.py:437
  90.1 25.2 %collective-permute-start.19 = (f32[5,64,256]{2,1,0:T(8,128)}, f32[5,64,256]{2,1,0:T(8,128)S(1)}, u32[]{:S(2)}, u32[]{:S(2)}) collective-permute-start(f32[5,64,256]{2,1,0:T(8,128)} %get-tuple-element.42), channel_id=1, source_target_pairs={{0,16},{8,24},{16,0},{24,8},{32,48},{40,56},{48,32},{56,40},{64,80... | collective-permute-start | bytes 983048 | tf_op jit(solution)/shard_map/ppermute | solution.py:437
  98.3 0.7 copy-start.4
  98.3 17.5 %collective-permute-start.20 = (f32[5,64,256]{2,1,0:T(8,128)}, f32[5,64,256]{2,1,0:T(8,128)}, u32[]{:S(2)}, u32[]{:S(2)}) collective-permute-start(f32[5,64,256]{2,1,0:T(8,128)} %get-tuple-element.43), channel_id=1, source_target_pairs={{0,64},{8,72},{16,80},{24,88},{32,96},{40,104},{48,112},{56,120},{... | collective-permute-start | bytes 983048 | tf_op jit(solution)/shard_map/ppermute | solution.py:437
  99.0 5.1 %copy-start.5 = (f32[5,64,256]{2,1,0:T(8,128)}, f32[5,64,256]{2,1,0:T(8,128)S(1)}, u32[]{:S(2)}) copy-start(f32[5,64,256]{2,1,0:T(8,128)S(1)} %collective-permute-done.18.refs_2_) | copy-start | bytes 983044
  99.0 19.1 %collective-permute-start.21 = (f32[5,64,256]{2,1,0:T(8,128)}, f32[5,64,256]{2,1,0:T(8,128)S(1)}, u32[]{:S(2)}, u32[]{:S(2)}) collective-permute-start(f32[5,64,256]{2,1,0:T(8,128)} %get-tuple-element.44), channel_id=1, source_target_pairs={{0,48},{8,56},{16,32},{24,40},{32,80},{40,88},{48,64},{56,72},{64,... | collective-permute-start | bytes 983048 | tf_op jit(solution)/shard_map/ppermute | solution.py:437
  100.5 4.6 %copy-start = (f32[5,4,64,256]{3,2,1,0:T(8,128)}, f32[5,4,64,256]{3,2,1,0:T(8,128)S(1)}, u32[]{:S(2)}) copy-start(f32[5,4,64,256]{3,2,1,0:T(8,128)S(1)} %collective-permute-done.low_ref) | copy-start | bytes 3932164
  100.5 17.6 %collective-permute-start.22 = (f32[5,64,256]{2,1,0:T(8,128)}, f32[5,64,256]{2,1,0:T(8,128)}, u32[]{:S(2)}, u32[]{:S(2)}) collective-permute-start(f32[5,64,256]{2,1,0:T(8,128)} %get-tuple-element.45), channel_id=1, source_target_pairs={{0,112},{8,120},{16,96},{24,104},{32,16},{40,24},{48,0},{56,8},{64... | collective-permute-start | bytes 983048 | tf_op jit(solution)/shard_map/ppermute | solution.py:437
  104.1 1.1 copy-start.1
  104.1 21.5 %collective-permute-start.23 = (f32[5,64,256]{2,1,0:T(8,128)}, f32[5,64,256]{2,1,0:T(8,128)}, u32[]{:S(2)}, u32[]{:S(2)}) collective-permute-start(f32[5,64,256]{2,1,0:T(8,128)} %get-tuple-element.46), channel_id=1, source_target_pairs={{0,80},{8,88},{16,64},{24,72},{32,112},{40,120},{48,96},{56,104},{... | collective-permute-start | bytes 983048 | tf_op jit(solution)/shard_map/ppermute | solution.py:437
  115.3 0.7 copy-start.3
  118.2 7.5 %copy-start.2 = (f32[5,64,256]{2,1,0:T(8,128)}, f32[5,64,256]{2,1,0:T(8,128)S(1)}, u32[]{:S(2)}) copy-start(f32[5,64,256]{2,1,0:T(8,128)S(1)} %collective-permute-done.21.refs_0_) | copy-start | bytes 983044
where the time goes:
time: 129 us; the launch traced here: 128 us
  starting transfers between devices  56.1 us (43%)
  Pallas kernels  49.7 us (39%)
  waiting for transfers between devices  19.1 us (15%)
  local copies, waits for them, and re-layouts  2.91 us (2%)
    ppermute x8, starting transfers between devices, shards(): other.append(lax.ppermute(same[o], 'gy', CORE_SWAP))  22 us
    ppermute x7, starting transfers between devices, shards(): same.append(lax.ppermute(pieces[o], 'gy', chip_perm(*OFFSETS[o])))  17.1 us
    ppermute x7, waiting for transfers between devices, shards(): arrived.append(lax.ppermute(parts[o], 'gy', chip_perm(*OFFSETS[o])))  15.7 us
    ppermute x7, starting transfers between devices, shards(): arrived.append(lax.ppermute(parts[o], 'gy', chip_perm(*OFFSETS[o])))  12.1 us
    pallas_call x1, Pallas kernels, late_lines(): pl.pallas_call(late_kernel, grid_spec=pltpu.PrefetchScalarGridSpec(num_sc...  11.4 us
    pallas_call x1, Pallas kernels, early_lines(): pl.pallas_call(early_kernel, grid_spec=pltpu.PrefetchScalarGridSpec(num_s...  9.41 us
    pallas_call x1, Pallas kernels, along_z(): pl.pallas_call(along_z_kernel, grid=(rows // step,), in_specs=[pl.BlockSp...  7.83 us
    pallas_call x3, Pallas kernels, join(): pl.pallas_call(functools.partial(join_kernel, where=where), in_specs=[pl....  6.68 us
  transfers between devices with their start and end apart: 24, of which 4 were waited for; matrix products, arithmetic and copies ran while one was open for 0% of the time, Pallas kernels for 35%

commit v1 on v0

--- a/solution.py
+++ b/solution.py
@@ -245,18 +245,75 @@
 
 
 def mixed(coupling_ref, axis, grads, f):
-    total = coupling_ref[axis, 0, f] * grads[0]
+    total = coupling_ref[0, axis, f] * grads[0]
     for g in range(1, len(grads)):
-        total = total + coupling_ref[axis, g, f] * grads[g]
+        total = total + coupling_ref[g, axis, f] * grads[g]
     return total
 
 
-def along_x_kernel(
-    coupling_ref, adjoint_ref, speed_ref, xd_ref, out_ref, top_ref, bottom_ref, gx_ref
+def edges_kernel(column_ref, adjoint_ref, top_ref, bottom_ref, near_ref, far_ref, hold, arrive, leave):
+    fields, depth = adjoint_ref.shape[:2]
+    half = HALO // 2
+    edge = jnp.where(column_ref[0] == 3, depth - HALO, 0)
+
+    def load(f):
+        return pltpu.make_async_copy(adjoint_ref.at[f], hold.at[f], arrive.at[f])
+
+    def stores(f):
+        return [
+            pltpu.make_async_copy(hold.at[f, pl.ds(start, size)], out.at[f], leave.at[f, k])
+            for k, (out, start, size) in enumerate(
+                (
+                    (near_ref, edge, half),
+                    (far_ref, edge + half, half),
+                    (top_ref, depth - HALO, HALO),
+                    (bottom_ref, 0, HALO),
+                )
+            )
+        ]
+
+    for f in range(fields):
+        load(f).start()
+    for f in range(fields):
+        load(f).wait()
+        for copy in stores(f):
+            copy.start()
+    for f in range(fields):
+        for copy in stores(f):
+            copy.wait()
+
+
+def edges(column, adjoint):
+    fields, _, rows, width = adjoint.shape
+    counts = (HALO, HALO, HALO // 2, HALO // 2)
+    anywhere = pl.BlockSpec(memory_space=pl.ANY)
+    return pl.pallas_call(
+        edges_kernel,
+        in_specs=[pl.BlockSpec(memory_space=pltpu.SMEM), anywhere],
+        out_specs=[anywhere] * len(counts),
+        out_shape=[jax.ShapeDtypeStruct((fields, count, rows, width), jnp.float32) for count in counts],
+        scratch_shapes=[
+            pltpu.VMEM(adjoint.shape, jnp.float32),
+            pltpu.SemaphoreType.DMA((fields,)),
+            pltpu.SemaphoreType.DMA((fields, len(counts))),
+        ],
+        name="edges",
+        cost_estimate=pl.CostEstimate(flops=0, bytes_accessed=7 * 1024 * 1024, transcendentals=0),
+    )(column, adjoint)
+
+
+def local_kernel(
+    column_ref, coupling_ref, adjoint_ref, low_ref, high_ref, near_ref, far_ref, speed_ref,
+    xd_ref, out_ref, full_ref, gx_ref,
 ):
     fields, depth, rows, width = adjoint_ref.shape
-    top_ref[...] = adjoint_ref[:, depth - HALO :]
-    bottom_ref[...] = adjoint_ref[:, :HALO]
+    half = HALO // 2
+    first, last = column_ref[0] == 0, column_ref[0] == 3
+    for g in range(fields):
+        for k in range(HALO):
+            wrapped = near_ref[g, k] if k < half else far_ref[g, k - half]
+            full_ref[g, k] = jnp.where(first, wrapped, low_ref[g, k])
+            full_ref[g, HALO + k] = jnp.where(last, wrapped, high_ref[g, k])
     flat = adjoint_ref[...].reshape(fields * depth * rows, width)
     fh, fl = split3(flat)
     xh, xl = split3(xd_ref[...])
@@ -266,52 +323,12 @@
 
     grad_x = product(fh, xh) + product(fl, xh) + product(fh, xl)
     gx_ref[...] = grad_x.reshape(fields, depth, rows, width)
-    for z in range(depth):
-        grads = [gx_ref[g, z] for g in range(fields)]
-        speed = speed_ref[z] * stepping
-        for f in range(fields):
-            out_ref[f, z] = adjoint_ref[f, z] + speed * mixed(coupling_ref, 0, grads, f)
-
-
-def along_x(coupling, adjoint, speed, x_derivative):
-    fields, depth, rows, width = adjoint.shape
-    step = 16
-    counts = (HALO, HALO)
-    return pl.pallas_call(
-        along_x_kernel,
-        grid=(rows // step,),
-        in_specs=[
-            pl.BlockSpec(memory_space=pltpu.SMEM),
-            pl.BlockSpec((fields, depth, step, width), lambda r: (0, 0, r, 0)),
-            pl.BlockSpec((depth, step, width), lambda r: (0, r, 0)),
-            pl.BlockSpec((width, width), lambda r: (0, 0)),
-        ],
-        out_specs=[
-            pl.BlockSpec((fields, depth, step, width), lambda r: (0, 0, r, 0)),
-        ]
-        + [
-            pl.BlockSpec((fields, count, step, width), lambda r: (0, 0, r, 0)) for count in counts
-        ],
-        out_shape=[jax.ShapeDtypeStruct(adjoint.shape, jnp.float32)]
-        + [jax.ShapeDtypeStruct((fields, count, rows, width), jnp.float32) for count in counts],
-        scratch_shapes=[pltpu.VMEM((fields, depth, step, width), jnp.float32)],
-        name="along_x",
-        cost_estimate=pl.CostEstimate(
-            flops=6 * fields * depth * rows * width * width,
-            bytes_accessed=6 * 1024 * 1024,
-            transcendentals=0,
-        ),
-    )(coupling, adjoint, speed, x_derivative)
-
-
-def along_z_kernel(coupling_ref, base_ref, adjoint_ref, low_ref, high_ref, speed_ref, out_ref):
-    fields, depth, _, _ = adjoint_ref.shape
 
     def plane(g, k):
         if k < 0:
-            return low_ref[g, HALO + k]
+            return full_ref[g, HALO + k]
         if k >= depth:
-            return high_ref[g, k - depth]
+            return full_ref[g, HALO + k - depth]
         return adjoint_ref[g, k]
 
     for z in range(depth):
@@ -322,37 +339,46 @@
                 term = weight * (plane(g, z + step + 1) - plane(g, z - step - 1))
                 total = term if total is None else total + term
             grads.append(total)
+        firsts = [gx_ref[g, z] for g in range(fields)]
         speed = speed_ref[z] * stepping
         for f in range(fields):
-            out_ref[f, z] = base_ref[f, z] + speed * mixed(coupling_ref, 2, grads, f)
-
-
-def along_z(coupling, base, adjoint, low, high, speed):
+            total = mixed(coupling_ref, 0, firsts, f) + mixed(coupling_ref, 2, grads, f)
+            out_ref[f, z] = adjoint_ref[f, z] + speed * total
+
+
+def local_terms(column, coupling, adjoint, low, high, near, far, speed, x_derivative):
     fields, depth, rows, width = adjoint.shape
     step = 8
     whole = pl.BlockSpec((fields, depth, step, width), lambda r: (0, 0, r, 0))
     side = pl.BlockSpec((fields, HALO, step, width), lambda r: (0, 0, r, 0))
-    return pl.pallas_call(
-        along_z_kernel,
+    part = pl.BlockSpec((fields, HALO // 2, step, width), lambda r: (0, 0, r, 0))
+    return pl.pallas_call(
+        local_kernel,
         grid=(rows // step,),
         in_specs=[
             pl.BlockSpec(memory_space=pltpu.SMEM),
-            whole,
+            pl.BlockSpec(memory_space=pltpu.SMEM),
             whole,
             side,
             side,
+            part,
+            part,
             pl.BlockSpec((depth, step, width), lambda r: (0, r, 0)),
+            pl.BlockSpec((width, width), lambda r: (0, 0)),
         ],
         out_specs=whole,
         out_shape=jax.ShapeDtypeStruct(adjoint.shape, jnp.float32),
-        input_output_aliases={1: 0},
-        name="along_z",
+        scratch_shapes=[
+            pltpu.VMEM((fields, 2 * HALO, step, width), jnp.float32),
+            pltpu.VMEM((fields, depth, step, width), jnp.float32),
+        ],
+        name="local",
         cost_estimate=pl.CostEstimate(
-            flops=70 * fields * depth * rows * width,
+            flops=6 * fields * depth * rows * width * width,
             bytes_accessed=12 * 1024 * 1024,
             transcendentals=0,
         ),
-    )(coupling, base, adjoint, low, high, speed)
+    )(column, coupling, adjoint, low, high, near, far, speed, x_derivative)
 
 
 def join_kernel(me_ref, base_ref, *refs, where):
@@ -412,7 +438,9 @@
     _, depth, rows, _ = adjoint.shape
     chips = lax.axis_size("gy") // 2
     assert chips == depth == 8 and y_operators.shape[1] == 16 * rows
+    coupling = jnp.transpose(coupling, (1, 0, 2))
     me = lax.axis_index("gy").astype(jnp.int32)[None]
+    column = (lax.axis_index("gz").astype(jnp.int32) & 3)[None]
     pieces = pack(me, adjoint, speed)
     same = [pieces[0]]
     for o in range(1, 8):
@@ -421,17 +449,23 @@
     for o in range(8):
         other.append(lax.ppermute(same[o], "gy", CORE_SWAP))
 
-    result, top, bottom = along_x(coupling, adjoint, speed, x_derivative)
-    count = lax.axis_size("gz")
-    forward = [(i, (i + 1) % count) for i in range(count)]
-    backward = [(i, (i - 1) % count) for i in range(count)]
-    low = lax.ppermute(top, "gz", forward)
-    high = lax.ppermute(bottom, "gz", backward)
+    top, bottom, near, far = edges(column, adjoint)
+    runs = [4 * r for r in range(lax.axis_size("gz") // 4)]
+    near = lax.ppermute(near, "gz", [p for r in runs for p in ((r + 3, r), (r, r + 3))])
+    far = lax.ppermute(far, "gz", [p for r in runs for p in ((r + 3, r + 1), (r, r + 2))])
+    low = lax.ppermute(top, "gz", [(r + x, r + (x + 1) % 4) for r in runs for x in range(4)])
+    high = lax.ppermute(bottom, "gz", [(r + (x + 1) % 4, r + x) for r in runs for x in range(4)])
+    ends = (column[0] == 0) | (column[0] == 3)
+    crossing = jnp.where(ends, near, far)
+    near = lax.ppermute(crossing, "gz", [(r + x, (r ^ 4) + x) for r in runs for x in range(4)])
+    far = lax.ppermute(near, "gz", [p for r in runs for p in ((r + 1, r), (r + 2, r + 3))])
 
     early, late = own_operators(me, y_operators, chips, rows)
     sums = early_lines(me, early, same[:EARLY], other[:EARLY])
     parts = late_lines(me, coupling, late, sums, same[EARLY:], other[EARLY:], same)
-    result = along_z(coupling, result, adjoint, low, high, speed)
+    result = local_terms(
+        column, coupling, adjoint, low, high, near, far, speed, x_derivative
+    )
     arrived = [parts[0]]
     for o in range(1, 8):
         arrived.append(lax.ppermute(parts[o], "gy", chip_perm(*OFFSETS[o])))

time: 129 us -> 138 us (1.070); the launches traced: 128 us -> 135 us
  starting transfers between devices: 56.1 us -> 66.6 us
  waiting for transfers between devices: 19.1 us -> 16.6 us
  local copies, waits for them, and re-layouts: 2.91 us -> 1.52 us
    ppermute x2 -> x6, starting transfers between devices: 4.85 us -> 10.5 us  [the longest x1 4.37 us: shards(): lax.ppermute(near, 'gz', [p for r in runs for p in ((r + 3, r), (r, r + 3...]
    ppermute x8, starting transfers between devices: 22 us -> 26.6 us  [shards(): other.append(lax.ppermute(same[o], 'gy', CORE_SWAP))]
    ppermute x7, waiting for transfers between devices: 15.7 us -> 13.9 us  [shards(): arrived.append(lax.ppermute(parts[o], 'gy', chip_perm(*OFFSETS[o])))]
    unnamed x29 -> x26, local copies, waits for them, and re-layouts: 2.91 us -> 1.52 us
  transfers between devices with their start and end apart: 24 -> 28, of which waited for: 4 -> 5; matrix products, arithmetic and copies ran while one was open for 0% -> 1% of each run, Pallas kernels for 35% -> 32%
where the time goes in v1:
time: 138 us; the launch traced here: 135 us
  starting transfers between devices  66.6 us (48%)
  Pallas kernels  48.9 us (35%)
  waiting for transfers between devices  16.6 us (12%)
  local copies, waits for them, and re-layouts  1.52 us (1%)
    ppermute x8, starting transfers between devices, shards(): other.append(lax.ppermute(same[o], 'gy', CORE_SWAP))  26.6 us
    ppermute x7, starting transfers between devices, shards(): same.append(lax.ppermute(pieces[o], 'gy', chip_perm(*OFFSETS[o])))  17.2 us
    ppermute x7, waiting for transfers between devices, shards(): arrived.append(lax.ppermute(parts[o], 'gy', chip_perm(*OFFSETS[o])))  13.9 us
    ppermute x7, starting transfers between devices, shards(): arrived.append(lax.ppermute(parts[o], 'gy', chip_perm(*OFFSETS[o])))  12.3 us
    pallas_call x1, Pallas kernels, late_lines(): pl.pallas_call(late_kernel, grid_spec=pltpu.PrefetchScalarGridSpec(num_sc...  11.4 us
    pallas_call x1, Pallas kernels, local_terms(): pl.pallas_call(local_kernel, grid=(rows // step,), in_specs=[pl.BlockSpec...  9.81 us
    pallas_call x1, Pallas kernels, early_lines(): pl.pallas_call(early_kernel, grid_spec=pltpu.PrefetchScalarGridSpec(num_s...  9.39 us
    pallas_call x3, Pallas kernels, join(): pl.pallas_call(functools.partial(join_kernel, where=where), in_specs=[pl....  6.69 us
  transfers between devices with their start and end apart: 28, of which 5 were waited for; matrix products, arithmetic and copies ran while one was open for 1% of the time, Pallas kernels for 32%

profile of v1, /device:TPU:1, one launch (start us, length us, event | category | flops | bytes accessed | tf_op | source)
XLA Modules:
  0.0 134.8 jit_solution(12182631955931209646)
XLA Ops:
  0.0 2.8 %pack.1 = (f32[6,64,256]{2,1,0:T(8,128)}, f32[6,64,256]{2,1,0:T(8,128)}, f32[6,64,256]{2,1,0:T(8,128)}, f32[6,64,256]{2,1,0:T(8,128)}, f32[6,64,256]{2,1,0:T(8,1...) custom-call(s32[1]{0:T(128)} %bitcast.me_ref, f32[5,8,64,256]{3,2,1,0:T(8,128)} %adjoint_ref.5, ...), custom_call_target="tpu_custom_call" | custom-call | bytes 6291456 | tf_op jit(solution)/shard_map/pack/pallas_call | solution.py:81
  2.8 2.5 %collective-permute-start.6 = (f32[6,64,256]{2,1,0:T(8,128)}, f32[6,64,256]{2,1,0:T(8,128)S(1)}, u32[]{:S(2)}, u32[]{:S(2)}) collective-permute-start(f32[6,64,256]{2,1,0:T(8,128)} %get-tuple-element.34), channel_id=1, source_target_pairs={{0,32},{8,40},{16,48},{24,56},{32,64},{40,72},{48,80},{56,88},{64,... | collective-permute-start | bytes 1179656 | tf_op jit(solution)/shard_map/ppermute | solution.py:447
  5.4 2.2 %collective-permute-start.7 = (f32[6,64,256]{2,1,0:T(8,128)}, f32[6,64,256]{2,1,0:T(8,128)S(1)}, u32[]{:S(2)}, u32[]{:S(2)}) collective-permute-start(f32[6,64,256]{2,1,0:T(8,128)} %get-tuple-element.35), channel_id=1, source_target_pairs={{0,96},{8,104},{16,112},{24,120},{32,0},{40,8},{48,16},{56,24},{64... | collective-permute-start | bytes 1179656 | tf_op jit(solution)/shard_map/ppermute | solution.py:447
  7.6 2.9 %collective-permute-start.8 = (f32[6,64,256]{2,1,0:T(8,128)}, f32[6,64,256]{2,1,0:T(8,128)S(1)}, u32[]{:S(2)}, u32[]{:S(2)}) collective-permute-start(f32[6,64,256]{2,1,0:T(8,128)} %get-tuple-element.36), channel_id=1, source_target_pairs={{0,16},{8,24},{16,0},{24,8},{32,48},{40,56},{48,32},{56,40},{64,80... | collective-permute-start | bytes 1179656 | tf_op jit(solution)/shard_map/ppermute | solution.py:447
  10.5 1.2 collective-permute-start.9
  11.7 1.5 %collective-permute-start.13 = (f32[6,64,256]{2,1,0:T(8,128)}, f32[6,64,256]{2,1,0:T(8,128)}, u32[]{:S(2)}, u32[]{:S(2)}) collective-permute-start(f32[6,64,256]{2,1,0:T(8,128)} %get-tuple-element.37), channel_id=1, source_target_pairs={{0,64},{8,72},{16,80},{24,88},{32,96},{40,104},{48,112},{56,120},{... | collective-permute-start | bytes 1179656 | tf_op jit(solution)/shard_map/ppermute | solution.py:447
  13.2 3.2 %edges.1 = (f32[5,4,64,256]{3,2,1,0:T(8,128)}, f32[5,4,64,256]{3,2,1,0:T(8,128)}, f32[5,2,64,256]{3,2,1,0:T(8,128)}, f32[5,2,64,256]{3,2,1,0:T(8,128)}) custom-call(s32[1]{0:T(128)} %bitcast.1.column_ref, f32[5,8,64,256]{3,2,1,0:T(8,128)} %adjoint_ref.5), custom_call_target="tpu_custom_call" | custom-call | bytes 7340032 | tf_op jit(solution)/shard_map/edges/pallas_call | solution.py:290
  16.4 0.1 collective-permute-done.6.refs_1_.refs_10_
  16.5 4.4 %collective-permute-start.2 = (f32[5,2,64,256]{3,2,1,0:T(8,128)}, f32[5,2,64,256]{3,2,1,0:T(8,128)S(1)}, u32[]{:S(2)}, u32[]{:S(2)}) collective-permute-start(f32[5,2,64,256]{3,2,1,0:T(8,128)} %get-tuple-element.29), channel_id=1, source_target_pairs={{3,0},{0,3},{7,4},{4,7},{11,8},{8,11},{15,12},{12,15},{19,16},{16,... | collective-permute-start | bytes 1966088 | tf_op jit(solution)/shard_map/ppermute | solution.py:454
  20.9 0.0 collective-permute-done.7.refs_2_.refs_9_
  20.9 1.3 collective-permute-start.3
  22.3 0.0 collective-permute-done.8.refs_3_.refs_11_
  22.3 2.1 %collective-permute-start.14 = (f32[6,64,256]{2,1,0:T(8,128)}, f32[6,64,256]{2,1,0:T(8,128)}, u32[]{:S(2)}, u32[]{:S(2)}) collective-permute-start(f32[6,64,256]{2,1,0:T(8,128)} %get-tuple-element.38), channel_id=1, source_target_pairs={{0,48},{8,56},{16,32},{24,40},{32,80},{40,88},{48,64},{56,72},{64,... | collective-permute-start | bytes 1179656 | tf_op jit(solution)/shard_map/ppermute | solution.py:447
  24.3 0.0 collective-permute-done.9.refs_4_
  24.3 3.1 %collective-permute-start.15 = (f32[6,64,256]{2,1,0:T(8,128)}, f32[6,64,256]{2,1,0:T(8,128)S(1)}, u32[]{:S(2)}, u32[]{:S(2)}) collective-permute-start(f32[6,64,256]{2,1,0:T(8,128)} %get-tuple-element.39), channel_id=1, source_target_pairs={{0,112},{8,120},{16,96},{24,104},{32,16},{40,24},{48,0},{56,8},{64... | collective-permute-start | bytes 1179656 | tf_op jit(solution)/shard_map/ppermute | solution.py:447
  27.4 0.0 collective-permute-done.13.refs_0_.refs_12_
  27.4 2.9 %collective-permute-start.16 = (f32[6,64,256]{2,1,0:T(8,128)S(1)}, f32[6,64,256]{2,1,0:T(8,128)S(1)}, u32[]{:S(2)}, u32[]{:S(2)}) collective-permute-start(f32[6,64,256]{2,1,0:T(8,128)S(1)} %copy-done.12), channel_id=1, source_target_pairs={{0,80},{8,88},{16,64},{24,72},{32,112},{40,120},{48,96},{56,104},{... | collective-permute-start | bytes 1179656 | tf_op jit(solution)/shard_map/ppermute | solution.py:447
  30.3 2.6 %collective-permute-done.14.refs_1_.refs_14_ = f32[6,64,256]{2,1,0:T(8,128)} collective-permute-done((f32[6,64,256]{2,1,0:T(8,128)}, f32[6,64,256]{2,1,0:T(8,128)}, u32[]{:S(2)}, u32[]{:S(2)}) %collective-permute-start.14) | collective-permute-done | bytes 393248 | tf_op jit(solution)/shard_map/ppermute | solution.py:447
  32.9 14.2 %collective-permute-start.10 = (f32[6,64,256]{2,1,0:T(8,128)S(1)}, f32[6,64,256]{2,1,0:T(8,128)}, u32[]{:S(2)}, u32[]{:S(2)}) collective-permute-start(f32[6,64,256]{2,1,0:T(8,128)S(1)} %collective-permute-done.6.refs_1_.refs_10_), channel_id=1, source_target_pairs={{0,8},{8,0},{16,24},{24,16},{32,40},{40,32},{48,56},{56,48},{64,72... | collective-permute-start | bytes 1179656 | tf_op jit(solution)/shard_map/ppermute | solution.py:450
  47.1 0.0 collective-permute-done.15.refs_2_.refs_13_
  47.1 3.2 %collective-permute-start.11 = (f32[6,64,256]{2,1,0:T(8,128)S(1)}, f32[6,64,256]{2,1,0:T(8,128)}, u32[]{:S(2)}, u32[]{:S(2)}) collective-permute-start(f32[6,64,256]{2,1,0:T(8,128)S(1)} %collective-permute-done.7.refs_2_.refs_9_), channel_id=1, source_target_pairs={{0,8},{8,0},{16,24},{24,16},{32,40},{40,32},{48,56},{56,48},{64,72... | collective-permute-start | bytes 1179656 | tf_op jit(solution)/shard_map/ppermute | solution.py:450
  50.3 0.0 collective-permute-done.16.refs_3_.refs_15_
  50.3 0.7 copy-done.11
  51.1 6.4 %collective-permute-start.12 = (f32[6,64,256]{2,1,0:T(8,128)S(1)}, f32[6,64,256]{2,1,0:T(8,128)}, u32[]{:S(2)}, u32[]{:S(2)}) collective-permute-start(f32[6,64,256]{2,1,0:T(8,128)S(1)} %collective-permute-done.8.refs_3_.refs_11_), channel_id=1, source_target_pairs={{0,8},{8,0},{16,24},{24,16},{32,40},{40,32},{48,56},{56,48},{64,72... | collective-permute-start | bytes 1179656 | tf_op jit(solution)/shard_map/ppermute | solution.py:450
  57.5 0.0 collective-permute-done.2
  57.5 0.0 collective-permute-start.17
  57.5 0.0 collective-permute-done.3
  57.5 0.5 collective-permute-start.18
  58.0 0.9 broadcast_select_fusion
  59.0 0.0 collective-permute-done.10.refs_5_
  59.0 0.8 collective-permute-start.4
  59.8 0.0 collective-permute-done.11.refs_6_
  59.8 0.0 collective-permute-start
  59.8 0.0 collective-permute-done.12.refs_7_
  59.8 2.7 %collective-permute-start.1 = (f32[5,4,64,256]{3,2,1,0:T(8,128)}, f32[5,4,64,256]{3,2,1,0:T(8,128)S(1)}, u32[]{:S(2)}, u32[]{:S(2)}) collective-permute-start(f32[5,4,64,256]{3,2,1,0:T(8,128)} %get-tuple-element.28), channel_id=1, source_target_pairs={{1,0},{2,1},{3,2},{0,3},{5,4},{6,5},{7,6},{4,7},{9,8},{10,9},{11,1... | collective-permute-start | bytes 3932168 | tf_op jit(solution)/shard_map/ppermute | solution.py:457
  62.5 0.0 collective-permute-done.17.refs_4_
  62.5 0.9 collective-permute-start.19
  63.5 0.0 collective-permute-done.18.refs_5_
  63.5 0.1 collective-permute-start.20
  63.5 5.5 %operators.1 = (bf16[2,8,64,1536]{3,2,1,0:T(8,128)(2,1)}, bf16[2,8,64,1536]{3,2,1,0:T(8,128)(2,1)}) custom-call(s32[1]{0:T(128)} %bitcast.me_ref, f32[2,8,2,64,1024]{4,3,2,1,0:T(8,128)} %bitcast.6), custom_call_target="tpu_custom_call" | custom-call | flops 4194304 | bytes 10485760 | tf_op jit(solution)/shard_map/operators/pallas_call | solution.py:117
  69.1 9.4 %early_lines.1.sums_ref = f32[5,1024,256]{2,1,0:T(8,128)} custom-call(s32[1]{0:T(128)} %bitcast.me_ref, bf16[1024,1536]{1,0:T(8,128)(2,1)} %bitcast.10, f32[6,64,256]{2,1,0:T(8,128)} %get-tuple-element.33.refs_0_.refs_8_, f32[6,64,256]{2,1,0:T(8,128)} %copy-done.6, f32[6,64,256]{2,1,0:T(8,128)} %copy-done.7, f32[6,64,256]{2,1,0:T(8,128)} %copy-done.8, ...), custom_call_target="tpu_custom_call" | custom-call | flops 4026531840 | bytes 12582912 | tf_op jit(solution)/shard_map/early_lines/pallas_call | solution.py:162
  78.5 0.0 collective-permute-done.4.near_ref
  78.5 1.3 collective-permute-start.5
  79.8 0.0 collective-permute-done.20.refs_7_
  79.8 11.4 %late_lines.1 = (f32[5,64,256]{2,1,0:T(8,128)}, f32[5,64,256]{2,1,0:T(8,128)}, f32[5,64,256]{2,1,0:T(8,128)}, f32[5,64,256]{2,1,0:T(8,128)}, f32[5,64,256]{2,1,0...) custom-call(s32[1]{0:T(128)} %bitcast.me_ref, f32[5,3,5]{2,1,0:T(4,128)} %bitcast.7, ...), custom_call_target="tpu_custom_call" | custom-call | flops 4026531840 | bytes 16777216 | tf_op jit(solution)/shard_map/late_lines/pallas_call | solution.py:219
  91.3 0.1 collective-permute-start.21
  91.3 2.7 %collective-permute-start.22 = (f32[5,64,256]{2,1,0:T(8,128)}, f32[5,64,256]{2,1,0:T(8,128)S(1)}, u32[]{:S(2)}, u32[]{:S(2)}) collective-permute-start(f32[5,64,256]{2,1,0:T(8,128)} %get-tuple-element.43), channel_id=1, source_target_pairs={{0,96},{8,104},{16,112},{24,120},{32,0},{40,8},{48,16},{56,24},{64... | collective-permute-start | bytes 983048 | tf_op jit(solution)/shard_map/ppermute | solution.py:471
  94.0 7.7 %collective-permute-done.21.refs_1_ = f32[5,64,256]{2,1,0:T(8,128)S(1)} collective-permute-done((f32[5,64,256]{2,1,0:T(8,128)}, f32[5,64,256]{2,1,0:T(8,128)S(1)}, u32[]{:S(2)}, u32[]{:S(2)}) %collective-permute-start.21) | collective-permute-done | bytes 327712 | tf_op jit(solution)/shard_map/ppermute | solution.py:471
  101.7 2.0 %collective-permute-start.23 = (f32[5,64,256]{2,1,0:T(8,128)}, f32[5,64,256]{2,1,0:T(8,128)}, u32[]{:S(2)}, u32[]{:S(2)}) collective-permute-start(f32[5,64,256]{2,1,0:T(8,128)} %get-tuple-element.44), channel_id=1, source_target_pairs={{0,16},{8,24},{16,0},{24,8},{32,48},{40,56},{48,32},{56,40},{64,80... | collective-permute-start | bytes 983048 | tf_op jit(solution)/shard_map/ppermute | solution.py:471
  103.7 0.0 collective-permute-done.22.refs_2_
  103.7 0.0 collective-permute-done.low_ref
  103.7 2.7 %collective-permute-start.25 = (f32[5,64,256]{2,1,0:T(8,128)}, f32[5,64,256]{2,1,0:T(8,128)}, u32[]{:S(2)}, u32[]{:S(2)}) collective-permute-start(f32[5,64,256]{2,1,0:T(8,128)} %get-tuple-element.46), channel_id=1, source_target_pairs={{0,48},{8,56},{16,32},{24,40},{32,80},{40,88},{48,64},{56,72},{64,... | collective-permute-start | bytes 983048 | tf_op jit(solution)/shard_map/ppermute | solution.py:471
  106.4 2.5 %collective-permute-start.26 = (f32[5,64,256]{2,1,0:T(8,128)}, f32[5,64,256]{2,1,0:T(8,128)}, u32[]{:S(2)}, u32[]{:S(2)}) collective-permute-start(f32[5,64,256]{2,1,0:T(8,128)} %get-tuple-element.47), channel_id=1, source_target_pairs={{0,112},{8,120},{16,96},{24,104},{32,16},{40,24},{48,0},{56,8},{64... | collective-permute-start | bytes 983048 | tf_op jit(solution)/shard_map/ppermute | solution.py:471
  108.9 2.4 %collective-permute-start.27 = (f32[5,64,256]{2,1,0:T(8,128)}, f32[5,64,256]{2,1,0:T(8,128)S(1)}, u32[]{:S(2)}, u32[]{:S(2)}) collective-permute-start(f32[5,64,256]{2,1,0:T(8,128)} %get-tuple-element.48), channel_id=1, source_target_pairs={{0,80},{8,88},{16,64},{24,72},{32,112},{40,120},{48,96},{56,104},{... | collective-permute-start | bytes 983048 | tf_op jit(solution)/shard_map/ppermute | solution.py:471
  111.3 9.8 %local.1.base_ref = f32[5,8,64,256]{3,2,1,0:T(8,128)} custom-call(s32[1]{0:T(128)} %bitcast.1.column_ref, f32[5,3,5]{2,1,0:T(4,128)} %bitcast.8, f32[5,8,64,256]{3,2,1,0:T(8,128)} %adjoint_ref.5, f32[5,4,64,256]{3,2,1,0:T(8,128)} %copy-done, f32[5,4,64,256]{3,2,1,0:T(8,128)} %copy-done.1, f32[5,2,64,256]{3,2,1,0:T(8,128)} %copy-done.2, ...), custom_call_target="tpu_custom_call" | custom-call | flops 1006632960 | bytes 12582912 | tf_op jit(solution)/shard_map/local/pallas_call | solution.py:355
  121.1 2.3 %join.3.base_ref = f32[5,8,64,256]{3,2,1,0:T(8,128)} custom-call(s32[1]{0:T(128)} %bitcast.me_ref, f32[5,8,64,256]{3,2,1,0:T(8,128)} %local.1.base_ref, f32[5,64,256]{2,1,0:T(8,128)} %get-tuple-element.41.refs_0_, f32[5,64,256]{2,1,0:T(8,128)} %copy-done.3, f32[5,64,256]{2,1,0:T(8,128)} %copy-done.4), custom_call_target="tpu_custom_call", output_to_operand_aliasing={{}: (1, {})} | custom-call | flops 245760 | bytes 3145728 | tf_op jit(solution)/shard_map/join/pallas_call | solution.py:416
  123.4 0.0 collective-permute-done.23.refs_0_
  123.4 0.0 collective-permute-done.24.refs_1_
  123.4 2.1 %join.4.base_ref = f32[5,8,64,256]{3,2,1,0:T(8,128)} custom-call(s32[1]{0:T(128)} %bitcast.me_ref, f32[5,8,64,256]{3,2,1,0:T(8,128)} %join.3.base_ref, f32[5,64,256]{2,1,0:T(8,128)} %collective-permute-done.23.refs_0_, f32[5,64,256]{2,1,0:T(8,128)} %collective-permute-done.24.refs_1_), custom_call_target="tpu_custom_call", output_to_operand_aliasing={{}: (1, {})} | custom-call | flops 163840 | bytes 2097152 | tf_op jit(solution)/shard_map/join/pallas_call | solution.py:416
  125.5 0.0 collective-permute-done.25.refs_0_
  125.5 0.5 collective-permute-done.26.refs_1_
  126.1 5.7 %collective-permute-done.27.refs_2_ = f32[5,64,256]{2,1,0:T(8,128)S(1)} collective-permute-done((f32[5,64,256]{2,1,0:T(8,128)}, f32[5,64,256]{2,1,0:T(8,128)S(1)}, u32[]{:S(2)}, u32[]{:S(2)}) %collective-permute-start.27) | collective-permute-done | bytes 327712 | tf_op jit(solution)/shard_map/ppermute | solution.py:471
  131.8 0.7 copy-done.5
  132.5 2.3 %join.5 = f32[5,8,64,256]{3,2,1,0:T(8,128)} custom-call(s32[1]{0:T(128)} %bitcast.me_ref, f32[5,8,64,256]{3,2,1,0:T(8,128)} %join.4.base_ref, f32[5,64,256]{2,1,0:T(8,128)} %collective-permute-done.25.refs_0_, f32[5,64,256]{2,1,0:T(8,128)} %collective-permute-done.26.refs_1_, f32[5,64,256]{2,1,0:T(8,128)} %copy-done.5), custom_call_target="tpu_custom_call", output_to_operand_aliasing={{}: (1, {})} | custom-call | flops 245760 | bytes 3145728 | tf_op jit(solution)/shard_map/join/pallas_call | solution.py:416
  (28 shorter events, 0.1 us)
Async XLA Ops:
  2.8 24.6 %copy-start.12 = (f32[6,64,256]{2,1,0:T(8,128)S(1)}, f32[6,64,256]{2,1,0:T(8,128)}, u32[]{:S(2)}) copy-start(f32[6,64,256]{2,1,0:T(8,128)} %get-tuple-element.40) | copy-start | bytes 1179652
  2.8 13.7 %collective-permute-start.6 = (f32[6,64,256]{2,1,0:T(8,128)}, f32[6,64,256]{2,1,0:T(8,128)S(1)}, u32[]{:S(2)}, u32[]{:S(2)}) collective-permute-start(f32[6,64,256]{2,1,0:T(8,128)} %get-tuple-element.34), channel_id=1, source_target_pairs={{0,32},{8,40},{16,48},{24,56},{32,64},{40,72},{48,80},{56,88},{64,... | collective-permute-start | bytes 1179656 | tf_op jit(solution)/shard_map/ppermute | solution.py:447
  5.4 15.5 %collective-permute-start.7 = (f32[6,64,256]{2,1,0:T(8,128)}, f32[6,64,256]{2,1,0:T(8,128)S(1)}, u32[]{:S(2)}, u32[]{:S(2)}) collective-permute-start(f32[6,64,256]{2,1,0:T(8,128)} %get-tuple-element.35), channel_id=1, source_target_pairs={{0,96},{8,104},{16,112},{24,120},{32,0},{40,8},{48,16},{56,24},{64... | collective-permute-start | bytes 1179656 | tf_op jit(solution)/shard_map/ppermute | solution.py:447
  7.6 14.7 %collective-permute-start.8 = (f32[6,64,256]{2,1,0:T(8,128)}, f32[6,64,256]{2,1,0:T(8,128)S(1)}, u32[]{:S(2)}, u32[]{:S(2)}) collective-permute-start(f32[6,64,256]{2,1,0:T(8,128)} %get-tuple-element.36), channel_id=1, source_target_pairs={{0,16},{8,24},{16,0},{24,8},{32,48},{40,56},{48,32},{56,40},{64,80... | collective-permute-start | bytes 1179656 | tf_op jit(solution)/shard_map/ppermute | solution.py:447
  10.5 13.9 %collective-permute-start.9 = (f32[6,64,256]{2,1,0:T(8,128)}, f32[6,64,256]{2,1,0:T(8,128)S(1)}, u32[]{:S(2)}, u32[]{:S(2)}) collective-permute-start(f32[6,64,256]{2,1,0:T(8,128)} %get-tuple-element.33.refs_0_.refs_8_), channel_id=1, source_target_pairs={{0,8},{8,0},{16,24},{24,16},{32,40},{40,32},{48,56},{56,48},{64,72... | collective-permute-start | bytes 1179656 | tf_op jit(solution)/shard_map/ppermute | solution.py:450
  11.7 15.7 %collective-permute-start.13 = (f32[6,64,256]{2,1,0:T(8,128)}, f32[6,64,256]{2,1,0:T(8,128)}, u32[]{:S(2)}, u32[]{:S(2)}) collective-permute-start(f32[6,64,256]{2,1,0:T(8,128)} %get-tuple-element.37), channel_id=1, source_target_pairs={{0,64},{8,72},{16,80},{24,88},{32,96},{40,104},{48,112},{56,120},{... | collective-permute-start | bytes 1179656 | tf_op jit(solution)/shard_map/ppermute | solution.py:447
  16.5 42.5 %copy-start.6 = (f32[6,64,256]{2,1,0:T(8,128)}, f32[6,64,256]{2,1,0:T(8,128)S(1)}, u32[]{:S(2)}) copy-start(f32[6,64,256]{2,1,0:T(8,128)S(1)} %collective-permute-done.6.refs_1_.refs_10_) | copy-start | bytes 1179652
  16.5 41.0 %collective-permute-start.2 = (f32[5,2,64,256]{3,2,1,0:T(8,128)}, f32[5,2,64,256]{3,2,1,0:T(8,128)S(1)}, u32[]{:S(2)}, u32[]{:S(2)}) collective-permute-start(f32[5,2,64,256]{3,2,1,0:T(8,128)} %get-tuple-element.29), channel_id=1, source_target_pairs={{3,0},{0,3},{7,4},{4,7},{11,8},{8,11},{15,12},{12,15},{19,16},{16,... | collective-permute-start | bytes 1966088 | tf_op jit(solution)/shard_map/ppermute | solution.py:454
  20.9 38.9 %copy-start.7 = (f32[6,64,256]{2,1,0:T(8,128)}, f32[6,64,256]{2,1,0:T(8,128)S(1)}, u32[]{:S(2)}) copy-start(f32[6,64,256]{2,1,0:T(8,128)S(1)} %collective-permute-done.7.refs_2_.refs_9_) | copy-start | bytes 1179652
  20.9 36.6 %collective-permute-start.3 = (f32[5,2,64,256]{3,2,1,0:T(8,128)}, f32[5,2,64,256]{3,2,1,0:T(8,128)S(1)}, u32[]{:S(2)}, u32[]{:S(2)}) collective-permute-start(f32[5,2,64,256]{3,2,1,0:T(8,128)} %get-tuple-element.30), channel_id=1, source_target_pairs={{3,1},{0,2},{7,5},{4,6},{11,9},{8,10},{15,13},{12,14},{19,17},{16,... | collective-permute-start | bytes 1966088 | tf_op jit(solution)/shard_map/ppermute | solution.py:455
  22.3 37.5 %copy-start.8 = (f32[6,64,256]{2,1,0:T(8,128)}, f32[6,64,256]{2,1,0:T(8,128)S(1)}, u32[]{:S(2)}) copy-start(f32[6,64,256]{2,1,0:T(8,128)S(1)} %collective-permute-done.8.refs_3_.refs_11_) | copy-start | bytes 1179652
  22.3 10.6 %collective-permute-start.14 = (f32[6,64,256]{2,1,0:T(8,128)}, f32[6,64,256]{2,1,0:T(8,128)}, u32[]{:S(2)}, u32[]{:S(2)}) collective-permute-start(f32[6,64,256]{2,1,0:T(8,128)} %get-tuple-element.38), channel_id=1, source_target_pairs={{0,48},{8,56},{16,32},{24,40},{32,80},{40,88},{48,64},{56,72},{64,... | collective-permute-start | bytes 1179656 | tf_op jit(solution)/shard_map/ppermute | solution.py:447
  24.3 35.5 %copy-start.9 = (f32[6,64,256]{2,1,0:T(8,128)}, f32[6,64,256]{2,1,0:T(8,128)S(1)}, u32[]{:S(2)}) copy-start(f32[6,64,256]{2,1,0:T(8,128)S(1)} %collective-permute-done.9.refs_4_) | copy-start | bytes 1179652
  24.3 22.8 %collective-permute-start.15 = (f32[6,64,256]{2,1,0:T(8,128)}, f32[6,64,256]{2,1,0:T(8,128)S(1)}, u32[]{:S(2)}, u32[]{:S(2)}) collective-permute-start(f32[6,64,256]{2,1,0:T(8,128)} %get-tuple-element.39), channel_id=1, source_target_pairs={{0,112},{8,120},{16,96},{24,104},{32,16},{40,24},{48,0},{56,8},{64... | collective-permute-start | bytes 1179656 | tf_op jit(solution)/shard_map/ppermute | solution.py:447
  27.4 22.9 %collective-permute-start.16 = (f32[6,64,256]{2,1,0:T(8,128)S(1)}, f32[6,64,256]{2,1,0:T(8,128)S(1)}, u32[]{:S(2)}, u32[]{:S(2)}) collective-permute-start(f32[6,64,256]{2,1,0:T(8,128)S(1)} %copy-done.12), channel_id=1, source_target_pairs={{0,80},{8,88},{16,64},{24,72},{32,112},{40,120},{48,96},{56,104},{... | collective-permute-start | bytes 1179656 | tf_op jit(solution)/shard_map/ppermute | solution.py:447
  32.9 26.1 %collective-permute-start.10 = (f32[6,64,256]{2,1,0:T(8,128)S(1)}, f32[6,64,256]{2,1,0:T(8,128)}, u32[]{:S(2)}, u32[]{:S(2)}) collective-permute-start(f32[6,64,256]{2,1,0:T(8,128)S(1)} %collective-permute-done.6.refs_1_.refs_10_), channel_id=1, source_target_pairs={{0,8},{8,0},{16,24},{24,16},{32,40},{40,32},{48,56},{56,48},{64,72... | collective-permute-start | bytes 1179656 | tf_op jit(solution)/shard_map/ppermute | solution.py:450
  47.1 3.2 %copy-start.10 = (f32[6,64,256]{2,1,0:T(8,128)}, f32[6,64,256]{2,1,0:T(8,128)S(1)}, u32[]{:S(2)}) copy-start(f32[6,64,256]{2,1,0:T(8,128)S(1)} %collective-permute-done.15.refs_2_.refs_13_) | copy-start | bytes 1179652
  47.1 12.7 %collective-permute-start.11 = (f32[6,64,256]{2,1,0:T(8,128)S(1)}, f32[6,64,256]{2,1,0:T(8,128)}, u32[]{:S(2)}, u32[]{:S(2)}) collective-permute-start(f32[6,64,256]{2,1,0:T(8,128)S(1)} %collective-permute-done.7.refs_2_.refs_9_), channel_id=1, source_target_pairs={{0,8},{8,0},{16,24},{24,16},{32,40},{40,32},{48,56},{56,48},{64,72... | collective-permute-start | bytes 1179656 | tf_op jit(solution)/shard_map/ppermute | solution.py:450
  50.3 0.8 copy-start.11
  51.1 8.7 %collective-permute-start.12 = (f32[6,64,256]{2,1,0:T(8,128)S(1)}, f32[6,64,256]{2,1,0:T(8,128)}, u32[]{:S(2)}, u32[]{:S(2)}) collective-permute-start(f32[6,64,256]{2,1,0:T(8,128)S(1)} %collective-permute-done.8.refs_3_.refs_11_), channel_id=1, source_target_pairs={{0,8},{8,0},{16,24},{24,16},{32,40},{40,32},{48,56},{56,48},{64,72... | collective-permute-start | bytes 1179656 | tf_op jit(solution)/shard_map/ppermute | solution.py:450
  57.5 5.0 %collective-permute-start.17 = (f32[6,64,256]{2,1,0:T(8,128)}, f32[6,64,256]{2,1,0:T(8,128)}, u32[]{:S(2)}, u32[]{:S(2)}) collective-permute-start(f32[6,64,256]{2,1,0:T(8,128)} %collective-permute-done.13.refs_0_.refs_12_), channel_id=1, source_target_pairs={{0,8},{8,0},{16,24},{24,16},{32,40},{40,32},{48,56},{56,48},{64,72... | collective-permute-start | bytes 1179656 | tf_op jit(solution)/shard_map/ppermute | solution.py:450
  57.5 5.9 %collective-permute-start.18 = (f32[6,64,256]{2,1,0:T(8,128)}, f32[6,64,256]{2,1,0:T(8,128)}, u32[]{:S(2)}, u32[]{:S(2)}) collective-permute-start(f32[6,64,256]{2,1,0:T(8,128)} %collective-permute-done.14.refs_1_.refs_14_), channel_id=1, source_target_pairs={{0,8},{8,0},{16,24},{24,16},{32,40},{40,32},{48,56},{56,48},{64,72... | collective-permute-start | bytes 1179656 | tf_op jit(solution)/shard_map/ppermute | solution.py:450
  59.0 19.5 %collective-permute-start.4 = (f32[5,2,64,256]{3,2,1,0:T(8,128)}, f32[5,2,64,256]{3,2,1,0:T(8,128)S(1)}, u32[]{:S(2)}, u32[]{:S(2)}) collective-permute-start(f32[5,2,64,256]{3,2,1,0:T(8,128)} %broadcast_select_fusion), channel_id=1, source_target_pairs={{0,4},{1,5},{2,6},{3,7},{4,0},{5,1},{6,2},{7,3},{8,12},{9,13},{10,... | collective-permute-start | bytes 1966088 | tf_op jit(solution)/shard_map/ppermute | solution.py:460
  59.8 43.9 %collective-permute-start = (f32[5,4,64,256]{3,2,1,0:T(8,128)}, f32[5,4,64,256]{3,2,1,0:T(8,128)S(1)}, u32[]{:S(2)}, u32[]{:S(2)}) collective-permute-start(f32[5,4,64,256]{3,2,1,0:T(8,128)} %get-tuple-element.27), channel_id=1, source_target_pairs={{0,1},{1,2},{2,3},{3,0},{4,5},{5,6},{6,7},{7,4},{8,9},{9,10},{10,1... | collective-permute-start | bytes 3932168 | tf_op jit(solution)/shard_map/ppermute | solution.py:456
  59.8 46.6 %collective-permute-start.1 = (f32[5,4,64,256]{3,2,1,0:T(8,128)}, f32[5,4,64,256]{3,2,1,0:T(8,128)S(1)}, u32[]{:S(2)}, u32[]{:S(2)}) collective-permute-start(f32[5,4,64,256]{3,2,1,0:T(8,128)} %get-tuple-element.28), channel_id=1, source_target_pairs={{1,0},{2,1},{3,2},{0,3},{5,4},{6,5},{7,6},{4,7},{9,8},{10,9},{11,1... | collective-permute-start | bytes 3932168 | tf_op jit(solution)/shard_map/ppermute | solution.py:457
  62.5 17.2 %collective-permute-start.19 = (f32[6,64,256]{2,1,0:T(8,128)}, f32[6,64,256]{2,1,0:T(8,128)}, u32[]{:S(2)}, u32[]{:S(2)}) collective-permute-start(f32[6,64,256]{2,1,0:T(8,128)} %copy-done.10), channel_id=1, source_target_pairs={{0,8},{8,0},{16,24},{24,16},{32,40},{40,32},{48,56},{56,48},{64,72... | collective-permute-start | bytes 1179656 | tf_op jit(solution)/shard_map/ppermute | solution.py:450
  63.5 16.3 %collective-permute-start.20 = (f32[6,64,256]{2,1,0:T(8,128)}, f32[6,64,256]{2,1,0:T(8,128)}, u32[]{:S(2)}, u32[]{:S(2)}) collective-permute-start(f32[6,64,256]{2,1,0:T(8,128)} %copy-done.11), channel_id=1, source_target_pairs={{0,8},{8,0},{16,24},{24,16},{32,40},{40,32},{48,56},{56,48},{64,72... | collective-permute-start | bytes 1179656 | tf_op jit(solution)/shard_map/ppermute | solution.py:450
  78.5 12.8 %copy-start.2 = (f32[5,2,64,256]{3,2,1,0:T(8,128)}, f32[5,2,64,256]{3,2,1,0:T(8,128)S(1)}, u32[]{:S(2)}) copy-start(f32[5,2,64,256]{3,2,1,0:T(8,128)S(1)} %collective-permute-done.4.near_ref) | copy-start | bytes 1966084
  78.5 30.4 %collective-permute-start.5 = (f32[5,2,64,256]{3,2,1,0:T(8,128)S(1)}, f32[5,2,64,256]{3,2,1,0:T(8,128)}, u32[]{:S(2)}, u32[]{:S(2)}) collective-permute-start(f32[5,2,64,256]{3,2,1,0:T(8,128)S(1)} %collective-permute-done.4.near_ref), channel_id=1, source_target_pairs={{1,0},{2,3},{5,4},{6,7},{9,8},{10,11},{13,12},{14,15},{17,16},{18,... | collective-permute-start | bytes 1966088 | tf_op jit(solution)/shard_map/ppermute | solution.py:461
  91.3 10.4 %collective-permute-start.21 = (f32[5,64,256]{2,1,0:T(8,128)}, f32[5,64,256]{2,1,0:T(8,128)S(1)}, u32[]{:S(2)}, u32[]{:S(2)}) collective-permute-start(f32[5,64,256]{2,1,0:T(8,128)} %get-tuple-element.42), channel_id=1, source_target_pairs={{0,32},{8,40},{16,48},{24,56},{32,64},{40,72},{48,80},{56,88},{64,... | collective-permute-start | bytes 983048 | tf_op jit(solution)/shard_map/ppermute | solution.py:471
  91.3 12.3 %collective-permute-start.22 = (f32[5,64,256]{2,1,0:T(8,128)}, f32[5,64,256]{2,1,0:T(8,128)S(1)}, u32[]{:S(2)}, u32[]{:S(2)}) collective-permute-start(f32[5,64,256]{2,1,0:T(8,128)} %get-tuple-element.43), channel_id=1, source_target_pairs={{0,96},{8,104},{16,112},{24,120},{32,0},{40,8},{48,16},{56,24},{64... | collective-permute-start | bytes 983048 | tf_op jit(solution)/shard_map/ppermute | solution.py:471
  101.7 7.2 %copy-start.3 = (f32[5,64,256]{2,1,0:T(8,128)}, f32[5,64,256]{2,1,0:T(8,128)S(1)}, u32[]{:S(2)}) copy-start(f32[5,64,256]{2,1,0:T(8,128)S(1)} %collective-permute-done.21.refs_1_) | copy-start | bytes 983044
  101.7 21.8 %collective-permute-start.23 = (f32[5,64,256]{2,1,0:T(8,128)}, f32[5,64,256]{2,1,0:T(8,128)}, u32[]{:S(2)}, u32[]{:S(2)}) collective-permute-start(f32[5,64,256]{2,1,0:T(8,128)} %get-tuple-element.44), channel_id=1, source_target_pairs={{0,16},{8,24},{16,0},{24,8},{32,48},{40,56},{48,32},{56,40},{64,80... | collective-permute-start | bytes 983048 | tf_op jit(solution)/shard_map/ppermute | solution.py:471
  103.7 5.2 %copy-start.4 = (f32[5,64,256]{2,1,0:T(8,128)}, f32[5,64,256]{2,1,0:T(8,128)S(1)}, u32[]{:S(2)}) copy-start(f32[5,64,256]{2,1,0:T(8,128)S(1)} %collective-permute-done.22.refs_2_) | copy-start | bytes 983044
  103.7 19.8 %collective-permute-start.24 = (f32[5,64,256]{2,1,0:T(8,128)}, f32[5,64,256]{2,1,0:T(8,128)}, u32[]{:S(2)}, u32[]{:S(2)}) collective-permute-start(f32[5,64,256]{2,1,0:T(8,128)} %get-tuple-element.45), channel_id=1, source_target_pairs={{0,64},{8,72},{16,80},{24,88},{32,96},{40,104},{48,112},{56,120},{... | collective-permute-start | bytes 983048 | tf_op jit(solution)/shard_map/ppermute | solution.py:471
  103.7 7.6 %copy-start = (f32[5,4,64,256]{3,2,1,0:T(8,128)}, f32[5,4,64,256]{3,2,1,0:T(8,128)S(1)}, u32[]{:S(2)}) copy-start(f32[5,4,64,256]{3,2,1,0:T(8,128)S(1)} %collective-permute-done.low_ref) | copy-start | bytes 3932164
  103.7 21.8 %collective-permute-start.25 = (f32[5,64,256]{2,1,0:T(8,128)}, f32[5,64,256]{2,1,0:T(8,128)}, u32[]{:S(2)}, u32[]{:S(2)}) collective-permute-start(f32[5,64,256]{2,1,0:T(8,128)} %get-tuple-element.46), channel_id=1, source_target_pairs={{0,48},{8,56},{16,32},{24,40},{32,80},{40,88},{48,64},{56,72},{64,... | collective-permute-start | bytes 983048 | tf_op jit(solution)/shard_map/ppermute | solution.py:471
  106.4 4.9 %copy-start.1 = (f32[5,4,64,256]{3,2,1,0:T(8,128)}, f32[5,4,64,256]{3,2,1,0:T(8,128)S(1)}, u32[]{:S(2)}) copy-start(f32[5,4,64,256]{3,2,1,0:T(8,128)S(1)} %collective-permute-done.1.high_ref) | copy-start | bytes 3932164
  106.4 19.7 %collective-permute-start.26 = (f32[5,64,256]{2,1,0:T(8,128)}, f32[5,64,256]{2,1,0:T(8,128)}, u32[]{:S(2)}, u32[]{:S(2)}) collective-permute-start(f32[5,64,256]{2,1,0:T(8,128)} %get-tuple-element.47), channel_id=1, source_target_pairs={{0,112},{8,120},{16,96},{24,104},{32,16},{40,24},{48,0},{56,8},{64... | collective-permute-start | bytes 983048 | tf_op jit(solution)/shard_map/ppermute | solution.py:471
  108.9 22.9 %collective-permute-start.27 = (f32[5,64,256]{2,1,0:T(8,128)}, f32[5,64,256]{2,1,0:T(8,128)S(1)}, u32[]{:S(2)}, u32[]{:S(2)}) collective-permute-start(f32[5,64,256]{2,1,0:T(8,128)} %get-tuple-element.48), channel_id=1, source_target_pairs={{0,80},{8,88},{16,64},{24,72},{32,112},{40,120},{48,96},{56,104},{... | collective-permute-start | bytes 983048 | tf_op jit(solution)/shard_map/ppermute | solution.py:471
  131.8 0.7 copy-start.5

commit v2 on v1

--- a/solution.py
+++ b/solution.py
@@ -14,6 +14,8 @@
 
 OFFSETS = ((0, 0), (1, 0), (3, 0), (0, 1), (2, 0), (1, 1), (3, 1), (2, 1))
 EARLY = 4
+FIRST = 4
+LATER = ((4, 5, 6, 7),)
 HALO = len(stencil)
 
 
@@ -303,9 +305,10 @@
 
 
 def local_kernel(
-    column_ref, coupling_ref, adjoint_ref, low_ref, high_ref, near_ref, far_ref, speed_ref,
-    xd_ref, out_ref, full_ref, gx_ref,
+    me_ref, column_ref, coupling_ref, adjoint_ref, low_ref, high_ref, near_ref, far_ref,
+    speed_ref, xd_ref, *refs,
 ):
+    parts, (out_ref, full_ref, gx_ref) = refs[:-3], refs[-3:]
     fields, depth, rows, width = adjoint_ref.shape
     half = HALO // 2
     first, last = column_ref[0] == 0, column_ref[0] == 3
@@ -344,9 +347,13 @@
         for f in range(fields):
             total = mixed(coupling_ref, 0, firsts, f) + mixed(coupling_ref, 2, grads, f)
             out_ref[f, z] = adjoint_ref[f, z] + speed * total
-
-
-def local_terms(column, coupling, adjoint, low, high, near, far, speed, x_derivative):
+    for o, part_ref in enumerate(parts):
+        plane_of = source(me_ref[0], o)
+        for f in range(fields):
+            out_ref[f, plane_of] = out_ref[f, plane_of] + part_ref[f]
+
+
+def local_terms(me, column, coupling, adjoint, low, high, near, far, speed, x_derivative, parts):
     fields, depth, rows, width = adjoint.shape
     step = 8
     whole = pl.BlockSpec((fields, depth, step, width), lambda r: (0, 0, r, 0))
@@ -356,6 +363,7 @@
         local_kernel,
         grid=(rows // step,),
         in_specs=[
+            pl.BlockSpec(memory_space=pltpu.SMEM),
             pl.BlockSpec(memory_space=pltpu.SMEM),
             pl.BlockSpec(memory_space=pltpu.SMEM),
             whole,
@@ -365,7 +373,8 @@
             part,
             pl.BlockSpec((depth, step, width), lambda r: (0, r, 0)),
             pl.BlockSpec((width, width), lambda r: (0, 0)),
-        ],
+        ]
+        + [pl.BlockSpec((fields, step, width), lambda r: (0, r, 0))] * len(parts),
         out_specs=whole,
         out_shape=jax.ShapeDtypeStruct(adjoint.shape, jnp.float32),
         scratch_shapes=[
@@ -378,7 +387,7 @@
             bytes_accessed=12 * 1024 * 1024,
             transcendentals=0,
         ),
-    )(column, coupling, adjoint, low, high, near, far, speed, x_derivative)
+    )(me, column, coupling, adjoint, low, high, near, far, speed, x_derivative, *parts)
 
 
 def join_kernel(me_ref, base_ref, *refs, where):
@@ -463,13 +472,14 @@
     early, late = own_operators(me, y_operators, chips, rows)
     sums = early_lines(me, early, same[:EARLY], other[:EARLY])
     parts = late_lines(me, coupling, late, sums, same[EARLY:], other[EARLY:], same)
-    result = local_terms(
-        column, coupling, adjoint, low, high, near, far, speed, x_derivative
-    )
     arrived = [parts[0]]
     for o in range(1, 8):
         arrived.append(lax.ppermute(parts[o], "gy", chip_perm(*OFFSETS[o])))
-    for where in ((0, 1, 2), (3, 4), (5, 6, 7)):
+    result = local_terms(
+        me, column, coupling, adjoint, low, high, near, far, speed, x_derivative,
+        arrived[:FIRST],
+    )
+    for where in LATER:
         result = join(me, result, [arrived[o] for o in where], where)
     return result
 

time: 138 us -> 136 us (0.986)
  the two profiles are of different devices: /device:TPU:1 before, /device:TPU:32 now
where the time goes in v2:
time: 136 us; the launch traced here: 135 us
  Pallas kernels  45 us (33%)
  waiting for transfers between devices  44.8 us (33%)
  starting transfers between devices  42.6 us (31%)
  local copies, waits for them, and re-layouts  1.83 us (1%)
    ppermute x7, waiting for transfers between devices, shards(): same.append(lax.ppermute(pieces[o], 'gy', chip_perm(*OFFSETS[o])))  24.6 us
    ppermute x7, waiting for transfers between devices, shards(): arrived.append(lax.ppermute(parts[o], 'gy', chip_perm(*OFFSETS[o])))  20.1 us
    ppermute x7, starting transfers between devices, shards(): arrived.append(lax.ppermute(parts[o], 'gy', chip_perm(*OFFSETS[o])))  15.8 us
    ppermute x7, starting transfers between devices, shards(): same.append(lax.ppermute(pieces[o], 'gy', chip_perm(*OFFSETS[o])))  14.6 us
    pallas_call x1, Pallas kernels, late_lines(): pl.pallas_call(late_kernel, grid_spec=pltpu.PrefetchScalarGridSpec(num_sc...  11.4 us
    pallas_call x1, Pallas kernels, local_terms(): pl.pallas_call(local_kernel, grid=(rows // step,), in_specs=[pl.BlockSpec...  10.2 us
    pallas_call x1, Pallas kernels, early_lines(): pl.pallas_call(early_kernel, grid_spec=pltpu.PrefetchScalarGridSpec(num_s...  9.34 us
    pallas_call x1, Pallas kernels, own_operators(): pl.pallas_call(operator_kernel, grid_spec=pltpu.PrefetchScalarGridSpec(nu...  5.54 us
  transfers between devices with their start and end apart: 28, of which 7 were waited for; matrix products, arithmetic and copies ran while one was open for 1% of the time, Pallas kernels for 29%

profile of v2, /device:TPU:32, one launch (start us, length us, event | category | flops | bytes accessed | tf_op | source)
XLA Modules:
  0.0 135.4 jit_solution(4144876419529283244)
XLA Ops:
  0.0 2.8 %pack.1 = (f32[6,64,256]{2,1,0:T(8,128)}, f32[6,64,256]{2,1,0:T(8,128)}, f32[6,64,256]{2,1,0:T(8,128)}, f32[6,64,256]{2,1,0:T(8,128)}, f32[6,64,256]{2,1,0:T(8,1...) custom-call(s32[1]{0:T(128)} %bitcast.me_ref, f32[5,8,64,256]{3,2,1,0:T(8,128)} %adjoint_ref.5, ...), custom_call_target="tpu_custom_call" | custom-call | bytes 6291456 | tf_op jit(solution)/shard_map/pack/pallas_call | solution.py:83
  2.8 2.0 %collective-permute-start.6 = (f32[6,64,256]{2,1,0:T(8,128)}, f32[6,64,256]{2,1,0:T(8,128)S(1)}, u32[]{:S(2)}, u32[]{:S(2)}) collective-permute-start(f32[6,64,256]{2,1,0:T(8,128)} %get-tuple-element.34), channel_id=1, source_target_pairs={{0,32},{8,40},{16,48},{24,56},{32,64},{40,72},{48,80},{56,88},{64,... | collective-permute-start | bytes 1179656 | tf_op jit(solution)/shard_map/ppermute | solution.py:456
  4.8 0.1 collective-permute-start.7
  4.9 3.2 %collective-permute-start.8 = (f32[6,64,256]{2,1,0:T(8,128)}, f32[6,64,256]{2,1,0:T(8,128)S(1)}, u32[]{:S(2)}, u32[]{:S(2)}) collective-permute-start(f32[6,64,256]{2,1,0:T(8,128)} %get-tuple-element.36), channel_id=1, source_target_pairs={{0,16},{8,24},{16,0},{24,8},{32,48},{40,56},{48,32},{56,40},{64,80... | collective-permute-start | bytes 1179656 | tf_op jit(solution)/shard_map/ppermute | solution.py:456
  8.1 0.0 collective-permute-start.9
  8.1 3.0 %collective-permute-start.13 = (f32[6,64,256]{2,1,0:T(8,128)}, f32[6,64,256]{2,1,0:T(8,128)S(1)}, u32[]{:S(2)}, u32[]{:S(2)}) collective-permute-start(f32[6,64,256]{2,1,0:T(8,128)} %get-tuple-element.37), channel_id=1, source_target_pairs={{0,64},{8,72},{16,80},{24,88},{32,96},{40,104},{48,112},{56,120},{... | collective-permute-start | bytes 1179656 | tf_op jit(solution)/shard_map/ppermute | solution.py:456
  11.1 15.1 %collective-permute-done.6.refs_1_.refs_10_ = f32[6,64,256]{2,1,0:T(8,128)S(1)} collective-permute-done((f32[6,64,256]{2,1,0:T(8,128)}, f32[6,64,256]{2,1,0:T(8,128)S(1)}, u32[]{:S(2)}, u32[]{:S(2)}) %collective-permute-start.6) | collective-permute-done | bytes 393248 | tf_op jit(solution)/shard_map/ppermute | solution.py:456
  26.2 0.0 collective-permute-start.14
  26.2 0.0 collective-permute-done.7.refs_2_.refs_9_
  26.2 4.4 %collective-permute-start.15 = (f32[6,64,256]{2,1,0:T(8,128)}, f32[6,64,256]{2,1,0:T(8,128)}, u32[]{:S(2)}, u32[]{:S(2)}) collective-permute-start(f32[6,64,256]{2,1,0:T(8,128)} %get-tuple-element.39), channel_id=1, source_target_pairs={{0,112},{8,120},{16,96},{24,104},{32,16},{40,24},{48,0},{56,8},{64... | collective-permute-start | bytes 1179656 | tf_op jit(solution)/shard_map/ppermute | solution.py:456
  30.6 3.2 %edges.1 = (f32[5,4,64,256]{3,2,1,0:T(8,128)}, f32[5,4,64,256]{3,2,1,0:T(8,128)}, f32[5,2,64,256]{3,2,1,0:T(8,128)}, f32[5,2,64,256]{3,2,1,0:T(8,128)}) custom-call(s32[1]{0:T(128)} %bitcast.1.column_ref, f32[5,8,64,256]{3,2,1,0:T(8,128)} %adjoint_ref.5), custom_call_target="tpu_custom_call" | custom-call | bytes 7340032 | tf_op jit(solution)/shard_map/edges/pallas_call | solution.py:292
  33.8 0.0 collective-permute-done.8.refs_3_.refs_11_
  33.8 4.7 %collective-permute-start.2 = (f32[5,2,64,256]{3,2,1,0:T(8,128)}, f32[5,2,64,256]{3,2,1,0:T(8,128)S(1)}, u32[]{:S(2)}, u32[]{:S(2)}) collective-permute-start(f32[5,2,64,256]{3,2,1,0:T(8,128)} %get-tuple-element.29), channel_id=1, source_target_pairs={{3,0},{0,3},{7,4},{4,7},{11,8},{8,11},{15,12},{12,15},{19,16},{16,... | collective-permute-start | bytes 1966088 | tf_op jit(solution)/shard_map/ppermute | solution.py:463
  38.5 0.0 collective-permute-done.9.refs_4_
  38.5 0.7 copy-done.12
  39.2 1.3 collective-permute-start.3
  40.6 0.0 collective-permute-done.13.refs_0_.refs_12_
  40.6 1.9 %collective-permute-start.16 = (f32[6,64,256]{2,1,0:T(8,128)}, f32[6,64,256]{2,1,0:T(8,128)S(1)}, u32[]{:S(2)}, u32[]{:S(2)}) collective-permute-start(f32[6,64,256]{2,1,0:T(8,128)} %get-tuple-element.40), channel_id=1, source_target_pairs={{0,80},{8,88},{16,64},{24,72},{32,112},{40,120},{48,96},{56,104},{... | collective-permute-start | bytes 1179656 | tf_op jit(solution)/shard_map/ppermute | solution.py:456
  42.5 0.0 collective-permute-done.14.refs_1_.refs_14_
  42.5 0.0 collective-permute-start.10
  42.5 0.0 collective-permute-done.15.refs_2_.refs_13_
  42.6 0.5 collective-permute-start.11
  43.1 9.5 %collective-permute-done.16.refs_3_.refs_15_ = f32[6,64,256]{2,1,0:T(8,128)S(1)} collective-permute-done((f32[6,64,256]{2,1,0:T(8,128)}, f32[6,64,256]{2,1,0:T(8,128)S(1)}, u32[]{:S(2)}, u32[]{:S(2)}) %collective-permute-start.16) | collective-permute-done | bytes 393248 | tf_op jit(solution)/shard_map/ppermute | solution.py:456
  52.6 0.0 collective-permute-start.12
  52.6 0.0 collective-permute-done.2
  52.6 0.5 collective-permute-start.17
  53.1 0.0 collective-permute-done.3
  53.1 0.2 copy-done.13
  53.3 0.0 collective-permute-start.18
  53.3 5.5 %operators.1 = (bf16[2,8,64,1536]{3,2,1,0:T(8,128)(2,1)}, bf16[2,8,64,1536]{3,2,1,0:T(8,128)(2,1)}) custom-call(s32[1]{0:T(128)} %bitcast.me_ref, f32[2,8,2,64,1024]{4,3,2,1,0:T(8,128)} %bitcast.6), custom_call_target="tpu_custom_call" | custom-call | flops 4194304 | bytes 10485760 | tf_op jit(solution)/shard_map/operators/pallas_call | solution.py:119
  58.9 0.0 collective-permute-done.10.refs_5_
  58.9 0.6 collective-permute-start.19
  59.5 0.0 collective-permute-done.11.refs_6_
  59.5 0.1 collective-permute-start.20
  59.6 0.9 broadcast_select_fusion
  60.5 0.0 collective-permute-done.12.refs_7_
  60.5 0.0 collective-permute-start
  60.5 0.0 collective-permute-done.17.refs_4_
  60.5 3.2 %collective-permute-start.1 = (f32[5,4,64,256]{3,2,1,0:T(8,128)}, f32[5,4,64,256]{3,2,1,0:T(8,128)S(1)}, u32[]{:S(2)}, u32[]{:S(2)}) collective-permute-start(f32[5,4,64,256]{3,2,1,0:T(8,128)} %get-tuple-element.28), channel_id=1, source_target_pairs={{1,0},{2,1},{3,2},{0,3},{5,4},{6,5},{7,6},{4,7},{9,8},{10,9},{11,1... | collective-permute-start | bytes 3932168 | tf_op jit(solution)/shard_map/ppermute | solution.py:466
  63.8 0.0 collective-permute-done.18.refs_5_
  63.8 0.0 collective-permute-start.4
  63.8 9.3 %early_lines.1.sums_ref = f32[5,1024,256]{2,1,0:T(8,128)} custom-call(s32[1]{0:T(128)} %bitcast.me_ref, bf16[1024,1536]{1,0:T(8,128)(2,1)} %bitcast.10, f32[6,64,256]{2,1,0:T(8,128)} %get-tuple-element.33.refs_0_.refs_8_, f32[6,64,256]{2,1,0:T(8,128)} %copy-done.7, f32[6,64,256]{2,1,0:T(8,128)} %copy-done.8, f32[6,64,256]{2,1,0:T(8,128)} %copy-done.9, ...), custom_call_target="tpu_custom_call" | custom-call | flops 4026531840 | bytes 12582912 | tf_op jit(solution)/shard_map/early_lines/pallas_call | solution.py:164
  73.1 0.0 collective-permute-done.19.refs_6_
  73.1 0.0 collective-permute-done.20.refs_7_
  73.1 11.4 %late_lines.1 = (f32[5,64,256]{2,1,0:T(8,128)}, f32[5,64,256]{2,1,0:T(8,128)}, f32[5,64,256]{2,1,0:T(8,128)}, f32[5,64,256]{2,1,0:T(8,128)}, f32[5,64,256]{2,1,0...) custom-call(s32[1]{0:T(128)} %bitcast.me_ref, f32[5,3,5]{2,1,0:T(4,128)} %bitcast.7, ...), custom_call_target="tpu_custom_call" | custom-call | flops 4026531840 | bytes 16777216 | tf_op jit(solution)/shard_map/late_lines/pallas_call | solution.py:221
  84.5 2.4 %collective-permute-start.21 = (f32[5,64,256]{2,1,0:T(8,128)}, f32[5,64,256]{2,1,0:T(8,128)S(1)}, u32[]{:S(2)}, u32[]{:S(2)}) collective-permute-start(f32[5,64,256]{2,1,0:T(8,128)} %get-tuple-element.42), channel_id=1, source_target_pairs={{0,32},{8,40},{16,48},{24,56},{32,64},{40,72},{48,80},{56,88},{64,... | collective-permute-start | bytes 983048 | tf_op jit(solution)/shard_map/ppermute | solution.py:477
  86.9 0.0 collective-permute-done.4.near_ref
  87.0 1.3 collective-permute-start.5
  88.2 0.8 collective-permute-start.22
  89.0 6.3 %collective-permute-done.21.refs_1_ = f32[5,64,256]{2,1,0:T(8,128)S(1)} collective-permute-done((f32[5,64,256]{2,1,0:T(8,128)}, f32[5,64,256]{2,1,0:T(8,128)S(1)}, u32[]{:S(2)}, u32[]{:S(2)}) %collective-permute-start.21) | collective-permute-done | bytes 327712 | tf_op jit(solution)/shard_map/ppermute | solution.py:477
  95.3 1.7 %collective-permute-start.23 = (f32[5,64,256]{2,1,0:T(8,128)}, f32[5,64,256]{2,1,0:T(8,128)S(1)}, u32[]{:S(2)}, u32[]{:S(2)}) collective-permute-start(f32[5,64,256]{2,1,0:T(8,128)} %get-tuple-element.44), channel_id=1, source_target_pairs={{0,16},{8,24},{16,0},{24,8},{32,48},{40,56},{48,32},{56,40},{64,80... | collective-permute-start | bytes 983048 | tf_op jit(solution)/shard_map/ppermute | solution.py:477
  97.0 0.8 collective-permute-done.22.refs_2_
  97.8 3.7 %collective-permute-start.24 = (f32[5,64,256]{2,1,0:T(8,128)}, f32[5,64,256]{2,1,0:T(8,128)}, u32[]{:S(2)}, u32[]{:S(2)}) collective-permute-start(f32[5,64,256]{2,1,0:T(8,128)} %get-tuple-element.45), channel_id=1, source_target_pairs={{0,64},{8,72},{16,80},{24,88},{32,96},{40,104},{48,112},{56,120},{... | collective-permute-start | bytes 983048 | tf_op jit(solution)/shard_map/ppermute | solution.py:477
  101.4 4.3 %collective-permute-done.23.refs_3_ = f32[5,64,256]{2,1,0:T(8,128)S(1)} collective-permute-done((f32[5,64,256]{2,1,0:T(8,128)}, f32[5,64,256]{2,1,0:T(8,128)S(1)}, u32[]{:S(2)}, u32[]{:S(2)}) %collective-permute-start.23) | collective-permute-done | bytes 327712 | tf_op jit(solution)/shard_map/ppermute | solution.py:477
  105.7 1.1 collective-permute-start.25
  106.8 0.0 collective-permute-done.low_ref
  106.8 3.4 %collective-permute-start.26 = (f32[5,64,256]{2,1,0:T(8,128)}, f32[5,64,256]{2,1,0:T(8,128)}, u32[]{:S(2)}, u32[]{:S(2)}) collective-permute-start(f32[5,64,256]{2,1,0:T(8,128)} %get-tuple-element.47), channel_id=1, source_target_pairs={{0,112},{8,120},{16,96},{24,104},{32,16},{40,24},{48,0},{56,8},{64... | collective-permute-start | bytes 983048 | tf_op jit(solution)/shard_map/ppermute | solution.py:477
  110.2 2.8 %collective-permute-start.27 = (f32[5,64,256]{2,1,0:T(8,128)}, f32[5,64,256]{2,1,0:T(8,128)}, u32[]{:S(2)}, u32[]{:S(2)}) collective-permute-start(f32[5,64,256]{2,1,0:T(8,128)} %get-tuple-element.48), channel_id=1, source_target_pairs={{0,80},{8,88},{16,64},{24,72},{32,112},{40,120},{48,96},{56,104},{... | collective-permute-start | bytes 983048 | tf_op jit(solution)/shard_map/ppermute | solution.py:477
  113.0 0.8 copy-done.3
  113.8 10.2 %local.1.base_ref = f32[5,8,64,256]{3,2,1,0:T(8,128)} custom-call(s32[1]{0:T(128)} %bitcast.me_ref, s32[1]{0:T(128)} %bitcast.1.column_ref, f32[5,3,5]{2,1,0:T(4,128)} %bitcast.8, f32[5,8,64,256]{3,2,1,0:T(8,128)} %adjoint_ref.5, f32[5,4,64,256]{3,2,1,0:T(8,128)} %copy-done, f32[5,4,64,256]{3,2,1,0:T(8,128)} %copy-done.1, f32[5,2,64,256]{3,2,1,0:T(8,128)} %copy-done.2, ...), custom_call_target="tpu_custom_call" | custom-call | flops 1006632960 | bytes 12582912 | tf_op jit(solution)/shard_map/local/pallas_call | solution.py:362
  124.0 0.0 collective-permute-done.24.refs_0_
  124.1 1.9 %collective-permute-done.26.refs_2_ = f32[5,64,256]{2,1,0:T(8,128)} collective-permute-done((f32[5,64,256]{2,1,0:T(8,128)}, f32[5,64,256]{2,1,0:T(8,128)}, u32[]{:S(2)}, u32[]{:S(2)}) %collective-permute-start.26) | collective-permute-done | bytes 327712 | tf_op jit(solution)/shard_map/ppermute | solution.py:477
  125.9 6.9 %collective-permute-done.27.refs_3_ = f32[5,64,256]{2,1,0:T(8,128)} collective-permute-done((f32[5,64,256]{2,1,0:T(8,128)}, f32[5,64,256]{2,1,0:T(8,128)}, u32[]{:S(2)}, u32[]{:S(2)}) %collective-permute-start.27) | collective-permute-done | bytes 327712 | tf_op jit(solution)/shard_map/ppermute | solution.py:477
  132.8 2.5 %join.1 = f32[5,8,64,256]{3,2,1,0:T(8,128)} custom-call(s32[1]{0:T(128)} %bitcast.me_ref, f32[5,8,64,256]{3,2,1,0:T(8,128)} %local.1.base_ref, f32[5,64,256]{2,1,0:T(8,128)} %collective-permute-done.24.refs_0_, f32[5,64,256]{2,1,0:T(8,128)} %collective-permute-done.25.refs_1_, ...), custom_call_target="tpu_custom_call", output_to_operand_aliasing={{}: (1, {})} | custom-call | flops 327680 | bytes 4194304 | tf_op jit(solution)/shard_map/join/pallas_call | solution.py:425
  (28 shorter events, 0.1 us)
Async XLA Ops:
  2.8 23.3 %collective-permute-start.6 = (f32[6,64,256]{2,1,0:T(8,128)}, f32[6,64,256]{2,1,0:T(8,128)S(1)}, u32[]{:S(2)}, u32[]{:S(2)}) collective-permute-start(f32[6,64,256]{2,1,0:T(8,128)} %get-tuple-element.34), channel_id=1, source_target_pairs={{0,32},{8,40},{16,48},{24,56},{32,64},{40,72},{48,80},{56,88},{64,... | collective-permute-start | bytes 1179656 | tf_op jit(solution)/shard_map/ppermute | solution.py:456
  4.8 21.4 %collective-permute-start.7 = (f32[6,64,256]{2,1,0:T(8,128)}, f32[6,64,256]{2,1,0:T(8,128)S(1)}, u32[]{:S(2)}, u32[]{:S(2)}) collective-permute-start(f32[6,64,256]{2,1,0:T(8,128)} %get-tuple-element.35), channel_id=1, source_target_pairs={{0,96},{8,104},{16,112},{24,120},{32,0},{40,8},{48,16},{56,24},{64... | collective-permute-start | bytes 1179656 | tf_op jit(solution)/shard_map/ppermute | solution.py:456
  4.9 28.9 %collective-permute-start.8 = (f32[6,64,256]{2,1,0:T(8,128)}, f32[6,64,256]{2,1,0:T(8,128)S(1)}, u32[]{:S(2)}, u32[]{:S(2)}) collective-permute-start(f32[6,64,256]{2,1,0:T(8,128)} %get-tuple-element.36), channel_id=1, source_target_pairs={{0,16},{8,24},{16,0},{24,8},{32,48},{40,56},{48,32},{56,40},{64,80... | collective-permute-start | bytes 1179656 | tf_op jit(solution)/shard_map/ppermute | solution.py:456
  8.1 30.4 %collective-permute-start.9 = (f32[6,64,256]{2,1,0:T(8,128)}, f32[6,64,256]{2,1,0:T(8,128)S(1)}, u32[]{:S(2)}, u32[]{:S(2)}) collective-permute-start(f32[6,64,256]{2,1,0:T(8,128)} %get-tuple-element.33.refs_0_.refs_8_), channel_id=1, source_target_pairs={{0,8},{8,0},{16,24},{24,16},{32,40},{40,32},{48,56},{56,48},{64,72... | collective-permute-start | bytes 1179656 | tf_op jit(solution)/shard_map/ppermute | solution.py:459
  8.1 32.4 %collective-permute-start.13 = (f32[6,64,256]{2,1,0:T(8,128)}, f32[6,64,256]{2,1,0:T(8,128)S(1)}, u32[]{:S(2)}, u32[]{:S(2)}) collective-permute-start(f32[6,64,256]{2,1,0:T(8,128)} %get-tuple-element.37), channel_id=1, source_target_pairs={{0,64},{8,72},{16,80},{24,88},{32,96},{40,104},{48,112},{56,120},{... | collective-permute-start | bytes 1179656 | tf_op jit(solution)/shard_map/ppermute | solution.py:456
  26.2 32.7 %copy-start.7 = (f32[6,64,256]{2,1,0:T(8,128)}, f32[6,64,256]{2,1,0:T(8,128)S(1)}, u32[]{:S(2)}) copy-start(f32[6,64,256]{2,1,0:T(8,128)S(1)} %collective-permute-done.6.refs_1_.refs_10_) | copy-start | bytes 1179652
  26.2 16.3 %collective-permute-start.14 = (f32[6,64,256]{2,1,0:T(8,128)}, f32[6,64,256]{2,1,0:T(8,128)S(1)}, u32[]{:S(2)}, u32[]{:S(2)}) collective-permute-start(f32[6,64,256]{2,1,0:T(8,128)} %get-tuple-element.38), channel_id=1, source_target_pairs={{0,48},{8,56},{16,32},{24,40},{32,80},{40,88},{48,64},{56,72},{64,... | collective-permute-start | bytes 1179656 | tf_op jit(solution)/shard_map/ppermute | solution.py:456
  26.2 32.7 %copy-start.8 = (f32[6,64,256]{2,1,0:T(8,128)}, f32[6,64,256]{2,1,0:T(8,128)S(1)}, u32[]{:S(2)}) copy-start(f32[6,64,256]{2,1,0:T(8,128)S(1)} %collective-permute-done.7.refs_2_.refs_9_) | copy-start | bytes 1179652
  26.2 16.3 %collective-permute-start.15 = (f32[6,64,256]{2,1,0:T(8,128)}, f32[6,64,256]{2,1,0:T(8,128)}, u32[]{:S(2)}, u32[]{:S(2)}) collective-permute-start(f32[6,64,256]{2,1,0:T(8,128)} %get-tuple-element.39), channel_id=1, source_target_pairs={{0,112},{8,120},{16,96},{24,104},{32,16},{40,24},{48,0},{56,8},{64... | collective-permute-start | bytes 1179656 | tf_op jit(solution)/shard_map/ppermute | solution.py:456
  33.8 25.1 %copy-start.9 = (f32[6,64,256]{2,1,0:T(8,128)}, f32[6,64,256]{2,1,0:T(8,128)S(1)}, u32[]{:S(2)}) copy-start(f32[6,64,256]{2,1,0:T(8,128)S(1)} %collective-permute-done.8.refs_3_.refs_11_) | copy-start | bytes 1179652
  33.8 18.8 %collective-permute-start.2 = (f32[5,2,64,256]{3,2,1,0:T(8,128)}, f32[5,2,64,256]{3,2,1,0:T(8,128)S(1)}, u32[]{:S(2)}, u32[]{:S(2)}) collective-permute-start(f32[5,2,64,256]{3,2,1,0:T(8,128)} %get-tuple-element.29), channel_id=1, source_target_pairs={{3,0},{0,3},{7,4},{4,7},{11,8},{8,11},{15,12},{12,15},{19,16},{16,... | collective-permute-start | bytes 1966088 | tf_op jit(solution)/shard_map/ppermute | solution.py:463
  38.5 0.7 copy-start.12
  39.2 13.8 %collective-permute-start.3 = (f32[5,2,64,256]{3,2,1,0:T(8,128)}, f32[5,2,64,256]{3,2,1,0:T(8,128)S(1)}, u32[]{:S(2)}, u32[]{:S(2)}) collective-permute-start(f32[5,2,64,256]{3,2,1,0:T(8,128)} %get-tuple-element.30), channel_id=1, source_target_pairs={{3,1},{0,2},{7,5},{4,6},{11,9},{8,10},{15,13},{12,14},{19,17},{16,... | collective-permute-start | bytes 1966088 | tf_op jit(solution)/shard_map/ppermute | solution.py:464
  40.6 18.3 %copy-start.10 = (f32[6,64,256]{2,1,0:T(8,128)}, f32[6,64,256]{2,1,0:T(8,128)S(1)}, u32[]{:S(2)}) copy-start(f32[6,64,256]{2,1,0:T(8,128)S(1)} %collective-permute-done.13.refs_0_.refs_12_) | copy-start | bytes 1179652
  40.6 12.0 %collective-permute-start.16 = (f32[6,64,256]{2,1,0:T(8,128)}, f32[6,64,256]{2,1,0:T(8,128)S(1)}, u32[]{:S(2)}, u32[]{:S(2)}) collective-permute-start(f32[6,64,256]{2,1,0:T(8,128)} %get-tuple-element.40), channel_id=1, source_target_pairs={{0,80},{8,88},{16,64},{24,72},{32,112},{40,120},{48,96},{56,104},{... | collective-permute-start | bytes 1179656 | tf_op jit(solution)/shard_map/ppermute | solution.py:456
  42.5 16.3 %copy-start.11 = (f32[6,64,256]{2,1,0:T(8,128)}, f32[6,64,256]{2,1,0:T(8,128)S(1)}, u32[]{:S(2)}) copy-start(f32[6,64,256]{2,1,0:T(8,128)S(1)} %collective-permute-done.14.refs_1_.refs_14_) | copy-start | bytes 1179652
  42.5 16.4 %collective-permute-start.10 = (f32[6,64,256]{2,1,0:T(8,128)S(1)}, f32[6,64,256]{2,1,0:T(8,128)}, u32[]{:S(2)}, u32[]{:S(2)}) collective-permute-start(f32[6,64,256]{2,1,0:T(8,128)S(1)} %collective-permute-done.6.refs_1_.refs_10_), channel_id=1, source_target_pairs={{0,8},{8,0},{16,24},{24,16},{32,40},{40,32},{48,56},{56,48},{64,72... | collective-permute-start | bytes 1179656 | tf_op jit(solution)/shard_map/ppermute | solution.py:459
  42.6 16.9 %collective-permute-start.11 = (f32[6,64,256]{2,1,0:T(8,128)S(1)}, f32[6,64,256]{2,1,0:T(8,128)}, u32[]{:S(2)}, u32[]{:S(2)}) collective-permute-start(f32[6,64,256]{2,1,0:T(8,128)S(1)} %collective-permute-done.7.refs_2_.refs_9_), channel_id=1, source_target_pairs={{0,8},{8,0},{16,24},{24,16},{32,40},{40,32},{48,56},{56,48},{64,72... | collective-permute-start | bytes 1179656 | tf_op jit(solution)/shard_map/ppermute | solution.py:459
  52.6 0.7 copy-start.13
  52.6 8.0 %collective-permute-start.12 = (f32[6,64,256]{2,1,0:T(8,128)S(1)}, f32[6,64,256]{2,1,0:T(8,128)}, u32[]{:S(2)}, u32[]{:S(2)}) collective-permute-start(f32[6,64,256]{2,1,0:T(8,128)S(1)} %collective-permute-done.8.refs_3_.refs_11_), channel_id=1, source_target_pairs={{0,8},{8,0},{16,24},{24,16},{32,40},{40,32},{48,56},{56,48},{64,72... | collective-permute-start | bytes 1179656 | tf_op jit(solution)/shard_map/ppermute | solution.py:459
  52.6 8.0 %collective-permute-start.17 = (f32[6,64,256]{2,1,0:T(8,128)S(1)}, f32[6,64,256]{2,1,0:T(8,128)}, u32[]{:S(2)}, u32[]{:S(2)}) collective-permute-start(f32[6,64,256]{2,1,0:T(8,128)S(1)} %collective-permute-done.13.refs_0_.refs_12_), channel_id=1, source_target_pairs={{0,8},{8,0},{16,24},{24,16},{32,40},{40,32},{48,56},{56,48},{64,72... | collective-permute-start | bytes 1179656 | tf_op jit(solution)/shard_map/ppermute | solution.py:459
  53.3 10.5 %collective-permute-start.18 = (f32[6,64,256]{2,1,0:T(8,128)S(1)}, f32[6,64,256]{2,1,0:T(8,128)}, u32[]{:S(2)}, u32[]{:S(2)}) collective-permute-start(f32[6,64,256]{2,1,0:T(8,128)S(1)} %collective-permute-done.14.refs_1_.refs_14_), channel_id=1, source_target_pairs={{0,8},{8,0},{16,24},{24,16},{32,40},{40,32},{48,56},{56,48},{64,72... | collective-permute-start | bytes 1179656 | tf_op jit(solution)/shard_map/ppermute | solution.py:459
  58.9 14.2 %collective-permute-start.19 = (f32[6,64,256]{2,1,0:T(8,128)}, f32[6,64,256]{2,1,0:T(8,128)}, u32[]{:S(2)}, u32[]{:S(2)}) collective-permute-start(f32[6,64,256]{2,1,0:T(8,128)} %collective-permute-done.15.refs_2_.refs_13_), channel_id=1, source_target_pairs={{0,8},{8,0},{16,24},{24,16},{32,40},{40,32},{48,56},{56,48},{64,72... | collective-permute-start | bytes 1179656 | tf_op jit(solution)/shard_map/ppermute | solution.py:459
  59.5 13.6 %collective-permute-start.20 = (f32[6,64,256]{2,1,0:T(8,128)}, f32[6,64,256]{2,1,0:T(8,128)}, u32[]{:S(2)}, u32[]{:S(2)}) collective-permute-start(f32[6,64,256]{2,1,0:T(8,128)} %copy-done.13), channel_id=1, source_target_pairs={{0,8},{8,0},{16,24},{24,16},{32,40},{40,32},{48,56},{56,48},{64,72... | collective-permute-start | bytes 1179656 | tf_op jit(solution)/shard_map/ppermute | solution.py:459
  60.5 46.3 %collective-permute-start = (f32[5,4,64,256]{3,2,1,0:T(8,128)}, f32[5,4,64,256]{3,2,1,0:T(8,128)S(1)}, u32[]{:S(2)}, u32[]{:S(2)}) collective-permute-start(f32[5,4,64,256]{3,2,1,0:T(8,128)} %get-tuple-element.27), channel_id=1, source_target_pairs={{0,1},{1,2},{2,3},{3,0},{4,5},{5,6},{6,7},{7,4},{8,9},{9,10},{10,1... | collective-permute-start | bytes 3932168 | tf_op jit(solution)/shard_map/ppermute | solution.py:465
  60.5 49.6 %collective-permute-start.1 = (f32[5,4,64,256]{3,2,1,0:T(8,128)}, f32[5,4,64,256]{3,2,1,0:T(8,128)S(1)}, u32[]{:S(2)}, u32[]{:S(2)}) collective-permute-start(f32[5,4,64,256]{3,2,1,0:T(8,128)} %get-tuple-element.28), channel_id=1, source_target_pairs={{1,0},{2,1},{3,2},{0,3},{5,4},{6,5},{7,6},{4,7},{9,8},{10,9},{11,1... | collective-permute-start | bytes 3932168 | tf_op jit(solution)/shard_map/ppermute | solution.py:466
  63.8 23.2 %collective-permute-start.4 = (f32[5,2,64,256]{3,2,1,0:T(8,128)}, f32[5,2,64,256]{3,2,1,0:T(8,128)S(1)}, u32[]{:S(2)}, u32[]{:S(2)}) collective-permute-start(f32[5,2,64,256]{3,2,1,0:T(8,128)} %broadcast_select_fusion), channel_id=1, source_target_pairs={{0,4},{1,5},{2,6},{3,7},{4,0},{5,1},{6,2},{7,3},{8,12},{9,13},{10,... | collective-permute-start | bytes 1966088 | tf_op jit(solution)/shard_map/ppermute | solution.py:469
  84.5 10.8 %collective-permute-start.21 = (f32[5,64,256]{2,1,0:T(8,128)}, f32[5,64,256]{2,1,0:T(8,128)S(1)}, u32[]{:S(2)}, u32[]{:S(2)}) collective-permute-start(f32[5,64,256]{2,1,0:T(8,128)} %get-tuple-element.42), channel_id=1, source_target_pairs={{0,32},{8,40},{16,48},{24,56},{32,64},{40,72},{48,80},{56,88},{64,... | collective-permute-start | bytes 983048 | tf_op jit(solution)/shard_map/ppermute | solution.py:477
  87.0 26.9 %copy-start.2 = (f32[5,2,64,256]{3,2,1,0:T(8,128)}, f32[5,2,64,256]{3,2,1,0:T(8,128)S(1)}, u32[]{:S(2)}) copy-start(f32[5,2,64,256]{3,2,1,0:T(8,128)S(1)} %collective-permute-done.4.near_ref) | copy-start | bytes 1966084
  87.0 26.0 %collective-permute-start.5 = (f32[5,2,64,256]{3,2,1,0:T(8,128)S(1)}, f32[5,2,64,256]{3,2,1,0:T(8,128)S(1)}, u32[]{:S(2)}, u32[]{:S(2)}) collective-permute-start(f32[5,2,64,256]{3,2,1,0:T(8,128)S(1)} %collective-permute-done.4.near_ref), channel_id=1, source_target_pairs={{1,0},{2,3},{5,4},{6,7},{9,8},{10,11},{13,12},{14,15},{17,16},{18,... | collective-permute-start | bytes 1966088 | tf_op jit(solution)/shard_map/ppermute | solution.py:470
  88.2 9.5 %collective-permute-start.22 = (f32[5,64,256]{2,1,0:T(8,128)}, f32[5,64,256]{2,1,0:T(8,128)S(1)}, u32[]{:S(2)}, u32[]{:S(2)}) collective-permute-start(f32[5,64,256]{2,1,0:T(8,128)} %get-tuple-element.43), channel_id=1, source_target_pairs={{0,96},{8,104},{16,112},{24,120},{32,0},{40,8},{48,16},{56,24},{64... | collective-permute-start | bytes 983048 | tf_op jit(solution)/shard_map/ppermute | solution.py:477
  95.3 17.7 %copy-start.4 = (f32[5,64,256]{2,1,0:T(8,128)}, f32[5,64,256]{2,1,0:T(8,128)S(1)}, u32[]{:S(2)}) copy-start(f32[5,64,256]{2,1,0:T(8,128)S(1)} %collective-permute-done.21.refs_1_) | copy-start | bytes 983044
  95.3 10.4 %collective-permute-start.23 = (f32[5,64,256]{2,1,0:T(8,128)}, f32[5,64,256]{2,1,0:T(8,128)S(1)}, u32[]{:S(2)}, u32[]{:S(2)}) collective-permute-start(f32[5,64,256]{2,1,0:T(8,128)} %get-tuple-element.44), channel_id=1, source_target_pairs={{0,16},{8,24},{16,0},{24,8},{32,48},{40,56},{48,32},{56,40},{64,80... | collective-permute-start | bytes 983048 | tf_op jit(solution)/shard_map/ppermute | solution.py:477
  97.8 15.2 %copy-start.5 = (f32[5,64,256]{2,1,0:T(8,128)}, f32[5,64,256]{2,1,0:T(8,128)S(1)}, u32[]{:S(2)}) copy-start(f32[5,64,256]{2,1,0:T(8,128)S(1)} %collective-permute-done.22.refs_2_) | copy-start | bytes 983044
  97.8 26.3 %collective-permute-start.24 = (f32[5,64,256]{2,1,0:T(8,128)}, f32[5,64,256]{2,1,0:T(8,128)}, u32[]{:S(2)}, u32[]{:S(2)}) collective-permute-start(f32[5,64,256]{2,1,0:T(8,128)} %get-tuple-element.45), channel_id=1, source_target_pairs={{0,64},{8,72},{16,80},{24,88},{32,96},{40,104},{48,112},{56,120},{... | collective-permute-start | bytes 983048 | tf_op jit(solution)/shard_map/ppermute | solution.py:477
  105.7 7.3 %copy-start.6 = (f32[5,64,256]{2,1,0:T(8,128)}, f32[5,64,256]{2,1,0:T(8,128)S(1)}, u32[]{:S(2)}) copy-start(f32[5,64,256]{2,1,0:T(8,128)S(1)} %collective-permute-done.23.refs_3_) | copy-start | bytes 983044
  105.7 18.3 %collective-permute-start.25 = (f32[5,64,256]{2,1,0:T(8,128)}, f32[5,64,256]{2,1,0:T(8,128)}, u32[]{:S(2)}, u32[]{:S(2)}) collective-permute-start(f32[5,64,256]{2,1,0:T(8,128)} %get-tuple-element.46), channel_id=1, source_target_pairs={{0,48},{8,56},{16,32},{24,40},{32,80},{40,88},{48,64},{56,72},{64,... | collective-permute-start | bytes 983048 | tf_op jit(solution)/shard_map/ppermute | solution.py:477
  106.8 7.0 %copy-start = (f32[5,4,64,256]{3,2,1,0:T(8,128)}, f32[5,4,64,256]{3,2,1,0:T(8,128)S(1)}, u32[]{:S(2)}) copy-start(f32[5,4,64,256]{3,2,1,0:T(8,128)S(1)} %collective-permute-done.low_ref) | copy-start | bytes 3932164
  106.8 19.1 %collective-permute-start.26 = (f32[5,64,256]{2,1,0:T(8,128)}, f32[5,64,256]{2,1,0:T(8,128)}, u32[]{:S(2)}, u32[]{:S(2)}) collective-permute-start(f32[5,64,256]{2,1,0:T(8,128)} %get-tuple-element.47), channel_id=1, source_target_pairs={{0,112},{8,120},{16,96},{24,104},{32,16},{40,24},{48,0},{56,8},{64... | collective-permute-start | bytes 983048 | tf_op jit(solution)/shard_map/ppermute | solution.py:477
  110.2 3.7 %copy-start.1 = (f32[5,4,64,256]{3,2,1,0:T(8,128)}, f32[5,4,64,256]{3,2,1,0:T(8,128)S(1)}, u32[]{:S(2)}) copy-start(f32[5,4,64,256]{3,2,1,0:T(8,128)S(1)} %collective-permute-done.1.high_ref) | copy-start | bytes 3932164
  110.2 22.7 %collective-permute-start.27 = (f32[5,64,256]{2,1,0:T(8,128)}, f32[5,64,256]{2,1,0:T(8,128)}, u32[]{:S(2)}, u32[]{:S(2)}) collective-permute-start(f32[5,64,256]{2,1,0:T(8,128)} %get-tuple-element.48), channel_id=1, source_target_pairs={{0,80},{8,88},{16,64},{24,72},{32,112},{40,120},{48,96},{56,104},{... | collective-permute-start | bytes 983048 | tf_op jit(solution)/shard_map/ppermute | solution.py:477
  113.0 0.8 copy-start.3

commit v3 on v2

--- a/solution.py
+++ b/solution.py
@@ -15,7 +15,7 @@
 OFFSETS = ((0, 0), (1, 0), (3, 0), (0, 1), (2, 0), (1, 1), (3, 1), (2, 1))
 EARLY = 4
 FIRST = 4
-LATER = ((4, 5, 6, 7),)
+LATER = ((4, 5, 6), (7,))
 HALO = len(stencil)
 
 
@@ -49,14 +49,14 @@
     return high, low
 
 
-def pack_kernel(me_ref, adjoint_ref, speed_ref, *refs):
-    count = len(OFFSETS)
+def pack_kernel(me_ref, adjoint_ref, speed_ref, *refs, which):
+    count = len(which)
     outs = refs[:count]
     hold, arrive, leave = refs[count:]
     fields = adjoint_ref.shape[0]
 
     def loads(o):
-        plane = target(me_ref[0], o)
+        plane = target(me_ref[0], which[o])
         return (
             pltpu.make_async_copy(
                 adjoint_ref.at[:, plane], hold.at[o, pl.ds(0, fields)], arrive.at[o, 0]
@@ -64,24 +64,23 @@
             pltpu.make_async_copy(speed_ref.at[plane], hold.at[o, fields], arrive.at[o, 1]),
         )
 
-    order = list(range(1, count)) + [0]
-    for o in order:
+    for o in range(count):
         for copy in loads(o):
             copy.start()
-    for o in order:
+    for o in range(count):
         for copy in loads(o):
             copy.wait()
         pltpu.make_async_copy(hold.at[o], outs[o], leave.at[o]).start()
-    for o in order:
+    for o in range(count):
         pltpu.make_async_copy(hold.at[o], outs[o], leave.at[o]).wait()
 
 
-def pack(me, adjoint, speed):
+def pack(me, adjoint, speed, which):
     fields, _, rows, width = adjoint.shape
-    count = len(OFFSETS)
+    count = len(which)
     anywhere = pl.BlockSpec(memory_space=pl.ANY)
     return pl.pallas_call(
-        pack_kernel,
+        functools.partial(pack_kernel, which=which),
         in_specs=[pl.BlockSpec(memory_space=pltpu.SMEM), anywhere, anywhere],
         out_specs=[anywhere] * count,
         out_shape=[jax.ShapeDtypeStruct((fields + 1, rows, width), jnp.float32)] * count,
@@ -95,7 +94,51 @@
     )(me, adjoint, speed)
 
 
-def operator_kernel(me_ref, op_ref, early_ref, late_ref):
+def operator_kernel(
+    me_ref, column_ref, op_ref, adjoint_ref, early_ref, late_ref, near_ref, far_ref, top_ref,
+    bottom_ref, hold, arrive, leave,
+):
+    fields, depth = adjoint_ref.shape[:2]
+    half = HALO // 2
+    edge = jnp.where(column_ref[0] == 3, depth - HALO, 0)
+    step = pl.program_id(0) * pl.num_programs(1) + pl.program_id(1)
+    steps = pl.num_programs(0) * pl.num_programs(1)
+
+    def load(f):
+        return pltpu.make_async_copy(adjoint_ref.at[f], hold.at[f], arrive.at[f])
+
+    def stores(f):
+        return [
+            pltpu.make_async_copy(hold.at[f, pl.ds(start, size)], out.at[f], leave.at[f, k])
+            for k, (out, start, size) in enumerate(
+                (
+                    (near_ref, edge, half),
+                    (far_ref, edge + half, half),
+                    (top_ref, depth - HALO, HALO),
+                    (bottom_ref, 0, HALO),
+                )
+            )
+        ]
+
+    @pl.when(step == 0)
+    def _():
+        for f in range(fields):
+            load(f).start()
+
+    @pl.when(step == 1)
+    def _():
+        for f in range(fields):
+            load(f).wait()
+        for f in range(fields):
+            for copy in stores(f):
+                copy.start()
+
+    @pl.when(step == steps - 1)
+    def _():
+        for f in range(fields):
+            for copy in stores(f):
+                copy.wait()
+
     chips = op_ref.shape[1]
     pair = op_ref.shape[4] // 8
     size = EARLY * pair
@@ -110,31 +153,43 @@
             out_ref[0, t, :, 2 * size + at : 2 * size + at + pair] = low
 
 
-def own_operators(me, y_operators, chips, rows):
+def prepare(me, column, y_operators, adjoint):
     ops, size, _ = y_operators.shape
+    fields, chips, rows, width = adjoint.shape
+    counts = (HALO // 2, HALO // 2, HALO, HALO)
+    anywhere = pl.BlockSpec(memory_space=pl.ANY)
     shaped = y_operators.reshape(ops, chips, 2, rows, size)
     wide = 3 * size // 2
     step = 4
     out_spec = pl.BlockSpec((1, step, rows, wide), lambda o, t, me: (o, t, 0, 0))
-    early, late = pl.pallas_call(
+    early, late, *sides = pl.pallas_call(
         operator_kernel,
         grid_spec=pltpu.PrefetchScalarGridSpec(
             num_scalar_prefetch=1,
             grid=(ops, chips // step),
             in_specs=[
+                pl.BlockSpec(memory_space=pltpu.SMEM),
                 pl.BlockSpec(
                     (1, step, 1, rows, size), lambda o, t, me: (o, t, me[0] & 1, 0, 0)
-                )
+                ),
+                anywhere,
             ],
-            out_specs=[out_spec] * 2,
-        ),
-        out_shape=[jax.ShapeDtypeStruct((ops, chips, rows, wide), jnp.bfloat16)] * 2,
+            out_specs=[out_spec] * 2 + [anywhere] * len(counts),
+            scratch_shapes=[
+                pltpu.VMEM(adjoint.shape, jnp.float32),
+                pltpu.SemaphoreType.DMA((fields,)),
+                pltpu.SemaphoreType.DMA((fields, len(counts))),
+            ],
+        ),
+        out_shape=[jax.ShapeDtypeStruct((ops, chips, rows, wide), jnp.bfloat16)] * 2
+        + [jax.ShapeDtypeStruct((fields, count, rows, width), jnp.float32) for count in counts],
         name="operators",
         cost_estimate=pl.CostEstimate(
             flops=4 * 1024 * 1024, bytes_accessed=10 * 1024 * 1024, transcendentals=0
         ),
-    )(me, shaped)
-    return early.reshape(ops * chips * rows, wide), late.reshape(ops * chips * rows, wide)
+    )(me, column, shaped, adjoint)
+    flat = (ops * chips * rows, wide)
+    return early.reshape(flat), late.reshape(flat), sides
 
 
 def load_parts(core, same, other, parts):
@@ -186,7 +241,7 @@
     same, other = refs[:EARLY], refs[EARLY : 2 * EARLY]
     speeds = refs[2 * EARLY : 2 * EARLY + count]
     outs = refs[2 * EARLY + count : 2 * EARLY + 2 * count]
-    parts, grads = refs[2 * EARLY + 2 * count :]
+    parts, grads, ready, leave = refs[2 * EARLY + 2 * count :]
     field = pl.program_id(0)
     fields = pl.num_programs(0)
     rows = same[0].shape[1]
@@ -198,17 +253,21 @@
     @pl.when(field == fields - 1)
     def _():
         half = grads.shape[1] // 2
-        for o in range(count):
+        order = list(range(1, count)) + [0]
+        for o in order:
             start = pl.multiple_of(target(me_ref[0], o) * rows, rows)
             for part in range(0, rows, 16):
                 firsts = [grads[g, pl.ds(start + part, 16), :] for g in range(5)]
                 speed = speeds[o][0, pl.ds(part, 16), :] * stepping
                 for f in range(5):
                     second = grads[f, pl.ds(start + half + part, 16), :]
-                    outs[o][f, pl.ds(part, 16), :] = (
+                    ready[o, f, pl.ds(part, 16), :] = (
                         speed * mixed(coupling_ref, 1, firsts, f)
                         + (viscous * stepping) * second
                     )
+            pltpu.make_async_copy(ready.at[o], outs[o], leave.at[o]).start()
+        for o in order:
+            pltpu.make_async_copy(ready.at[o], outs[o], leave.at[o]).wait()
 
 
 def late_lines(me, coupling, operators, sums, same, other, everyone):
@@ -230,10 +289,12 @@
             ]
             + [piece] * (2 * EARLY)
             + [last] * count,
-            out_specs=[pl.BlockSpec((fields, rows, width), lambda f, me: (0, 0, 0))] * count,
+            out_specs=[pl.BlockSpec(memory_space=pl.ANY)] * count,
             scratch_shapes=[
                 pltpu.VMEM((size, width), jnp.bfloat16),
                 pltpu.VMEM((fields, height, width), jnp.float32),
+                pltpu.VMEM((count, fields, rows, width), jnp.float32),
+                pltpu.SemaphoreType.DMA((count,)),
             ],
         ),
         out_shape=[jax.ShapeDtypeStruct((fields, rows, width), jnp.float32)] * count,
@@ -251,57 +312,6 @@
     for g in range(1, len(grads)):
         total = total + coupling_ref[g, axis, f] * grads[g]
     return total
-
-
-def edges_kernel(column_ref, adjoint_ref, top_ref, bottom_ref, near_ref, far_ref, hold, arrive, leave):
-    fields, depth = adjoint_ref.shape[:2]
-    half = HALO // 2
-    edge = jnp.where(column_ref[0] == 3, depth - HALO, 0)
-
-    def load(f):
-        return pltpu.make_async_copy(adjoint_ref.at[f], hold.at[f], arrive.at[f])
-
-    def stores(f):
-        return [
-            pltpu.make_async_copy(hold.at[f, pl.ds(start, size)], out.at[f], leave.at[f, k])
-            for k, (out, start, size) in enumerate(
-                (
-                    (near_ref, edge, half),
-                    (far_ref, edge + half, half),
-                    (top_ref, depth - HALO, HALO),
-                    (bottom_ref, 0, HALO),
-                )
-            )
-        ]
-
-    for f in range(fields):
-        load(f).start()
-    for f in range(fields):
-        load(f).wait()
-        for copy in stores(f):
-            copy.start()
-    for f in range(fields):
-        for copy in stores(f):
-            copy.wait()
-
-
-def edges(column, adjoint):
-    fields, _, rows, width = adjoint.shape
-    counts = (HALO, HALO, HALO // 2, HALO // 2)
-    anywhere = pl.BlockSpec(memory_space=pl.ANY)
-    return pl.pallas_call(
-        edges_kernel,
-        in_specs=[pl.BlockSpec(memory_space=pltpu.SMEM), anywhere],
-        out_specs=[anywhere] * len(counts),
-        out_shape=[jax.ShapeDtypeStruct((fields, count, rows, width), jnp.float32) for count in counts],
-        scratch_shapes=[
-            pltpu.VMEM(adjoint.shape, jnp.float32),
-            pltpu.SemaphoreType.DMA((fields,)),
-            pltpu.SemaphoreType.DMA((fields, len(counts))),
-        ],
-        name="edges",
-        cost_estimate=pl.CostEstimate(flops=0, bytes_accessed=7 * 1024 * 1024, transcendentals=0),
-    )(column, adjoint)
 
 
 def local_kernel(
@@ -450,7 +460,8 @@
     coupling = jnp.transpose(coupling, (1, 0, 2))
     me = lax.axis_index("gy").astype(jnp.int32)[None]
     column = (lax.axis_index("gz").astype(jnp.int32) & 3)[None]
-    pieces = pack(me, adjoint, speed)
+    *pieces, own = pack(me, adjoint, speed, (1, 2, 3, 4, 5, 6, 7, 0))
+    pieces = [own, *pieces]
     same = [pieces[0]]
     for o in range(1, 8):
         same.append(lax.ppermute(pieces[o], "gy", chip_perm(*OFFSETS[o])))
@@ -458,7 +469,7 @@
     for o in range(8):
         other.append(lax.ppermute(same[o], "gy", CORE_SWAP))
 
-    top, bottom, near, far = edges(column, adjoint)
+    early, late, (near, far, top, bottom) = prepare(me, column, y_operators, adjoint)
     runs = [4 * r for r in range(lax.axis_size("gz") // 4)]
     near = lax.ppermute(near, "gz", [p for r in runs for p in ((r + 3, r), (r, r + 3))])
     far = lax.ppermute(far, "gz", [p for r in runs for p in ((r + 3, r + 1), (r, r + 2))])
@@ -469,7 +480,6 @@
     near = lax.ppermute(crossing, "gz", [(r + x, (r ^ 4) + x) for r in runs for x in range(4)])
     far = lax.ppermute(near, "gz", [p for r in runs for p in ((r + 1, r), (r + 2, r + 3))])
 
-    early, late = own_operators(me, y_operators, chips, rows)
     sums = early_lines(me, early, same[:EARLY], other[:EARLY])
     parts = late_lines(me, coupling, late, sums, same[EARLY:], other[EARLY:], same)
     arrived = [parts[0]]

time: 136 us -> 134 us (0.985)
  waiting for transfers between devices: 44.8 us -> 42.6 us
    ppermute x7, waiting for transfers between devices: 20.1 us -> 17.9 us  [shards(): arrived.append(lax.ppermute(parts[o], 'gy', chip_perm(*OFFSETS[o])))]
    pallas_call x1 -> x2, Pallas kernels: 2.52 us -> 4.15 us  [join(): pl.pallas_call(functools.partial(join_kernel, where=where), in_specs=[pl....]
    pallas_call x3 -> x2, Pallas kernels: 11.5 us -> 10.4 us  [the longest x1 7.59 us: prepare(): pl.pallas_call(operator_kernel, grid_spec=pltpu.PrefetchScalarGridSpec(nu...]
  transfers between devices with their start and end apart: 28 -> 28, of which waited for: 7 -> 8; matrix products, arithmetic and copies ran while one was open for 1% -> 1% of each run, Pallas kernels for 29% -> 30%
where the time goes in v3:
time: 134 us; the launch traced here: 133 us
  Pallas kernels  44.8 us (33%)
  waiting for transfers between devices  42.6 us (32%)
  starting transfers between devices  42.5 us (32%)
  local copies, waits for them, and re-layouts  1.83 us (1%)
    ppermute x7, waiting for transfers between devices, shards(): same.append(lax.ppermute(pieces[o], 'gy', chip_perm(*OFFSETS[o])))  24.5 us
    ppermute x7, waiting for transfers between devices, shards(): arrived.append(lax.ppermute(parts[o], 'gy', chip_perm(*OFFSETS[o])))  17.9 us
    ppermute x7, starting transfers between devices, shards(): arrived.append(lax.ppermute(parts[o], 'gy', chip_perm(*OFFSETS[o])))  15.7 us
    ppermute x7, starting transfers between devices, shards(): same.append(lax.ppermute(pieces[o], 'gy', chip_perm(*OFFSETS[o])))  14.6 us
    pallas_call x1, Pallas kernels, late_lines(): pl.pallas_call(late_kernel, grid_spec=pltpu.PrefetchScalarGridSpec(num_sc...  10.7 us
    pallas_call x1, Pallas kernels, local_terms(): pl.pallas_call(local_kernel, grid=(rows // step,), in_specs=[pl.BlockSpec...  10.2 us
    pallas_call x1, Pallas kernels, early_lines(): pl.pallas_call(early_kernel, grid_spec=pltpu.PrefetchScalarGridSpec(num_s...  9.35 us
    pallas_call x1, Pallas kernels, prepare(): pl.pallas_call(operator_kernel, grid_spec=pltpu.PrefetchScalarGridSpec(nu...  7.59 us
  transfers between devices with their start and end apart: 28, of which 8 were waited for; matrix products, arithmetic and copies ran while one was open for 1% of the time, Pallas kernels for 30%

profile of v3, /device:TPU:32, one launch (start us, length us, event | category | flops | bytes accessed | tf_op | source)
XLA Modules:
  0.0 132.9 jit_solution(2243285661542652611)
XLA Ops:
  0.0 2.8 %pack.1 = (f32[6,64,256]{2,1,0:T(8,128)}, f32[6,64,256]{2,1,0:T(8,128)}, f32[6,64,256]{2,1,0:T(8,128)}, f32[6,64,256]{2,1,0:T(8,128)}, f32[6,64,256]{2,1,0:T(8,1...) custom-call(s32[1]{0:T(128)} %bitcast.me_ref, f32[5,8,64,256]{3,2,1,0:T(8,128)} %adjoint_ref.5, ...), custom_call_target="tpu_custom_call" | custom-call | bytes 6291456 | tf_op jit(solution)/shard_map/pack/pallas_call | solution.py:82
  2.8 2.0 %collective-permute-start.6 = (f32[6,64,256]{2,1,0:T(8,128)}, f32[6,64,256]{2,1,0:T(8,128)S(1)}, u32[]{:S(2)}, u32[]{:S(2)}) collective-permute-start(f32[6,64,256]{2,1,0:T(8,128)} %get-tuple-element.34), channel_id=1, source_target_pairs={{0,32},{8,40},{16,48},{24,56},{32,64},{40,72},{48,80},{56,88},{64,... | collective-permute-start | bytes 1179656 | tf_op jit(solution)/shard_map/ppermute | solution.py:467
  4.8 0.1 collective-permute-start.7
  4.9 3.2 %collective-permute-start.8 = (f32[6,64,256]{2,1,0:T(8,128)}, f32[6,64,256]{2,1,0:T(8,128)S(1)}, u32[]{:S(2)}, u32[]{:S(2)}) collective-permute-start(f32[6,64,256]{2,1,0:T(8,128)} %get-tuple-element.36), channel_id=1, source_target_pairs={{0,16},{8,24},{16,0},{24,8},{32,48},{40,56},{48,32},{56,40},{64,80... | collective-permute-start | bytes 1179656 | tf_op jit(solution)/shard_map/ppermute | solution.py:467
  8.1 0.0 collective-permute-start.9
  8.1 3.0 %collective-permute-start.13 = (f32[6,64,256]{2,1,0:T(8,128)}, f32[6,64,256]{2,1,0:T(8,128)S(1)}, u32[]{:S(2)}, u32[]{:S(2)}) collective-permute-start(f32[6,64,256]{2,1,0:T(8,128)} %get-tuple-element.37), channel_id=1, source_target_pairs={{0,64},{8,72},{16,80},{24,88},{32,96},{40,104},{48,112},{56,120},{... | collective-permute-start | bytes 1179656 | tf_op jit(solution)/shard_map/ppermute | solution.py:467
  11.1 15.1 %collective-permute-done.6.refs_1_.refs_10_ = f32[6,64,256]{2,1,0:T(8,128)S(1)} collective-permute-done((f32[6,64,256]{2,1,0:T(8,128)}, f32[6,64,256]{2,1,0:T(8,128)S(1)}, u32[]{:S(2)}, u32[]{:S(2)}) %collective-permute-start.6) | collective-permute-done | bytes 393248 | tf_op jit(solution)/shard_map/ppermute | solution.py:467
  26.2 0.0 collective-permute-start.14
  26.2 0.0 collective-permute-done.7.refs_2_.refs_9_
  26.2 4.4 %collective-permute-start.15 = (f32[6,64,256]{2,1,0:T(8,128)}, f32[6,64,256]{2,1,0:T(8,128)}, u32[]{:S(2)}, u32[]{:S(2)}) collective-permute-start(f32[6,64,256]{2,1,0:T(8,128)} %get-tuple-element.39), channel_id=1, source_target_pairs={{0,112},{8,120},{16,96},{24,104},{32,16},{40,24},{48,0},{56,8},{64... | collective-permute-start | bytes 1179656 | tf_op jit(solution)/shard_map/ppermute | solution.py:467
  30.6 7.6 %operators.1 = (bf16[2,8,64,1536]{3,2,1,0:T(8,128)(2,1)}, bf16[2,8,64,1536]{3,2,1,0:T(8,128)(2,1)}, f32[5,2,64,256]{3,2,1,0:T(8,128)}, f32[5,2,64,256]{3,2,1,0:T...) custom-call(s32[1]{0:T(128)} %bitcast.me_ref, s32[1]{0:T(128)} %bitcast.1.column_ref, ...), custom_call_target="tpu_custom_call" | custom-call | flops 4194304 | bytes 10485760 | tf_op jit(solution)/shard_map/operators/pallas_call | solution.py:165
  38.2 0.0 collective-permute-done.8.refs_3_.refs_11_
  38.3 4.7 %collective-permute-start.2 = (f32[5,2,64,256]{3,2,1,0:T(8,128)}, f32[5,2,64,256]{3,2,1,0:T(8,128)S(1)}, u32[]{:S(2)}, u32[]{:S(2)}) collective-permute-start(f32[5,2,64,256]{3,2,1,0:T(8,128)} %get-tuple-element.29), channel_id=1, source_target_pairs={{3,0},{0,3},{7,4},{4,7},{11,8},{8,11},{15,12},{12,15},{19,16},{16,... | collective-permute-start | bytes 1966088 | tf_op jit(solution)/shard_map/ppermute | solution.py:474
  42.9 0.0 collective-permute-done.9.refs_4_
  42.9 0.7 copy-done.12
  43.7 1.3 collective-permute-start.3
  45.0 0.0 collective-permute-done.13.refs_0_.refs_12_
  45.0 1.9 %collective-permute-start.16 = (f32[6,64,256]{2,1,0:T(8,128)}, f32[6,64,256]{2,1,0:T(8,128)S(1)}, u32[]{:S(2)}, u32[]{:S(2)}) collective-permute-start(f32[6,64,256]{2,1,0:T(8,128)} %get-tuple-element.40), channel_id=1, source_target_pairs={{0,80},{8,88},{16,64},{24,72},{32,112},{40,120},{48,96},{56,104},{... | collective-permute-start | bytes 1179656 | tf_op jit(solution)/shard_map/ppermute | solution.py:467
  47.0 0.0 collective-permute-done.14.refs_1_.refs_14_
  47.0 0.1 collective-permute-start.10
  47.1 0.0 collective-permute-done.15.refs_2_.refs_13_
  47.1 0.5 collective-permute-start.11
  47.6 9.4 %collective-permute-done.16.refs_3_.refs_15_ = f32[6,64,256]{2,1,0:T(8,128)S(1)} collective-permute-done((f32[6,64,256]{2,1,0:T(8,128)}, f32[6,64,256]{2,1,0:T(8,128)S(1)}, u32[]{:S(2)}, u32[]{:S(2)}) %collective-permute-start.16) | collective-permute-done | bytes 393248 | tf_op jit(solution)/shard_map/ppermute | solution.py:467
  57.0 0.0 collective-permute-start.12
  57.0 0.0 collective-permute-done.2
  57.0 0.5 collective-permute-start.17
  57.5 0.0 collective-permute-done.3
  57.5 0.2 copy-done.13
  57.8 0.0 collective-permute-start.18
  57.8 0.0 collective-permute-done.10.refs_5_
  57.8 0.5 collective-permute-start.19
  58.3 0.0 collective-permute-done.11.refs_6_
  58.3 0.1 collective-permute-start.20
  58.4 0.9 broadcast_select_fusion
  59.3 0.0 collective-permute-done.12.refs_7_
  59.3 0.0 collective-permute-start
  59.3 0.1 collective-permute-done.17.refs_4_
  59.4 3.2 %collective-permute-start.1 = (f32[5,4,64,256]{3,2,1,0:T(8,128)}, f32[5,4,64,256]{3,2,1,0:T(8,128)S(1)}, u32[]{:S(2)}, u32[]{:S(2)}) collective-permute-start(f32[5,4,64,256]{3,2,1,0:T(8,128)} %get-tuple-element.28), channel_id=1, source_target_pairs={{1,0},{2,1},{3,2},{0,3},{5,4},{6,5},{7,6},{4,7},{9,8},{10,9},{11,1... | collective-permute-start | bytes 3932168 | tf_op jit(solution)/shard_map/ppermute | solution.py:477
  62.6 0.0 collective-permute-done.18.refs_5_
  62.6 0.0 collective-permute-start.4
  62.6 9.4 %early_lines.1.sums_ref = f32[5,1024,256]{2,1,0:T(8,128)} custom-call(s32[1]{0:T(128)} %bitcast.me_ref, bf16[1024,1536]{1,0:T(8,128)(2,1)} %bitcast.10, f32[6,64,256]{2,1,0:T(8,128)} %get-tuple-element.33.refs_0_.refs_8_, f32[6,64,256]{2,1,0:T(8,128)} %copy-done.7, f32[6,64,256]{2,1,0:T(8,128)} %copy-done.8, f32[6,64,256]{2,1,0:T(8,128)} %copy-done.9, ...), custom_call_target="tpu_custom_call" | custom-call | flops 4026531840 | bytes 12582912 | tf_op jit(solution)/shard_map/early_lines/pallas_call | solution.py:219
  72.0 0.0 collective-permute-done.19.refs_6_
  72.0 10.7 %late_lines.1 = (f32[5,64,256]{2,1,0:T(8,128)}, f32[5,64,256]{2,1,0:T(8,128)}, f32[5,64,256]{2,1,0:T(8,128)}, f32[5,64,256]{2,1,0:T(8,128)}, f32[5,64,256]{2,1,0...) custom-call(s32[1]{0:T(128)} %bitcast.me_ref, f32[5,3,5]{2,1,0:T(4,128)} %bitcast.7, ...), custom_call_target="tpu_custom_call" | custom-call | flops 4026531840 | bytes 16777216 | tf_op jit(solution)/shard_map/late_lines/pallas_call | solution.py:280
  82.7 2.4 %collective-permute-start.21 = (f32[5,64,256]{2,1,0:T(8,128)}, f32[5,64,256]{2,1,0:T(8,128)S(1)}, u32[]{:S(2)}, u32[]{:S(2)}) collective-permute-start(f32[5,64,256]{2,1,0:T(8,128)} %get-tuple-element.42), channel_id=1, source_target_pairs={{0,32},{8,40},{16,48},{24,56},{32,64},{40,72},{48,80},{56,88},{64,... | collective-permute-start | bytes 983048 | tf_op jit(solution)/shard_map/ppermute | solution.py:487
  85.1 0.0 collective-permute-done.4.near_ref
  85.1 1.3 collective-permute-start.5
  86.4 0.8 collective-permute-start.22
  87.1 6.3 %collective-permute-done.21.refs_1_ = f32[5,64,256]{2,1,0:T(8,128)S(1)} collective-permute-done((f32[5,64,256]{2,1,0:T(8,128)}, f32[5,64,256]{2,1,0:T(8,128)S(1)}, u32[]{:S(2)}, u32[]{:S(2)}) %collective-permute-start.21) | collective-permute-done | bytes 327712 | tf_op jit(solution)/shard_map/ppermute | solution.py:487
  93.5 1.7 %collective-permute-start.23 = (f32[5,64,256]{2,1,0:T(8,128)}, f32[5,64,256]{2,1,0:T(8,128)S(1)}, u32[]{:S(2)}, u32[]{:S(2)}) collective-permute-start(f32[5,64,256]{2,1,0:T(8,128)} %get-tuple-element.44), channel_id=1, source_target_pairs={{0,16},{8,24},{16,0},{24,8},{32,48},{40,56},{48,32},{56,40},{64,80... | collective-permute-start | bytes 983048 | tf_op jit(solution)/shard_map/ppermute | solution.py:487
  95.1 0.8 collective-permute-done.22.refs_2_
  95.9 3.6 %collective-permute-start.24 = (f32[5,64,256]{2,1,0:T(8,128)}, f32[5,64,256]{2,1,0:T(8,128)}, u32[]{:S(2)}, u32[]{:S(2)}) collective-permute-start(f32[5,64,256]{2,1,0:T(8,128)} %get-tuple-element.45), channel_id=1, source_target_pairs={{0,64},{8,72},{16,80},{24,88},{32,96},{40,104},{48,112},{56,120},{... | collective-permute-start | bytes 983048 | tf_op jit(solution)/shard_map/ppermute | solution.py:487
  99.6 4.3 %collective-permute-done.23.refs_3_ = f32[5,64,256]{2,1,0:T(8,128)S(1)} collective-permute-done((f32[5,64,256]{2,1,0:T(8,128)}, f32[5,64,256]{2,1,0:T(8,128)S(1)}, u32[]{:S(2)}, u32[]{:S(2)}) %collective-permute-start.23) | collective-permute-done | bytes 327712 | tf_op jit(solution)/shard_map/ppermute | solution.py:487
  103.9 1.1 collective-permute-start.25
  105.0 3.3 %collective-permute-start.26 = (f32[5,64,256]{2,1,0:T(8,128)}, f32[5,64,256]{2,1,0:T(8,128)}, u32[]{:S(2)}, u32[]{:S(2)}) collective-permute-start(f32[5,64,256]{2,1,0:T(8,128)} %get-tuple-element.47), channel_id=1, source_target_pairs={{0,112},{8,120},{16,96},{24,104},{32,16},{40,24},{48,0},{56,8},{64... | collective-permute-start | bytes 983048 | tf_op jit(solution)/shard_map/ppermute | solution.py:487
  108.3 0.0 collective-permute-done.1.high_ref
  108.3 2.8 %collective-permute-start.27 = (f32[5,64,256]{2,1,0:T(8,128)}, f32[5,64,256]{2,1,0:T(8,128)}, u32[]{:S(2)}, u32[]{:S(2)}) collective-permute-start(f32[5,64,256]{2,1,0:T(8,128)} %get-tuple-element.48), channel_id=1, source_target_pairs={{0,80},{8,88},{16,64},{24,72},{32,112},{40,120},{48,96},{56,104},{... | collective-permute-start | bytes 983048 | tf_op jit(solution)/shard_map/ppermute | solution.py:487
  111.1 0.0 collective-permute-done.5.far_ref
  111.2 0.8 copy-done.3
  112.0 10.2 %local.1.base_ref = f32[5,8,64,256]{3,2,1,0:T(8,128)} custom-call(s32[1]{0:T(128)} %bitcast.me_ref, s32[1]{0:T(128)} %bitcast.1.column_ref, f32[5,3,5]{2,1,0:T(4,128)} %bitcast.8, f32[5,8,64,256]{3,2,1,0:T(8,128)} %adjoint_ref.5, f32[5,4,64,256]{3,2,1,0:T(8,128)} %copy-done, f32[5,4,64,256]{3,2,1,0:T(8,128)} %copy-done.1, f32[5,2,64,256]{3,2,1,0:T(8,128)} %copy-done.2, ...), custom_call_target="tpu_custom_call" | custom-call | flops 1006632960 | bytes 12582912 | tf_op jit(solution)/shard_map/local/pallas_call | solution.py:372
  122.2 0.0 collective-permute-done.25.refs_1_
  122.2 1.9 %collective-permute-done.26.refs_2_ = f32[5,64,256]{2,1,0:T(8,128)} collective-permute-done((f32[5,64,256]{2,1,0:T(8,128)}, f32[5,64,256]{2,1,0:T(8,128)}, u32[]{:S(2)}, u32[]{:S(2)}) %collective-permute-start.26) | collective-permute-done | bytes 327712 | tf_op jit(solution)/shard_map/ppermute | solution.py:487
  124.1 2.3 %join.2.base_ref = f32[5,8,64,256]{3,2,1,0:T(8,128)} custom-call(s32[1]{0:T(128)} %bitcast.me_ref, f32[5,8,64,256]{3,2,1,0:T(8,128)} %local.1.base_ref, f32[5,64,256]{2,1,0:T(8,128)} %collective-permute-done.24.refs_0_, f32[5,64,256]{2,1,0:T(8,128)} %collective-permute-done.25.refs_1_, ...), custom_call_target="tpu_custom_call", output_to_operand_aliasing={{}: (1, {})} | custom-call | flops 245760 | bytes 3145728 | tf_op jit(solution)/shard_map/join/pallas_call | solution.py:435
  126.4 4.6 %collective-permute-done.27.refs_0_ = f32[5,64,256]{2,1,0:T(8,128)} collective-permute-done((f32[5,64,256]{2,1,0:T(8,128)}, f32[5,64,256]{2,1,0:T(8,128)}, u32[]{:S(2)}, u32[]{:S(2)}) %collective-permute-start.27) | collective-permute-done | bytes 327712 | tf_op jit(solution)/shard_map/ppermute | solution.py:487
  131.0 1.9 %join.3 = f32[5,8,64,256]{3,2,1,0:T(8,128)} custom-call(s32[1]{0:T(128)} %bitcast.me_ref, f32[5,8,64,256]{3,2,1,0:T(8,128)} %join.2.base_ref, f32[5,64,256]{2,1,0:T(8,128)} %collective-permute-done.27.refs_0_), custom_call_target="tpu_custom_call", output_to_operand_aliasing={{}: (1, {})} | custom-call | flops 81920 | bytes 1048576 | tf_op jit(solution)/shard_map/join/pallas_call | solution.py:435
  (28 shorter events, 0.1 us)
Async XLA Ops:
  2.8 23.3 %collective-permute-start.6 = (f32[6,64,256]{2,1,0:T(8,128)}, f32[6,64,256]{2,1,0:T(8,128)S(1)}, u32[]{:S(2)}, u32[]{:S(2)}) collective-permute-start(f32[6,64,256]{2,1,0:T(8,128)} %get-tuple-element.34), channel_id=1, source_target_pairs={{0,32},{8,40},{16,48},{24,56},{32,64},{40,72},{48,80},{56,88},{64,... | collective-permute-start | bytes 1179656 | tf_op jit(solution)/shard_map/ppermute | solution.py:467
  4.8 21.4 %collective-permute-start.7 = (f32[6,64,256]{2,1,0:T(8,128)}, f32[6,64,256]{2,1,0:T(8,128)S(1)}, u32[]{:S(2)}, u32[]{:S(2)}) collective-permute-start(f32[6,64,256]{2,1,0:T(8,128)} %get-tuple-element.35), channel_id=1, source_target_pairs={{0,96},{8,104},{16,112},{24,120},{32,0},{40,8},{48,16},{56,24},{64... | collective-permute-start | bytes 1179656 | tf_op jit(solution)/shard_map/ppermute | solution.py:467
  4.9 33.3 %collective-permute-start.8 = (f32[6,64,256]{2,1,0:T(8,128)}, f32[6,64,256]{2,1,0:T(8,128)S(1)}, u32[]{:S(2)}, u32[]{:S(2)}) collective-permute-start(f32[6,64,256]{2,1,0:T(8,128)} %get-tuple-element.36), channel_id=1, source_target_pairs={{0,16},{8,24},{16,0},{24,8},{32,48},{40,56},{48,32},{56,40},{64,80... | collective-permute-start | bytes 1179656 | tf_op jit(solution)/shard_map/ppermute | solution.py:467
  8.1 34.8 %collective-permute-start.9 = (f32[6,64,256]{2,1,0:T(8,128)}, f32[6,64,256]{2,1,0:T(8,128)S(1)}, u32[]{:S(2)}, u32[]{:S(2)}) collective-permute-start(f32[6,64,256]{2,1,0:T(8,128)} %get-tuple-element.33.refs_0_.refs_8_), channel_id=1, source_target_pairs={{0,8},{8,0},{16,24},{24,16},{32,40},{40,32},{48,56},{56,48},{64,72... | collective-permute-start | bytes 1179656 | tf_op jit(solution)/shard_map/ppermute | solution.py:470
  8.1 36.9 %collective-permute-start.13 = (f32[6,64,256]{2,1,0:T(8,128)}, f32[6,64,256]{2,1,0:T(8,128)S(1)}, u32[]{:S(2)}, u32[]{:S(2)}) collective-permute-start(f32[6,64,256]{2,1,0:T(8,128)} %get-tuple-element.37), channel_id=1, source_target_pairs={{0,64},{8,72},{16,80},{24,88},{32,96},{40,104},{48,112},{56,120},{... | collective-permute-start | bytes 1179656 | tf_op jit(solution)/shard_map/ppermute | solution.py:467
  26.2 20.8 %copy-start.7 = (f32[6,64,256]{2,1,0:T(8,128)}, f32[6,64,256]{2,1,0:T(8,128)S(1)}, u32[]{:S(2)}) copy-start(f32[6,64,256]{2,1,0:T(8,128)S(1)} %collective-permute-done.6.refs_1_.refs_10_) | copy-start | bytes 1179652
  26.2 20.8 %collective-permute-start.14 = (f32[6,64,256]{2,1,0:T(8,128)}, f32[6,64,256]{2,1,0:T(8,128)S(1)}, u32[]{:S(2)}, u32[]{:S(2)}) collective-permute-start(f32[6,64,256]{2,1,0:T(8,128)} %get-tuple-element.38), channel_id=1, source_target_pairs={{0,48},{8,56},{16,32},{24,40},{32,80},{40,88},{48,64},{56,72},{64,... | collective-permute-start | bytes 1179656 | tf_op jit(solution)/shard_map/ppermute | solution.py:467
  26.2 20.9 %copy-start.8 = (f32[6,64,256]{2,1,0:T(8,128)}, f32[6,64,256]{2,1,0:T(8,128)S(1)}, u32[]{:S(2)}) copy-start(f32[6,64,256]{2,1,0:T(8,128)S(1)} %collective-permute-done.7.refs_2_.refs_9_) | copy-start | bytes 1179652
  26.2 20.9 %collective-permute-start.15 = (f32[6,64,256]{2,1,0:T(8,128)}, f32[6,64,256]{2,1,0:T(8,128)}, u32[]{:S(2)}, u32[]{:S(2)}) collective-permute-start(f32[6,64,256]{2,1,0:T(8,128)} %get-tuple-element.39), channel_id=1, source_target_pairs={{0,112},{8,120},{16,96},{24,104},{32,16},{40,24},{48,0},{56,8},{64... | collective-permute-start | bytes 1179656 | tf_op jit(solution)/shard_map/ppermute | solution.py:467
  38.2 21.2 %copy-start.9 = (f32[6,64,256]{2,1,0:T(8,128)}, f32[6,64,256]{2,1,0:T(8,128)S(1)}, u32[]{:S(2)}) copy-start(f32[6,64,256]{2,1,0:T(8,128)S(1)} %collective-permute-done.8.refs_3_.refs_11_) | copy-start | bytes 1179652
  38.3 18.8 %collective-permute-start.2 = (f32[5,2,64,256]{3,2,1,0:T(8,128)}, f32[5,2,64,256]{3,2,1,0:T(8,128)S(1)}, u32[]{:S(2)}, u32[]{:S(2)}) collective-permute-start(f32[5,2,64,256]{3,2,1,0:T(8,128)} %get-tuple-element.29), channel_id=1, source_target_pairs={{3,0},{0,3},{7,4},{4,7},{11,8},{8,11},{15,12},{12,15},{19,16},{16,... | collective-permute-start | bytes 1966088 | tf_op jit(solution)/shard_map/ppermute | solution.py:474
  42.9 0.7 copy-start.12
  43.7 13.8 %collective-permute-start.3 = (f32[5,2,64,256]{3,2,1,0:T(8,128)}, f32[5,2,64,256]{3,2,1,0:T(8,128)S(1)}, u32[]{:S(2)}, u32[]{:S(2)}) collective-permute-start(f32[5,2,64,256]{3,2,1,0:T(8,128)} %get-tuple-element.30), channel_id=1, source_target_pairs={{3,1},{0,2},{7,5},{4,6},{11,9},{8,10},{15,13},{12,14},{19,17},{16,... | collective-permute-start | bytes 1966088 | tf_op jit(solution)/shard_map/ppermute | solution.py:475
  45.0 14.4 %copy-start.10 = (f32[6,64,256]{2,1,0:T(8,128)}, f32[6,64,256]{2,1,0:T(8,128)S(1)}, u32[]{:S(2)}) copy-start(f32[6,64,256]{2,1,0:T(8,128)S(1)} %collective-permute-done.13.refs_0_.refs_12_) | copy-start | bytes 1179652
  45.0 12.0 %collective-permute-start.16 = (f32[6,64,256]{2,1,0:T(8,128)}, f32[6,64,256]{2,1,0:T(8,128)S(1)}, u32[]{:S(2)}, u32[]{:S(2)}) collective-permute-start(f32[6,64,256]{2,1,0:T(8,128)} %get-tuple-element.40), channel_id=1, source_target_pairs={{0,80},{8,88},{16,64},{24,72},{32,112},{40,120},{48,96},{56,104},{... | collective-permute-start | bytes 1179656 | tf_op jit(solution)/shard_map/ppermute | solution.py:467
  47.0 15.6 %copy-start.11 = (f32[6,64,256]{2,1,0:T(8,128)}, f32[6,64,256]{2,1,0:T(8,128)S(1)}, u32[]{:S(2)}) copy-start(f32[6,64,256]{2,1,0:T(8,128)S(1)} %collective-permute-done.14.refs_1_.refs_14_) | copy-start | bytes 1179652
  47.0 10.8 %collective-permute-start.10 = (f32[6,64,256]{2,1,0:T(8,128)S(1)}, f32[6,64,256]{2,1,0:T(8,128)}, u32[]{:S(2)}, u32[]{:S(2)}) collective-permute-start(f32[6,64,256]{2,1,0:T(8,128)S(1)} %collective-permute-done.6.refs_1_.refs_10_), channel_id=1, source_target_pairs={{0,8},{8,0},{16,24},{24,16},{32,40},{40,32},{48,56},{56,48},{64,72... | collective-permute-start | bytes 1179656 | tf_op jit(solution)/shard_map/ppermute | solution.py:470
  47.1 11.2 %collective-permute-start.11 = (f32[6,64,256]{2,1,0:T(8,128)S(1)}, f32[6,64,256]{2,1,0:T(8,128)}, u32[]{:S(2)}, u32[]{:S(2)}) collective-permute-start(f32[6,64,256]{2,1,0:T(8,128)S(1)} %collective-permute-done.7.refs_2_.refs_9_), channel_id=1, source_target_pairs={{0,8},{8,0},{16,24},{24,16},{32,40},{40,32},{48,56},{56,48},{64,72... | collective-permute-start | bytes 1179656 | tf_op jit(solution)/shard_map/ppermute | solution.py:470
  57.0 0.8 copy-start.13
  57.0 2.3 %collective-permute-start.12 = (f32[6,64,256]{2,1,0:T(8,128)S(1)}, f32[6,64,256]{2,1,0:T(8,128)}, u32[]{:S(2)}, u32[]{:S(2)}) collective-permute-start(f32[6,64,256]{2,1,0:T(8,128)S(1)} %collective-permute-done.8.refs_3_.refs_11_), channel_id=1, source_target_pairs={{0,8},{8,0},{16,24},{24,16},{32,40},{40,32},{48,56},{56,48},{64,72... | collective-permute-start | bytes 1179656 | tf_op jit(solution)/shard_map/ppermute | solution.py:470
  57.0 2.4 %collective-permute-start.17 = (f32[6,64,256]{2,1,0:T(8,128)S(1)}, f32[6,64,256]{2,1,0:T(8,128)}, u32[]{:S(2)}, u32[]{:S(2)}) collective-permute-start(f32[6,64,256]{2,1,0:T(8,128)S(1)} %collective-permute-done.13.refs_0_.refs_12_), channel_id=1, source_target_pairs={{0,8},{8,0},{16,24},{24,16},{32,40},{40,32},{48,56},{56,48},{64,72... | collective-permute-start | bytes 1179656 | tf_op jit(solution)/shard_map/ppermute | solution.py:470
  57.8 4.9 %collective-permute-start.18 = (f32[6,64,256]{2,1,0:T(8,128)S(1)}, f32[6,64,256]{2,1,0:T(8,128)}, u32[]{:S(2)}, u32[]{:S(2)}) collective-permute-start(f32[6,64,256]{2,1,0:T(8,128)S(1)} %collective-permute-done.14.refs_1_.refs_14_), channel_id=1, source_target_pairs={{0,8},{8,0},{16,24},{24,16},{32,40},{40,32},{48,56},{56,48},{64,72... | collective-permute-start | bytes 1179656 | tf_op jit(solution)/shard_map/ppermute | solution.py:470
  57.8 14.2 %collective-permute-start.19 = (f32[6,64,256]{2,1,0:T(8,128)}, f32[6,64,256]{2,1,0:T(8,128)}, u32[]{:S(2)}, u32[]{:S(2)}) collective-permute-start(f32[6,64,256]{2,1,0:T(8,128)} %collective-permute-done.15.refs_2_.refs_13_), channel_id=1, source_target_pairs={{0,8},{8,0},{16,24},{24,16},{32,40},{40,32},{48,56},{56,48},{64,72... | collective-permute-start | bytes 1179656 | tf_op jit(solution)/shard_map/ppermute | solution.py:470
  58.3 13.7 %collective-permute-start.20 = (f32[6,64,256]{2,1,0:T(8,128)}, f32[6,64,256]{2,1,0:T(8,128)}, u32[]{:S(2)}, u32[]{:S(2)}) collective-permute-start(f32[6,64,256]{2,1,0:T(8,128)} %copy-done.13), channel_id=1, source_target_pairs={{0,8},{8,0},{16,24},{24,16},{32,40},{40,32},{48,56},{56,48},{64,72... | collective-permute-start | bytes 1179656 | tf_op jit(solution)/shard_map/ppermute | solution.py:470
  59.3 45.7 %collective-permute-start = (f32[5,4,64,256]{3,2,1,0:T(8,128)}, f32[5,4,64,256]{3,2,1,0:T(8,128)S(1)}, u32[]{:S(2)}, u32[]{:S(2)}) collective-permute-start(f32[5,4,64,256]{3,2,1,0:T(8,128)} %get-tuple-element.27), channel_id=1, source_target_pairs={{0,1},{1,2},{2,3},{3,0},{4,5},{5,6},{6,7},{7,4},{8,9},{9,10},{10,1... | collective-permute-start | bytes 3932168 | tf_op jit(solution)/shard_map/ppermute | solution.py:476
  59.4 48.9 %collective-permute-start.1 = (f32[5,4,64,256]{3,2,1,0:T(8,128)}, f32[5,4,64,256]{3,2,1,0:T(8,128)S(1)}, u32[]{:S(2)}, u32[]{:S(2)}) collective-permute-start(f32[5,4,64,256]{3,2,1,0:T(8,128)} %get-tuple-element.28), channel_id=1, source_target_pairs={{1,0},{2,1},{3,2},{0,3},{5,4},{6,5},{7,6},{4,7},{9,8},{10,9},{11,1... | collective-permute-start | bytes 3932168 | tf_op jit(solution)/shard_map/ppermute | solution.py:477
  62.6 22.5 %collective-permute-start.4 = (f32[5,2,64,256]{3,2,1,0:T(8,128)}, f32[5,2,64,256]{3,2,1,0:T(8,128)S(1)}, u32[]{:S(2)}, u32[]{:S(2)}) collective-permute-start(f32[5,2,64,256]{3,2,1,0:T(8,128)} %broadcast_select_fusion), channel_id=1, source_target_pairs={{0,4},{1,5},{2,6},{3,7},{4,0},{5,1},{6,2},{7,3},{8,12},{9,13},{10,... | collective-permute-start | bytes 1966088 | tf_op jit(solution)/shard_map/ppermute | solution.py:480
  82.7 10.8 %collective-permute-start.21 = (f32[5,64,256]{2,1,0:T(8,128)}, f32[5,64,256]{2,1,0:T(8,128)S(1)}, u32[]{:S(2)}, u32[]{:S(2)}) collective-permute-start(f32[5,64,256]{2,1,0:T(8,128)} %get-tuple-element.42), channel_id=1, source_target_pairs={{0,32},{8,40},{16,48},{24,56},{32,64},{40,72},{48,80},{56,88},{64,... | collective-permute-start | bytes 983048 | tf_op jit(solution)/shard_map/ppermute | solution.py:487
  85.1 26.9 %copy-start.2 = (f32[5,2,64,256]{3,2,1,0:T(8,128)}, f32[5,2,64,256]{3,2,1,0:T(8,128)S(1)}, u32[]{:S(2)}) copy-start(f32[5,2,64,256]{3,2,1,0:T(8,128)S(1)} %collective-permute-done.4.near_ref) | copy-start | bytes 1966084
  85.1 26.1 %collective-permute-start.5 = (f32[5,2,64,256]{3,2,1,0:T(8,128)S(1)}, f32[5,2,64,256]{3,2,1,0:T(8,128)S(1)}, u32[]{:S(2)}, u32[]{:S(2)}) collective-permute-start(f32[5,2,64,256]{3,2,1,0:T(8,128)S(1)} %collective-permute-done.4.near_ref), channel_id=1, source_target_pairs={{1,0},{2,3},{5,4},{6,7},{9,8},{10,11},{13,12},{14,15},{17,16},{18,... | collective-permute-start | bytes 1966088 | tf_op jit(solution)/shard_map/ppermute | solution.py:481
  86.4 9.6 %collective-permute-start.22 = (f32[5,64,256]{2,1,0:T(8,128)}, f32[5,64,256]{2,1,0:T(8,128)S(1)}, u32[]{:S(2)}, u32[]{:S(2)}) collective-permute-start(f32[5,64,256]{2,1,0:T(8,128)} %get-tuple-element.43), channel_id=1, source_target_pairs={{0,96},{8,104},{16,112},{24,120},{32,0},{40,8},{48,16},{56,24},{64... | collective-permute-start | bytes 983048 | tf_op jit(solution)/shard_map/ppermute | solution.py:487
  93.5 17.7 %copy-start.4 = (f32[5,64,256]{2,1,0:T(8,128)}, f32[5,64,256]{2,1,0:T(8,128)S(1)}, u32[]{:S(2)}) copy-start(f32[5,64,256]{2,1,0:T(8,128)S(1)} %collective-permute-done.21.refs_1_) | copy-start | bytes 983044
  93.5 10.4 %collective-permute-start.23 = (f32[5,64,256]{2,1,0:T(8,128)}, f32[5,64,256]{2,1,0:T(8,128)S(1)}, u32[]{:S(2)}, u32[]{:S(2)}) collective-permute-start(f32[5,64,256]{2,1,0:T(8,128)} %get-tuple-element.44), channel_id=1, source_target_pairs={{0,16},{8,24},{16,0},{24,8},{32,48},{40,56},{48,32},{56,40},{64,80... | collective-permute-start | bytes 983048 | tf_op jit(solution)/shard_map/ppermute | solution.py:487
  95.9 15.2 %copy-start.5 = (f32[5,64,256]{2,1,0:T(8,128)}, f32[5,64,256]{2,1,0:T(8,128)S(1)}, u32[]{:S(2)}) copy-start(f32[5,64,256]{2,1,0:T(8,128)S(1)} %collective-permute-done.22.refs_2_) | copy-start | bytes 983044
  95.9 26.3 %collective-permute-start.24 = (f32[5,64,256]{2,1,0:T(8,128)}, f32[5,64,256]{2,1,0:T(8,128)}, u32[]{:S(2)}, u32[]{:S(2)}) collective-permute-start(f32[5,64,256]{2,1,0:T(8,128)} %get-tuple-element.45), channel_id=1, source_target_pairs={{0,64},{8,72},{16,80},{24,88},{32,96},{40,104},{48,112},{56,120},{... | collective-permute-start | bytes 983048 | tf_op jit(solution)/shard_map/ppermute | solution.py:487
  103.9 7.3 %copy-start.6 = (f32[5,64,256]{2,1,0:T(8,128)}, f32[5,64,256]{2,1,0:T(8,128)S(1)}, u32[]{:S(2)}) copy-start(f32[5,64,256]{2,1,0:T(8,128)S(1)} %collective-permute-done.23.refs_3_) | copy-start | bytes 983044
  103.9 18.3 %collective-permute-start.25 = (f32[5,64,256]{2,1,0:T(8,128)}, f32[5,64,256]{2,1,0:T(8,128)}, u32[]{:S(2)}, u32[]{:S(2)}) collective-permute-start(f32[5,64,256]{2,1,0:T(8,128)} %get-tuple-element.46), channel_id=1, source_target_pairs={{0,48},{8,56},{16,32},{24,40},{32,80},{40,88},{48,64},{56,72},{64,... | collective-permute-start | bytes 983048 | tf_op jit(solution)/shard_map/ppermute | solution.py:487
  105.0 7.0 %copy-start = (f32[5,4,64,256]{3,2,1,0:T(8,128)}, f32[5,4,64,256]{3,2,1,0:T(8,128)S(1)}, u32[]{:S(2)}) copy-start(f32[5,4,64,256]{3,2,1,0:T(8,128)S(1)} %collective-permute-done.low_ref) | copy-start | bytes 3932164
  105.0 19.1 %collective-permute-start.26 = (f32[5,64,256]{2,1,0:T(8,128)}, f32[5,64,256]{2,1,0:T(8,128)}, u32[]{:S(2)}, u32[]{:S(2)}) collective-permute-start(f32[5,64,256]{2,1,0:T(8,128)} %get-tuple-element.47), channel_id=1, source_target_pairs={{0,112},{8,120},{16,96},{24,104},{32,16},{40,24},{48,0},{56,8},{64... | collective-permute-start | bytes 983048 | tf_op jit(solution)/shard_map/ppermute | solution.py:487
  108.3 3.7 %copy-start.1 = (f32[5,4,64,256]{3,2,1,0:T(8,128)}, f32[5,4,64,256]{3,2,1,0:T(8,128)S(1)}, u32[]{:S(2)}) copy-start(f32[5,4,64,256]{3,2,1,0:T(8,128)S(1)} %collective-permute-done.1.high_ref) | copy-start | bytes 3932164
  108.3 22.7 %collective-permute-start.27 = (f32[5,64,256]{2,1,0:T(8,128)}, f32[5,64,256]{2,1,0:T(8,128)}, u32[]{:S(2)}, u32[]{:S(2)}) collective-permute-start(f32[5,64,256]{2,1,0:T(8,128)} %get-tuple-element.48), channel_id=1, source_target_pairs={{0,80},{8,88},{16,64},{24,72},{32,112},{40,120},{48,96},{56,104},{... | collective-permute-start | bytes 983048 | tf_op jit(solution)/shard_map/ppermute | solution.py:487
  111.1 0.8 copy-start.3
